TPU v7x, 128 devices: a whole 4x4x4 slice. The times are simulated.
128 devices in a mesh: gx: 64 (over x, y, z), gy: 2 (over core).
Axes of the slice: x: 4, y: 4, z: 4, core: 2. Of those that a mesh axis runs over, the one named last changes fastest.
Arguments:
- operator: float32 [243, 131072], P(None, ('gx', 'gy')), may hold values from -0.6 to 10.6
- basis_u: float32 [144, 131072], P(None, ('gx', 'gy')), may hold values from -6 to 6
- basis_c: float32 [144, 131072], P(None, ('gx', 'gy')), may hold values from -6 to 6
- right_side: float32 [3, 131072], P(None, ('gx', 'gy')), may hold values from -16 to 16
- new_rows: int32 [131072], P(('gx', 'gy')), may hold values from 0 to 131071, as said below
Outputs:
- solution: float32 [3, 131072], P(None, ('gx', 'gy'))
- residual: float32 [3, 131072], P(None, ('gx', 'gy'))
Inputs may be any that keep to these rules, and one draw needn't show every extreme that they name: `new_rows`: each block row gets one new index (a permutation). Each device sends 0 to 16 of its old rows to each device, and each device both sends exactly 16 rows to some peer and receives exactly 16 rows from some peer.
All inputs are finite; a program needn't handle non-finite values.
Results may differ from a plain program's by a relative error of at most 0.0003.
Values sent between devices are 32-bit elements; how exact they have to be, the bound alone decides.
No kernel may reach another device: no remote copies, remote signals or barrier semaphores. Data moves between devices by JAX's collectives and lax.ppermute only.
A program may use at most 64 MiB of HBM per device.

v0:
```python
import functools

import jax
import jax.numpy as jnp
from jax import lax
from jax.sharding import Mesh
from jax.sharding import PartitionSpec as P

CX = 1
CY = 8
CZ = 128
K = 48
GX_GY = ("gx_0", "gx_1", "gx_2", "gy")
GX = ("gx_0", "gx_1", "gx_2")


def with_halo(cells, sides, width):
    for axis, dim in sides:
        count = lax.axis_size(axis)
        ends = count - 1
        head = lax.slice_in_dim(cells, 0, width, axis=dim)
        tail = lax.slice_in_dim(cells, cells.shape[dim] - width, cells.shape[dim], axis=dim)
        cells = jnp.concatenate(
            [
                lax.ppermute(tail, axis, [(i, (i + 1) % count) for i in range(ends)]),
                cells,
                lax.ppermute(head, axis, [((i + 1) % count, i) for i in range(ends)]),
            ],
            axis=dim,
        )
    return cells


def over_axes(shard, axes):
    return functools.reduce(lax.psum, axes, shard)


def stencil(coef, padded):
    size_x = padded.shape[1] - 2
    size_y = padded.shape[2] - 2
    size_z = padded.shape[3] - 2
    total = jnp.zeros((3, size_x, size_y, size_z), jnp.float32)
    for k in range(27):
        dx, dy, dz = (k // 9, k // 3 % 3, k % 3)
        moved = padded[:, dx : dx + size_x, dy : dy + size_y, dz : dz + size_z]
        total = total + jnp.sum(coef[k] * moved[None], axis=1)
    return total


def apply_op(coef, vector):
    block = vector.reshape(3, CX, CY, CZ)
    padded = with_halo(block, ((GX, 1), ("gy", 2)), 1)
    padded = jnp.pad(padded, ((0, 0), (0, 0), (0, 0), (1, 1)))
    return stencil(coef, padded).reshape(3, CX * CY * CZ)


def project(basis, vector):
    return jnp.einsum("amp,ap->m", basis, vector, precision=lax.Precision.HIGHEST)


def combine(basis, coeffs):
    return jnp.einsum("amp,m->ap", basis, coeffs, precision=lax.Precision.HIGHEST)


def body(operator, basis_u, basis_c, right_side, new_rows):
    rows = operator.shape[1]
    count_x = lax.axis_size(GX)
    count_y = lax.axis_size("gy")
    peers = count_x * count_y
    capacity = 2 * rows // peers
    payload = jnp.concatenate([operator, basis_u, basis_c, right_side], 0)
    c_start = 243 + 3 * K
    width = payload.shape[0]
    target = new_rows // rows
    local_row = new_rows % rows
    onehot = (target[:, None] == jnp.arange(peers, dtype=jnp.int32)[None, :]).astype(jnp.int32)
    rank = jnp.sum(jnp.cumsum(onehot, 0) * onehot, 1) - 1
    slot = target * capacity + rank
    buffer = jnp.zeros((width, peers * capacity), jnp.float32).at[:, slot].set(payload)
    labels = jnp.full((1, peers * capacity), rows, jnp.int32).at[0, slot].set(local_row)
    got, tags = (
        lax.all_to_all(buffer, GX_GY, split_axis=1, concat_axis=1, tiled=True),
        lax.all_to_all(labels, GX_GY, split_axis=1, concat_axis=1, tiled=True),
    )
    placed = jnp.zeros((width, rows), jnp.float32).at[:, tags[0]].set(got, mode="drop")
    coef = placed[:243].reshape(27, 3, 3, CX, CY, CZ)
    c_rows = placed[c_start : c_start + 3 * K].reshape(3, K, rows)
    load = placed[c_start + 3 * K :]
    gram_local = jnp.einsum("amp,anp->mn", c_rows, c_rows, precision=lax.Precision.HIGHEST)
    eye = jnp.eye(K, dtype=jnp.float32)
    gram, raw_start, load_sq = (
        over_axes(gram_local, GX_GY),
        over_axes(jnp.einsum("amp,ap->m", c_rows, load, precision=lax.Precision.HIGHEST), GX_GY),
        over_axes(jnp.sum(load * load), GX_GY),
    )
    lower_inv = jax.scipy.linalg.solve_triangular(jnp.linalg.cholesky(gram), eye, lower=True)
    cq = jnp.einsum("mn,anp->amp", lower_inv, c_rows, precision=lax.Precision.HIGHEST)
    start = jnp.dot(lower_inv, raw_start, precision=lax.Precision.HIGHEST)
    first_r = load - combine(cq, start)
    beta = jnp.sqrt(load_sq - jnp.sum(start * start))
    vec_one = first_r / beta

    def sums_of(image, vectors):
        local = (
            (project(cq, image),)
            + tuple((jnp.sum(vector * image) for vector in vectors))
            + (jnp.sum(image * image),)
        )
        return jax.tree.map(lambda part: over_axes(part, GX_GY), local)

    image = apply_op(coef, vec_one)
    proj_one, h11, image_sq = sums_of(image, (vec_one,))
    h21 = jnp.sqrt(image_sq - jnp.sum(proj_one * proj_one) - h11 * h11)
    vec_two = (image - combine(cq, proj_one) - h11 * vec_one) / h21
    image = apply_op(coef, vec_two)
    proj_two, h12, h22, image_sq = sums_of(image, (vec_one, vec_two))
    h32 = jnp.sqrt(image_sq - jnp.sum(proj_two * proj_two) - h12 * h12 - h22 * h22)
    m11 = h11 * h11 + h21 * h21
    m12 = h11 * h12 + h21 * h22
    m22 = h12 * h12 + h22 * h22 + h32 * h32
    g_one = beta * h11
    g_two = beta * h12
    determ = m11 * m22 - m12 * m12
    y_one = (m22 * g_one - m12 * g_two) / determ
    y_two = (m11 * g_two - m12 * g_one) / determ
    mixing = start - y_one * proj_one - y_two * proj_two
    u_weights = jnp.dot(lower_inv.T, mixing, precision=lax.Precision.HIGHEST)
    u_rows = placed[243 : 243 + 3 * K].reshape(3, K, rows)
    u_term = combine(u_rows, u_weights)
    solution = u_term + y_one * vec_one + y_two * vec_two
    residual = load - apply_op(coef, solution)
    return (solution, residual)


def solution(mesh):
    torus = Mesh(mesh.devices.reshape(4, 4, 4, mesh.shape["gy"]), ("gx_0", "gx_1", "gx_2", "gy"))
    placed = (P(None, GX_GY), P(None, GX_GY), P(None, GX_GY), P(None, GX_GY), P(GX_GY))
    return jax.shard_map(
        body,
        mesh=torus,
        in_specs=placed,
        out_specs=(P(None, GX_GY), P(None, GX_GY)),
        check_vma=False,
    )
```

profile of v0, /device:TPU:2, one launch (start us, length us, event | category | flops | bytes accessed | tf_op | source)
XLA Modules:
  0.0 562.2 jit_solution(8068142257902148239)
XLA Ops:
  2.5 4.3 scatter_custom_fusion.2
  7.6 10.5 %all-to-all-start = ((s32[1,128,16]{2,0,1:T(1,128)}), s32[1,128,16]{2,0,1:T(1,128)S(1)}, u32[]{:S(2)}, u32[]{:S(2)}) async-start(s32[1,128,16]{2,0,1:T(1,128)} %bitcast.5), calls=%async_computation | async-start | bytes 131072 | tf_op jit(solution)/shard_map/all_to_all | solution.py:83
  21.9 8.2 %scatter_custom_fusion = f32[534,2048]{0,1:T(8,128)} fusion(s32[1024]{0:T(1024)S(1)} %compare_select_fusion.1, f32[1024,534]{1,0:T(8,128)} %copy.236, f32[]{:T(128)} %constant.79.clone.1), kind=kCustom, calls=%fused_computation.3 | custom fusion | bytes 4375040 | tf_op jit(solution)/shard_map/scatter | solution.py:79
  30.1 10.2 %all-to-all-start.1 = ((f32[534,128,16]{0,2,1:T(8,128)}), f32[534,128,16]{0,2,1:T(8,128)}, u32[]{:S(2)}, u32[]{:S(2)}) async-start(f32[534,128,16]{0,2,1:T(8,128)} %bitcast.475), calls=%async_computation.1 | async-start | bytes 10485760 | tf_op jit(solution)/shard_map/all_to_all | solution.py:82
  41.7 62.2 %all-to-all-done.1 = f32[534,128,16]{0,2,1:T(8,128)} async-done(((f32[534,128,16]{0,2,1:T(8,128)}), f32[534,128,16]{0,2,1:T(8,128)}, u32[]{:S(2)}, u32[]{:S(2)}) %all-to-all-start.1) | async-done | bytes 4374560 | tf_op jit(solution)/shard_map/all_to_all | solution.py:82
  103.9 10.4 %scatter_custom_fusion.1 = f32[534,1024]{0,1:T(8,128)S(1)} fusion(s32[2048]{0:T(1024)S(1)} %bitcast.698, f32[2048,534]{1,0:T(8,128)} %bitcast.10, f32[]{:T(128)} %constant.79.clone.1), kind=kCustom, calls=%fused_computation.6 | custom fusion | bytes 2187776 | tf_op jit(solution)/shard_map/scatter | solution.py:85
  123.1 15.5 %all-reduce.12 = (f32[48,48]{0,1:T(8,128)S(1)}, f32[48]{0:T(128)S(1)}, f32[]{:T(128)}) all-reduce(f32[48,48]{0,1:T(8,128)S(1)} %convolution_bitcast_fusion.1, f32[48]{0:T(128)S(1)} %convolution_bitcast_fusion.5, f32[]{:T(128)} %get-tuple-element.86), channel_id=1, replica_groups=mesh['gx_0'=4,'gx_1'=4,'gx_2'=4,'gy'=2] {'gx_0'}, use_global_device_ids=true, to_apply=%region_6.7 | all-reduce | flops 2353 | bytes 18824 | tf_op jit(solution)/shard_map/psum | solution.py:35
  138.5 16.7 %all-reduce.9 = (f32[48,48]{0,1:T(8,128)S(1)}, f32[48]{0:T(128)S(1)}, f32[]{:T(128)}) all-reduce(f32[48,48]{0,1:T(8,128)S(1)} %get-tuple-element.39, f32[48]{0:T(128)S(1)} %get-tuple-element.40, f32[]{:T(128)} %get-tuple-element.41), channel_id=1, replica_groups=mesh['gx_0'=4,'gx_1'=4,'gx_2'=4,'gy'=2] {'gx_1'}, use_global_device_ids=true, to_apply=%region_7.8 | all-reduce | flops 2353 | bytes 18824 | tf_op jit(solution)/shard_map/psum | solution.py:35
  155.3 17.4 %all-reduce.6 = (f32[48,48]{0,1:T(8,128)S(1)}, f32[48]{0:T(128)S(1)}, f32[]{:T(128)}) all-reduce(f32[48,48]{0,1:T(8,128)S(1)} %get-tuple-element.29, f32[48]{0:T(128)S(1)} %get-tuple-element.30, f32[]{:T(128)} %get-tuple-element.31), channel_id=1, replica_groups=mesh['gx_0'=4,'gx_1'=4,'gx_2'=4,'gy'=2] {'gx_2'}, use_global_device_ids=true, to_apply=%region_8.9 | all-reduce | flops 2353 | bytes 18824 | tf_op jit(solution)/shard_map/psum | solution.py:35
  172.7 4.5 all-reduce.15
  177.3 4.4 cholesky.17
  204.9 6.4 %fusion.39 = (f32[9,1024]{0,1:T(8,128)}, f32[9,1024]{0,1:T(8,128)}, f32[9,1024]{0,1:T(8,128)}, f32[9,1024]{0,1:T(8,128)}, f32[9,1024]{0,1:T(8,128)}, /*index=5*/...) fusion(f32[534,1024]{0,1:T(8,128)S(1)} %scatter_custom_fusion.1), kind=kLoop, calls=%fused_computation.251 | loop fusion | bytes 1400832 | tf_op jit(solution)/shard_map/slice | solution.py:46
  320.8 4.3 multiply_reduce_fusion.2
  329.2 11.1 %all-reduce.11 = (f32[48]{0:T(128)}, f32[]{:T(128)}, f32[]{:T(128)}) all-reduce(f32[48]{0:T(128)} %convolution_bitcast_fusion.4, f32[]{:T(128)} %get-tuple-element.57, f32[]{:T(128)} %get-tuple-element.55), channel_id=1, replica_groups=mesh['gx_0'=4,'gx_1'=4,'gx_2'=4,'gy'=2] {'gx_0'}, use_global_device_ids=true, to_apply=%region_49.50 | all-reduce | flops 50 | bytes 400 | tf_op jit(solution)/shard_map/psum | solution.py:35
  340.3 8.5 %all-reduce.8 = (f32[48]{0:T(128)}, f32[]{:T(128)}, f32[]{:T(128)}) all-reduce(f32[48]{0:T(128)} %get-tuple-element.36, f32[]{:T(128)} %get-tuple-element.37, f32[]{:T(128)} %get-tuple-element.38), channel_id=1, replica_groups=mesh['gx_0'=4,'gx_1'=4,'gx_2'=4,'gy'=2] {'gx_1'}, use_global_device_ids=true, to_apply=%region_50.51 | all-reduce | flops 50 | bytes 400 | tf_op jit(solution)/shard_map/psum | solution.py:35
  348.8 11.9 %all-reduce.5 = (f32[48]{0:T(128)}, f32[]{:T(128)}, f32[]{:T(128)}) all-reduce(f32[48]{0:T(128)} %get-tuple-element.26, f32[]{:T(128)} %get-tuple-element.27, f32[]{:T(128)} %get-tuple-element.28), channel_id=1, replica_groups=mesh['gx_0'=4,'gx_1'=4,'gx_2'=4,'gy'=2] {'gx_2'}, use_global_device_ids=true, to_apply=%region_51.52 | all-reduce | flops 50 | bytes 400 | tf_op jit(solution)/shard_map/psum | solution.py:35
  386.6 4.8 collective-permute-done.4
  395.3 4.2 collective-permute-start.6
  448.5 4.5 multiply_reduce_fusion
  457.0 9.0 %all-reduce.10 = (f32[48]{0:T(128)}, f32[]{:T(128)}, f32[]{:T(128)}, f32[]{:T(128)}) all-reduce(f32[48]{0:T(128)} %convolution_bitcast_fusion.3, f32[]{:T(128)} %get-tuple-element.11, f32[]{:T(128)} %get-tuple-element.10, f32[]{:T(128)} %get-tuple-element.52), channel_id=1, replica_groups=mesh['gx_0'=4,'gx_1'=4,'gx_2'=4,'gy'=2] {'gx_0'}, use_global_device_ids=true, to_apply=%region_106.107 | all-reduce | flops 51 | bytes 408 | tf_op jit(solution)/shard_map/psum | solution.py:35
  466.0 8.4 %all-reduce.7 = (f32[48]{0:T(128)}, f32[]{:T(128)}, f32[]{:T(128)}, f32[]{:T(128)}) all-reduce(f32[48]{0:T(128)} %get-tuple-element.32, f32[]{:T(128)} %get-tuple-element.33, f32[]{:T(128)} %get-tuple-element.34, f32[]{:T(128)} %get-tuple-element.35), channel_id=1, replica_groups=mesh['gx_0'=4,'gx_1'=4,'gx_2'=4,'gy'=2] {'gx_1'}, use_global_device_ids=true, to_apply=%region_107.108 | all-reduce | flops 51 | bytes 408 | tf_op jit(solution)/shard_map/psum | solution.py:35
  474.5 8.5 %all-reduce.4 = (f32[48]{0:T(128)}, f32[]{:T(128)}, f32[]{:T(128)}, f32[]{:T(128)}) all-reduce(f32[48]{0:T(128)} %get-tuple-element.22, f32[]{:T(128)} %get-tuple-element.23, f32[]{:T(128)} %get-tuple-element.24, f32[]{:T(128)} %get-tuple-element.25), channel_id=1, replica_groups=mesh['gx_0'=4,'gx_1'=4,'gx_2'=4,'gy'=2] {'gx_2'}, use_global_device_ids=true, to_apply=%region_108.109 | all-reduce | flops 51 | bytes 408 | tf_op jit(solution)/shard_map/psum | solution.py:35
  503.6 6.1 %collective-permute-start.9 = (f32[3,1,8,128]{3,1,2,0:T(1,128)S(1)}, f32[3,1,8,128]{3,1,2,0:T(1,128)S(1)}, u32[]{:S(2)}, u32[]{:S(2)}) collective-permute-start(f32[3,1,8,128]{3,1,2,0:T(1,128)S(1)} %copy.298), channel_id=1, source_target_pairs={{2,0},{4,2},{6,4},{8,6},{10,8},{12,10},{14,12},{16,14},{18,16},{20... | collective-permute-start | bytes 36872 | tf_op jit(solution)/shard_map/ppermute | solution.py:27
  522.8 4.2 collective-permute-start.10
  (310 shorter events, 294.0 us)
Async XLA Ops:
  0.6 1.8 copy-start.10
  0.7 17.4 %copy-start.9 = (f32[3,1024]{1,0:T(4,128)S(1)}, f32[3,1024]{1,0:T(4,128)}, u32[]{:S(2)}) copy-start(f32[3,1024]{1,0:T(4,128)} %param.8) | copy-start | bytes 36868
  0.7 17.4 %copy-start = (f32[144,1024]{1,0:T(8,128)S(1)}, f32[144,1024]{1,0:T(8,128)}, u32[]{:S(2)}) copy-start(f32[144,1024]{1,0:T(8,128)} %param.7) | copy-start | bytes 1769476
  7.6 22.5 %all-to-all-start = ((s32[1,128,16]{2,0,1:T(1,128)}), s32[1,128,16]{2,0,1:T(1,128)S(1)}, u32[]{:S(2)}, u32[]{:S(2)}) async-start(s32[1,128,16]{2,0,1:T(1,128)} %bitcast.5), calls=%async_computation | async-start | bytes 131072 | tf_op jit(solution)/shard_map/all_to_all | solution.py:83
  30.1 73.8 %all-to-all-start.1 = ((f32[534,128,16]{0,2,1:T(8,128)}), f32[534,128,16]{0,2,1:T(8,128)}, u32[]{:S(2)}, u32[]{:S(2)}) async-start(f32[534,128,16]{0,2,1:T(8,128)} %bitcast.475), calls=%async_computation.1 | async-start | bytes 10485760 | tf_op jit(solution)/shard_map/all_to_all | solution.py:82
  186.9 6.1 %copy-start.2 = (f32[48,48]{1,0:T(8,128)}, f32[48,48]{1,0:T(8,128)S(1)}, u32[]{:S(2)}) copy-start(f32[48,48]{1,0:T(8,128)S(1)} %fusion.17) | copy-start | bytes 27652
  196.1 78.2 %collective-permute-start.1 = (f32[3,1,8,128]{3,1,2,0:T(1,128)}, f32[3,1,8,128]{3,1,2,0:T(1,128)}, u32[]{:S(2)}, u32[]{:S(2)}) collective-permute-start(f32[3,1,8,128]{3,1,2,0:T(1,128)} %copy.242), channel_id=1, source_target_pairs={{2,0},{4,2},{6,4},{8,6},{10,8},{12,10},{14,12},{16,14},{18,16},{20... | collective-permute-start | bytes 36872 | tf_op jit(solution)/shard_map/ppermute | solution.py:27
  199.1 75.3 %collective-permute-start = (f32[3,1,8,128]{3,1,2,0:T(1,128)}, f32[3,1,8,128]{3,1,2,0:T(1,128)}, u32[]{:S(2)}, u32[]{:S(2)}) collective-permute-start(f32[3,1,8,128]{3,1,2,0:T(1,128)} %copy.242), channel_id=1, source_target_pairs={{0,2},{2,4},{4,6},{6,8},{8,10},{10,12},{12,14},{14,16},{16,18},{18... | collective-permute-start | bytes 36872 | tf_op jit(solution)/shard_map/ppermute | solution.py:25
  275.6 8.3 %collective-permute-start.2 = (f32[3,3,1,128]{3,1,2,0:T(4,128)}, f32[3,3,1,128]{3,1,2,0:T(4,128)}, u32[]{:S(2)}, u32[]{:S(2)}) collective-permute-start(f32[3,3,1,128]{3,1,2,0:T(4,128)} %get-tuple-element.166), channel_id=1, source_target_pairs={{0,1},{2,3},{4,5},{6,7},{8,9},{10,11},{12,13},{14,15},{16,17},{18,... | collective-permute-start | bytes 13832 | tf_op jit(solution)/shard_map/ppermute | solution.py:25
  277.9 6.0 %collective-permute-start.3 = (f32[3,3,1,128]{3,1,2,0:T(4,128)}, f32[3,3,1,128]{3,1,2,0:T(4,128)}, u32[]{:S(2)}, u32[]{:S(2)}) collective-permute-start(f32[3,3,1,128]{3,1,2,0:T(4,128)} %get-tuple-element.167), channel_id=1, source_target_pairs={{1,0},{3,2},{5,4},{7,6},{9,8},{11,10},{13,12},{15,14},{17,16},{19,... | collective-permute-start | bytes 13832 | tf_op jit(solution)/shard_map/ppermute | solution.py:27
  377.4 7.8 %collective-permute-start.5 = (f32[3,1,8,128]{3,1,2,0:T(1,128)}, f32[3,1,8,128]{3,1,2,0:T(1,128)}, u32[]{:S(2)}, u32[]{:S(2)}) collective-permute-start(f32[3,1,8,128]{3,1,2,0:T(1,128)} %copy.283), channel_id=1, source_target_pairs={{2,0},{4,2},{6,4},{8,6},{10,8},{12,10},{14,12},{16,14},{18,16},{20... | collective-permute-start | bytes 36872 | tf_op jit(solution)/shard_map/ppermute | solution.py:27
  381.2 10.1 %collective-permute-start.4 = (f32[3,1,8,128]{3,1,2,0:T(1,128)}, f32[3,1,8,128]{3,1,2,0:T(1,128)}, u32[]{:S(2)}, u32[]{:S(2)}) collective-permute-start(f32[3,1,8,128]{3,1,2,0:T(1,128)} %copy.283), channel_id=1, source_target_pairs={{0,2},{2,4},{4,6},{6,8},{8,10},{10,12},{12,14},{14,16},{16,18},{18... | collective-permute-start | bytes 36872 | tf_op jit(solution)/shard_map/ppermute | solution.py:25
  392.7 8.6 %collective-permute-start.7 = (f32[3,3,1,128]{3,1,2,0:T(4,128)}, f32[3,3,1,128]{3,1,2,0:T(4,128)}, u32[]{:S(2)}, u32[]{:S(2)}) collective-permute-start(f32[3,3,1,128]{3,1,2,0:T(4,128)} %get-tuple-element.165), channel_id=1, source_target_pairs={{1,0},{3,2},{5,4},{7,6},{9,8},{11,10},{13,12},{15,14},{17,16},{19,... | collective-permute-start | bytes 13832 | tf_op jit(solution)/shard_map/ppermute | solution.py:27
  395.3 11.0 %collective-permute-start.6 = (f32[3,3,1,128]{3,1,2,0:T(4,128)}, f32[3,3,1,128]{3,1,2,0:T(4,128)}, u32[]{:S(2)}, u32[]{:S(2)}) collective-permute-start(f32[3,3,1,128]{3,1,2,0:T(4,128)} %get-tuple-element.164), channel_id=1, source_target_pairs={{0,1},{2,3},{4,5},{6,7},{8,9},{10,11},{12,13},{14,15},{16,17},{18,... | collective-permute-start | bytes 13832 | tf_op jit(solution)/shard_map/ppermute | solution.py:25
  503.6 19.2 %copy-start.5 = (f32[3,1,8,128]{3,1,2,0:T(1,128)}, f32[3,1,8,128]{3,1,2,0:T(1,128)S(1)}, u32[]{:S(2)}) copy-start(f32[3,1,8,128]{3,1,2,0:T(1,128)S(1)} %copy.298) | copy-start | bytes 36868
  503.6 10.6 %collective-permute-start.9 = (f32[3,1,8,128]{3,1,2,0:T(1,128)S(1)}, f32[3,1,8,128]{3,1,2,0:T(1,128)S(1)}, u32[]{:S(2)}, u32[]{:S(2)}) collective-permute-start(f32[3,1,8,128]{3,1,2,0:T(1,128)S(1)} %copy.298), channel_id=1, source_target_pairs={{2,0},{4,2},{6,4},{8,6},{10,8},{12,10},{14,12},{16,14},{18,16},{20... | collective-permute-start | bytes 36872 | tf_op jit(solution)/shard_map/ppermute | solution.py:27
  509.7 9.8 %collective-permute-start.8 = (f32[3,1,8,128]{3,1,2,0:T(1,128)S(1)}, f32[3,1,8,128]{3,1,2,0:T(1,128)S(1)}, u32[]{:S(2)}, u32[]{:S(2)}) collective-permute-start(f32[3,1,8,128]{3,1,2,0:T(1,128)S(1)} %copy.298), channel_id=1, source_target_pairs={{0,2},{2,4},{4,6},{6,8},{8,10},{10,12},{12,14},{14,16},{16,18},{18... | collective-permute-start | bytes 36872 | tf_op jit(solution)/shard_map/ppermute | solution.py:25
  514.2 8.5 %copy-start.3 = (f32[3,1,8,128]{3,1,2,0:T(1,128)}, f32[3,1,8,128]{3,1,2,0:T(1,128)S(1)}, u32[]{:S(2)}) copy-start(f32[3,1,8,128]{3,1,2,0:T(1,128)S(1)} %collective-permute-done.9) | copy-start | bytes 36868
  519.5 3.3 copy-start.4
  520.1 7.8 %collective-permute-start.11 = (f32[3,3,1,128]{3,1,2,0:T(4,128)}, f32[3,3,1,128]{3,1,2,0:T(4,128)}, u32[]{:S(2)}, u32[]{:S(2)}) collective-permute-start(f32[3,3,1,128]{3,1,2,0:T(4,128)} %get-tuple-element.163), channel_id=1, source_target_pairs={{1,0},{3,2},{5,4},{7,6},{9,8},{11,10},{13,12},{15,14},{17,16},{19,... | collective-permute-start | bytes 13832 | tf_op jit(solution)/shard_map/ppermute | solution.py:27
  522.8 10.2 %collective-permute-start.10 = (f32[3,3,1,128]{3,1,2,0:T(4,128)}, f32[3,3,1,128]{3,1,2,0:T(4,128)}, u32[]{:S(2)}, u32[]{:S(2)}) collective-permute-start(f32[3,3,1,128]{3,1,2,0:T(4,128)} %get-tuple-element.162), channel_id=1, source_target_pairs={{0,1},{2,3},{4,5},{6,7},{8,9},{10,11},{12,13},{14,15},{16,17},{18,... | collective-permute-start | bytes 13832 | tf_op jit(solution)/shard_map/ppermute | solution.py:25
  540.0 13.7 %copy-start.8 = (f32[3,8,128]{2,1,0:T(8,128)S(1)}, f32[3,8,128]{2,1,0:T(8,128)}, u32[]{:S(2)}) copy-start(f32[3,8,128]{2,1,0:T(8,128)} %multiply_reduce_fusion.4) | copy-start | bytes 36868
  540.9 13.9 %copy-start.7 = (f32[3,8,128]{2,1,0:T(8,128)S(1)}, f32[3,8,128]{2,1,0:T(8,128)}, u32[]{:S(2)}) copy-start(f32[3,8,128]{2,1,0:T(8,128)} %multiply_reduce_fusion.11) | copy-start | bytes 36868
  545.6 10.2 %copy-start.6 = (f32[3,8,128]{2,1,0:T(8,128)S(1)}, f32[3,8,128]{2,1,0:T(8,128)}, u32[]{:S(2)}) copy-start(f32[3,8,128]{2,1,0:T(8,128)} %multiply_reduce_fusion.5) | copy-start | bytes 36868
  (2 other events, 2.3 us)
where the time goes:
time: 571 us; the launch traced here: 562 us
  local copies, waits for them, and re-layouts  172 us (30%)
  blocking collectives  118 us (21%)
  other arithmetic  116 us (20%)
  waiting for transfers between devices  70.9 us (12%)
  starting transfers between devices  55.1 us (10%)
  matrix products  18 us (3%)
  between operations  12.2 us (2%)
    psum x12, blocking collectives, over_axes(): return functools.reduce(lax.psum, axes, shard)  118 us
    reduce_sum x69, other arithmetic, stencil(): total = total + jnp.sum(coef[k] * moved[None], axis=1)  62.8 us
    all_to_all x1, waiting for transfers between devices, body(): lax.all_to_all(buffer, GX_GY, split_axis=1, concat_axis=1, tiled=True)  62.2 us
    slice x29, local copies, waits for them, and re-layouts, stencil(): total = total + jnp.sum(coef[k] * moved[None], axis=1)  49.3 us
    reduce_sum x30, local copies, waits for them, and re-layouts, stencil(): total = total + jnp.sum(coef[k] * moved[None], axis=1)  44.8 us
    unnamed x81, local copies, waits for them, and re-layouts  27.7 us
    ppermute x6, starting transfers between devices, with_halo(): lax.ppermute(tail, axis, [(i, (i + 1) % count) for i in range(ends)])  19.3 us
    ppermute x6, starting transfers between devices, with_halo(): lax.ppermute(head, axis, [((i + 1) % count, i) for i in range(ends)])  15.1 us
  transfers between devices with their start and end apart: 14, of which 3 were waited for; matrix products, arithmetic and copies ran while one was open for 20% of the time, Pallas kernels for 0%

commit v1 on v0

v1 whole, which is shorter than its diff:
```python
import functools

import jax
import jax.numpy as jnp
from jax import lax
from jax.experimental import pallas as pl
from jax.experimental.pallas import tpu as pltpu
from jax.sharding import Mesh
from jax.sharding import PartitionSpec as P

CY = 8
CZ = 128
K = 48
SLOTS = 16
PEERS = 128
ROWS = 1024
N_GX = 64
GX_GY = ("gx_0", "gx_1", "gx_2", "gy")
GX = ("gx_0", "gx_1", "gx_2")
F32 = jnp.float32
BF16 = jnp.bfloat16
HIGHEST = lax.Precision.HIGHEST
WIRE = 50
NT = (((1,), (1,)), ((), ()))
TN = (((0,), (0,)), ((), ()))
MAIN = 3 * 128


def split(x):
    high = x.astype(BF16)
    return high, (x - high.astype(F32)).astype(BF16)


def exact_dot(x, y, dims=(((1,), (0,)), ((), ()))):
    return lax.dot_general(x, y, dims, precision=HIGHEST, preferred_element_type=F32)


def half_sum(x):
    return x[:, :128] + x[:, 128:]


def pack_kernel(op_ref, c_ref, b_ref, rows_ref, wire_ref, info_ref, s_ref, p_ref, a_ref):
    new_rows = rows_ref[...]
    target = new_rows // ROWS
    local = new_rows % ROWS
    onehot = lax.broadcasted_iota(jnp.int32, (PEERS, ROWS), 0) == target
    onehot_f = jnp.where(onehot, 1.0, 0.0).astype(F32)
    onehot_b = onehot_f.astype(BF16)
    before = lax.broadcasted_iota(jnp.int32, (128, 128), 0) < lax.broadcasted_iota(jnp.int32, (128, 128), 1)
    before = jnp.where(before, 1.0, 0.0).astype(BF16)
    ones = jnp.ones((128, 128), BF16)
    seen = jnp.zeros((PEERS, 128), F32)
    ranks = []
    for block in range(ROWS // 128):
        part = onehot_b[:, block * 128 : (block + 1) * 128]
        count = jnp.dot(part, before, preferred_element_type=F32) + seen
        ranks.append(jnp.sum(onehot_f[:, block * 128 : (block + 1) * 128] * count, axis=0, keepdims=True))
        seen = seen + jnp.dot(part, ones, preferred_element_type=F32)
    rank = jnp.concatenate(ranks, axis=1)
    rank_at = jnp.where(onehot, rank, -1.0)
    for k in range(SLOTS):
        s_ref[k * PEERS : (k + 1) * PEERS, :] = jnp.where(rank_at == k, 1.0, 0.0).astype(BF16)
    info_ref[0:1, :] = target
    info_ref[1:2, :] = rank.astype(jnp.int32)
    info_ref[2:3, :] = local
    info_ref[3:8, :] = jnp.zeros((5, ROWS), jnp.int32)

    def put(tile, start, x):
        high, low = split(x)
        p_ref[tile * 256 + start : tile * 256 + start + x.shape[0], :] = high
        p_ref[tile * 256 + 128 + start : tile * 256 + 128 + start + x.shape[0], :] = low

    put(0, 0, c_ref[0:128, :])
    put(1, 0, c_ref[128:144, :])
    put(1, 16, op_ref[0:112, :])
    put(2, 0, op_ref[112:240, :])
    for tile in range(3):
        moved = lax.dot_general(
            s_ref[...], p_ref[tile * 256 : (tile + 1) * 256, :], NT, preferred_element_type=F32
        )
        for k in range(SLOTS):
            wire_ref[pl.ds(tile * SLOTS + k, PEERS, stride=WIRE), :] = half_sum(moved[k * PEERS : (k + 1) * PEERS])

    at_rank = lax.broadcasted_iota(jnp.int32, (SLOTS, ROWS), 0).astype(F32) == rank
    rest = [op_ref[240 + i : 241 + i, :] for i in range(3)] + [b_ref[i : i + 1, :] for i in range(3)]
    rest = [jnp.where(at_rank, row, 0.0) for row in rest + [local.astype(F32)]]
    rest = jnp.concatenate(rest + [jnp.zeros((SLOTS, ROWS), F32)], axis=0)
    rest = jnp.concatenate(split(rest), axis=0)
    wire_ref[pl.ds(48, PEERS, stride=WIRE), :] = half_sum(
        lax.dot_general(onehot_b, rest, NT, preferred_element_type=F32)
    )

    gram = jnp.zeros((64, 128), F32)
    a_ref[48:128, :] = jnp.zeros((80, ROWS), F32)
    for a in range(3):
        a_ref[0:48, :] = c_ref[a * K : (a + 1) * K, :]
        a_ref[48:49, :] = b_ref[a : a + 1, :]
        gram = gram + exact_dot(a_ref[0:64, :], a_ref[...], NT)
    wire_ref[pl.ds(49, PEERS, stride=WIRE), :] = jnp.concatenate([gram, jnp.zeros((64, 128), F32)], axis=0)


def two_level(values, labels, left_ref, right_ref):
    count = len(values)
    eight = lax.broadcasted_iota(jnp.int32, (CY, 128), 0)
    lanes = lax.broadcasted_iota(jnp.int32, (128, 128), 0)
    for k in range(SLOTS):
        label = labels[k].astype(jnp.int32)
        y, z = label // CZ, label % CZ
        cols = slice(k * 128, (k + 1) * 128)
        right_ref[:, cols] = jnp.where(lanes == z, 1.0, 0.0).astype(BF16)
        here = eight == y
        for c in range(count):
            left_ref[c * CY : (c + 1) * CY, cols] = jnp.where(here, values[c][k], 0.0)
    high, low = split(left_ref[0 : count * CY, :])
    right = right_ref[...]
    return lax.dot_general(high, right, NT, preferred_element_type=F32) + lax.dot_general(
        low, right, NT, preferred_element_type=F32
    )


def unpack_kernel(wire_ref, main_ref, ext_ref, t_ref, r_ref, left_ref, right_ref):
    rest = wire_ref[pl.ds(48, PEERS, stride=WIRE), :].T
    labels = [rest[6 * SLOTS + k : 6 * SLOTS + k + 1, :] for k in range(SLOTS)]
    node = lax.broadcasted_iota(jnp.int32, (ROWS, 128), 0).astype(F32)
    for k in range(SLOTS):
        t_ref[:, k * 128 : (k + 1) * 128] = jnp.where(node == labels[k], 1.0, 0.0).astype(BF16)
    for tile in range(3):
        for k in range(SLOTS):
            high, low = split(wire_ref[pl.ds(tile * SLOTS + k, PEERS, stride=WIRE), :])
            r_ref[k * 128 : (k + 1) * 128, 0:128] = high
            r_ref[k * 128 : (k + 1) * 128, 128:256] = low
        moved = jnp.dot(t_ref[...], r_ref[...], preferred_element_type=F32)
        for y in range(CY):
            block = half_sum(moved[y * CZ : (y + 1) * CZ])
            main_ref[pl.ds(tile * 128 * CY + y, 128, stride=CY), :] = block.T
    values = [[rest[f * SLOTS + k : f * SLOTS + k + 1, :] for k in range(SLOTS)] for f in range(6)]
    ext_ref[...] = two_level(values, labels, left_ref, right_ref)


def minus_combined(start, main_ref, weights):
    result = []
    for a in range(3):
        total = start[a]
        for m in range(K):
            row = (a * K + m) * CY
            total = total - main_ref[row : row + CY, :] * weights[m : m + 1, :]
        result.append(total)
    return result


def put_vector(vector, side_ref, v_ref, line_ref):
    lower = side_ref[0] == 0
    line_ref[...] = jnp.zeros((8, 128), F32)
    for a in range(3):
        v_ref[a * CY : (a + 1) * CY, :] = vector[a]
        line_ref[a : a + 1, :] = jnp.where(lower, vector[a][7:8, :], vector[a][0:1, :])


def first_kernel(side_ref, gram_ref, main_ref, ext_ref, v_ref, line_ref, inv_ref, start_ref, beta_ref):
    rows = gram_ref[0:48, :]
    row_id = lax.broadcasted_iota(jnp.int32, (K, 128), 0)
    lane = lax.broadcasted_iota(jnp.int32, (K, 128), 1)
    work = jnp.where(lane < K + 1, rows, jnp.where(lane - 64 == row_id, 1.0, 0.0))
    for j in range(K - 1):
        pivot = work[j : j + 1, :]
        scale = jnp.where(row_id > j, work[:, j : j + 1], 0.0) * (1.0 / work[j : j + 1, j : j + 1])
        work = work - scale * pivot
    diagonal = jnp.sum(jnp.where(lane == row_id, work, 0.0), axis=1, keepdims=True)
    work = work * (1.0 / jnp.sqrt(diagonal))
    start = jnp.broadcast_to(work[:, K : K + 1], (K, 128))
    inverse = jnp.where(lane < K, pltpu.roll(work, 64, 1), 0.0)
    inv_ref[...] = inverse
    start_ref[...] = start
    weights = exact_dot(inverse, start, TN)
    load_sq = jnp.broadcast_to(gram_ref[48:49, 48:49], (1, 128))
    beta = jnp.sqrt(load_sq - jnp.sum(start * start, axis=0, keepdims=True))
    beta_ref[...] = jnp.broadcast_to(beta, (8, 128))
    load = [ext_ref[24 + a * CY : 24 + (a + 1) * CY, :] for a in range(3)]
    vector = minus_combined(load, main_ref, weights)
    put_vector([v / beta for v in vector], side_ref, v_ref, line_ref)


def put_plane(pad_ref, dx, plane, line, side):
    for a in range(3):
        base = (dx * 3 + a) * 24
        edge = line[a : a + 1, :]
        pad_ref[base + 7 : base + 8, :] = jnp.where(side == 1, edge, 0.0)
        pad_ref[base + 8 : base + 16, :] = plane[a * CY : (a + 1) * CY, :]
        pad_ref[base + 16 : base + 17, :] = jnp.where(side == 0, edge, 0.0)


def stencil(main_ref, ext_ref, pad_ref):
    lane = lax.broadcasted_iota(jnp.int32, (CY, 128), 1)
    total = [jnp.zeros((CY, 128), F32) for _ in range(3)]
    for dx in range(3):
        for dy in range(3):
            for b in range(3):
                start = (dx * 3 + b) * 24 + 7 + dy
                here = pad_ref[start : start + CY, :]
                left = jnp.where(lane == 0, 0.0, pltpu.roll(here, 1, 1))
                right = jnp.where(lane == 127, 0.0, pltpu.roll(here, 127, 1))
                for dz, moved in enumerate((left, here, right)):
                    for a in range(3):
                        q = ((dx * 9 + dy * 3 + dz) * 3 + a) * 3 + b
                        if q < 240:
                            row = (3 * K + q) * CY
                            total[a] = total[a] + main_ref[row : row + CY, :] * moved
                        else:
                            row = (q - 240) * CY
                            total[a] = total[a] + ext_ref[row : row + CY, :] * moved
    return total


def image_kernel(count, side_ref, main_ref, ext_ref, line_ref, up_ref, down_ref, *refs):
    vectors, (image_ref, send_ref, pad_ref, part_ref) = refs[:count], refs[count:]
    side = side_ref[0]
    put_plane(pad_ref, 0, up_ref[0:24, :], up_ref[24:32, :], side)
    put_plane(pad_ref, 1, vectors[-1][...], line_ref[...], side)
    put_plane(pad_ref, 2, down_ref[0:24, :], down_ref[24:32, :], side)
    image = stencil(main_ref, ext_ref, pad_ref)
    for a in range(3):
        image_ref[a * CY : (a + 1) * CY, :] = image[a]
    for m in range(K):
        rows = [(a * K + m) * CY for a in range(3)]
        part_ref[m * CY : (m + 1) * CY, :] = sum(
            main_ref[row : row + CY, :] * image[a] for a, row in enumerate(rows)
        )
    others = [image] + [[ref[a * CY : (a + 1) * CY, :] for a in range(3)] for ref in vectors]
    for i in range(8):
        m = K + i
        if i < len(others):
            part_ref[m * CY : (m + 1) * CY, :] = sum(o * w for o, w in zip(others[i], image))
        else:
            part_ref[m * CY : (m + 1) * CY, :] = jnp.zeros((CY, 128), F32)
    part = sum(part_ref[pl.ds(y, K + 8, stride=CY), :] for y in range(CY))
    part = jnp.concatenate([part, jnp.zeros((128 - K - 8, 128), F32)], axis=0)
    send_ref[...] = exact_dot(jnp.ones((PEERS, 128), F32), part, NT)


def totals(got_ref):
    return exact_dot(got_ref[...], jnp.ones((PEERS, 128), F32), TN)


def next_kernel(side_ref, got_ref, main_ref, image_ref, one_ref, inv_ref, v_ref, line_ref, proj_ref, h_ref):
    sums = totals(got_ref)
    inverse = inv_ref[...]
    projection = exact_dot(inverse, sums)
    h11 = sums[K + 1 : K + 2, :]
    h21 = jnp.sqrt(sums[K : K + 1, :] - jnp.sum(projection * projection, axis=0, keepdims=True) - h11 * h11)
    weights = exact_dot(inverse, projection, TN)
    begin = [
        image_ref[a * CY : (a + 1) * CY, :] - h11 * one_ref[a * CY : (a + 1) * CY, :] for a in range(3)
    ]
    vector = minus_combined(begin, main_ref, weights)
    put_vector([v / h21 for v in vector], side_ref, v_ref, line_ref)
    proj_ref[...] = projection
    h_ref[...] = jnp.zeros((8, 128), F32)
    h_ref[0:1, :] = h11
    h_ref[1:2, :] = h21


def send_kernel(got_ref, inv_ref, start_ref, proj_ref, h_ref, beta_ref, u_ref, info_ref, wire_ref, y_ref):
    sums = totals(got_ref)
    inverse = inv_ref[...]
    proj_two = exact_dot(inverse, sums)
    h11, h21 = h_ref[0:1, :], h_ref[1:2, :]
    h12, h22 = sums[K + 1 : K + 2, :], sums[K + 2 : K + 3, :]
    h32_sq = sums[K : K + 1, :] - jnp.sum(proj_two * proj_two, axis=0, keepdims=True) - h12 * h12 - h22 * h22
    h32 = jnp.sqrt(h32_sq)
    beta = beta_ref[0:1, :]
    m11 = h11 * h11 + h21 * h21
    m12 = h11 * h12 + h21 * h22
    m22 = h12 * h12 + h22 * h22 + h32 * h32
    g_one = beta * h11
    g_two = beta * h12
    determ = m11 * m22 - m12 * m12
    y_one = (m22 * g_one - m12 * g_two) / determ
    y_two = (m11 * g_two - m12 * g_one) / determ
    y_ref[...] = jnp.zeros((8, 128), F32)
    y_ref[0:1, :] = y_one
    y_ref[1:2, :] = y_two
    mixing = start_ref[...] - y_one * proj_ref[...] - y_two * proj_two
    weights = exact_dot(inverse, mixing, TN)[0:K]
    wide = jnp.concatenate([weights] * (ROWS // 128), axis=1)
    target, rank, local = (info_ref[i : i + 1, :] for i in range(3))
    at_rank = lax.broadcasted_iota(jnp.int32, (SLOTS, ROWS), 0) == rank
    rows = [jnp.sum(u_ref[a * K : (a + 1) * K, :] * wide, axis=0, keepdims=True) for a in range(3)]
    rows = jnp.concatenate([jnp.where(at_rank, r, 0.0) for r in rows + [local.astype(F32)]], axis=0)
    rows = jnp.concatenate(split(rows), axis=0)
    onehot = lax.broadcasted_iota(jnp.int32, (PEERS, ROWS), 0) == target
    onehot = jnp.where(onehot, 1.0, 0.0).astype(BF16)
    mine = lax.dot_general(onehot, rows, NT, preferred_element_type=F32)
    mine = mine + pltpu.roll(mine, 64, 1)
    peer = lax.broadcasted_iota(jnp.int32, (PEERS, 128), 0)
    lane = lax.broadcasted_iota(jnp.int32, (PEERS, 128), 1)
    other = jnp.where(peer % 2 == 0, pltpu.roll(mine, PEERS - 1, 0), pltpu.roll(mine, 1, 0))
    pair = jnp.where(lane < 64, mine, other)
    wire_ref[pl.ds(0, PEERS, stride=3), :] = jnp.where(peer < 2, 0.0, pltpu.roll(pair, 2, 0))
    wire_ref[pl.ds(1, PEERS, stride=3), :] = pair
    wire_ref[pl.ds(2, PEERS, stride=3), :] = jnp.where(peer >= PEERS - 2, 0.0, pltpu.roll(pair, PEERS - 2, 0))


def last_kernel(
    side_ref, got_ref, main_ref, ext_ref, y_ref, one_ref, two_ref, im_one_ref, im_two_ref,
    sol_ref, res_ref, left_ref, right_ref, pad_ref,
):
    side = side_ref[0]
    for dx in range(3):
        got = got_ref[pl.ds(dx, PEERS, stride=3), :].T
        planes = []
        for base in (0, 64):
            values = [
                [got[base + a * SLOTS + k : base + a * SLOTS + k + 1, :] for k in range(SLOTS)] for a in range(3)
            ]
            labels = [got[base + 48 + k : base + 49 + k, :] for k in range(SLOTS)]
            planes.append(two_level(values, labels, left_ref, right_ref))
        own, other = planes
        lines = [
            jnp.where(side == 0, other[a * CY : a * CY + 1, :], other[a * CY + 7 : a * CY + 8, :]) for a in range(3)
        ]
        put_plane(pad_ref, dx, own, jnp.concatenate(lines, axis=0), side)
        if dx == 1:
            term = own
    image = stencil(main_ref, ext_ref, pad_ref)
    y_one, y_two = y_ref[0:1, :], y_ref[1:2, :]
    solution = term + y_one * one_ref[...] + y_two * two_ref[...]
    for a in range(3):
        rows = slice(a * CY, (a + 1) * CY)
        residual = ext_ref[24 + a * CY : 24 + (a + 1) * CY, :] - image[a]
        residual = residual - y_one * im_one_ref[rows, :] - y_two * im_two_ref[rows, :]
        for y in range(CY):
            cols = slice(y * CZ, (y + 1) * CZ)
            sol_ref[a : a + 1, cols] = solution[a * CY + y : a * CY + y + 1, :]
            res_ref[a : a + 1, cols] = residual[y : y + 1, :]


def shape(*dims, dtype=F32):
    return jax.ShapeDtypeStruct(dims, dtype)


def call(kernel, outs, scratch=(), scalars=0, inputs=0, limit=40, cost=None):
    smem = [pl.BlockSpec(memory_space=pltpu.SMEM)] * scalars
    vmem = [pl.BlockSpec(memory_space=pltpu.VMEM)] * (inputs - scalars)
    return pl.pallas_call(
        kernel,
        out_shape=outs,
        in_specs=smem + vmem,
        out_specs=tuple(pl.BlockSpec(memory_space=pltpu.VMEM) for _ in outs),
        scratch_shapes=list(scratch),
        compiler_params=pltpu.CompilerParams(vmem_limit_bytes=limit * 2**20),
        cost_estimate=cost,
    )


def exchange(rows):
    count = rows.shape[0] // PEERS
    shaped = rows.reshape(PEERS, count, 1, 128)
    got = lax.all_to_all(shaped, GX_GY, split_axis=0, concat_axis=0, tiled=True)
    return got.reshape(PEERS * count, 128)


def halo(vector, line):
    other = lax.ppermute(line, "gy", [(0, 1), (1, 0)])
    plane = jnp.concatenate([vector, other], axis=0)
    up = lax.ppermute(plane, GX, [(i, i + 1) for i in range(N_GX - 1)])
    down = lax.ppermute(plane, GX, [(i + 1, i) for i in range(N_GX - 1)])
    return other, up, down


def body(operator, basis_u, basis_c, right_side, new_rows):
    side = lax.axis_index("gy").astype(jnp.int32).reshape(1)
    wire, info = call(
        pack_kernel,
        (shape(PEERS * WIRE, 128), shape(8, ROWS, dtype=jnp.int32)),
        [
            pltpu.VMEM((PEERS * SLOTS, ROWS), BF16),
            pltpu.VMEM((2 * MAIN, ROWS), BF16),
            pltpu.VMEM((128, ROWS), F32),
        ],
        inputs=4,
    )(operator, basis_c, right_side, new_rows.reshape(1, ROWS))
    got = exchange(wire)
    gram_row = jnp.sum(got.reshape(PEERS, WIRE, 128)[:, WIRE - 1], axis=0, keepdims=True)
    gram = exchange(jnp.broadcast_to(gram_row, (PEERS, 128)))
    two_level_scratch = [pltpu.VMEM((48, SLOTS * PEERS), F32), pltpu.VMEM((128, SLOTS * PEERS), BF16)]
    main, ext = call(
        unpack_kernel,
        (shape(MAIN * CY, 128), shape(48, 128)),
        [pltpu.VMEM((ROWS, SLOTS * PEERS), BF16), pltpu.VMEM((SLOTS * PEERS, 256), BF16), *two_level_scratch],
        inputs=1,
        cost=pl.CostEstimate(flops=4 * 10**9, bytes_accessed=5 * 10**6, transcendentals=0),
    )(got)
    vector_outs = (shape(3 * CY, 128), shape(8, 128))
    one, line, inverse, start, beta = call(
        first_kernel, (*vector_outs, shape(K, 128), shape(K, 128), shape(8, 128)), scalars=1, inputs=4
    )(side, gram, main, ext)
    pad = pltpu.VMEM((9 * 24, 128), F32)
    image_scratch = [pad, pltpu.VMEM(((K + 8) * CY, 128), F32)]
    image_outs = (shape(3 * CY, 128), shape(PEERS, 128))
    image_one, send = call(functools.partial(image_kernel, 1), image_outs, image_scratch, scalars=1, inputs=7)(
        side, main, ext, *halo(one, line), one
    )
    sums = exchange(send)
    two, line, proj_one, h_one = call(
        next_kernel, (*vector_outs, shape(K, 128), shape(8, 128)), scalars=1, inputs=6
    )(side, sums, main, image_one, one, inverse)
    image_two, send = call(functools.partial(image_kernel, 2), image_outs, image_scratch, scalars=1, inputs=8)(
        side, main, ext, *halo(two, line), one, two
    )
    sums = exchange(send)
    wire, y = call(send_kernel, (shape(PEERS * 3, 128), shape(8, 128)), inputs=8)(
        sums, inverse, start, proj_one, h_one, beta, basis_u, info
    )
    got = exchange(wire)
    return call(
        last_kernel, (shape(3, ROWS), shape(3, ROWS)), [*two_level_scratch, pad], scalars=1, inputs=9
    )(side, got, main, ext, y, one, two, image_one, image_two)


def solution(mesh):
    torus = Mesh(mesh.devices.reshape(4, 4, 4, mesh.shape["gy"]), ("gx_0", "gx_1", "gx_2", "gy"))
    placed = (P(None, GX_GY), P(None, GX_GY), P(None, GX_GY), P(None, GX_GY), P(GX_GY))
    return jax.shard_map(
        body,
        mesh=torus,
        in_specs=placed,
        out_specs=(P(None, GX_GY), P(None, GX_GY)),
        check_vma=False,
    )
```

time: 571 us -> 167 us (0.29); the launches traced: 562 us -> 165 us
  local copies, waits for them, and re-layouts: 172 us -> 9.59 us
  other arithmetic: 116 us -> 0.03 us
  blocking collectives: 118 us -> 40.5 us
  starting transfers between devices: 55.1 us -> 28.3 us
  Pallas kernels: 0 us -> 22.1 us
  matrix products: 18 us -> 0 us
  between operations: 12.2 us -> 0.82 us
  waiting for transfers between devices: 70.9 us -> 63.6 us
    psum x12 -> x0, blocking collectives: 118 us -> none  [over_axes(): return functools.reduce(lax.psum, axes, shard)]
    reduce_sum x77 -> x1, other arithmetic: 79.6 us -> 0.03 us  [body(): jnp.sum(got.reshape(PEERS, WIRE, 128)[:, WIRE - 1], axis=0, keepdims=True)]
    slice x36 -> x0, local copies, waits for them, and re-layouts: 57.8 us -> none  [the longest x29 49.3 us: stencil(): total = total + jnp.sum(coef[k] * moved[None], axis=1)]
    reduce_sum x30 -> x0, local copies, waits for them, and re-layouts: 44.8 us -> none  [stencil(): total = total + jnp.sum(coef[k] * moved[None], axis=1)]
    all_to_all x0 -> x3, blocking collectives: none -> 40.5 us  [exchange(): got = lax.all_to_all(shaped, GX_GY, split_axis=0, concat_axis=0, tiled=True)]
    pallas_call x0 -> x8, Pallas kernels: none -> 22.1 us  [the longest x1 6.41 us: body(): call(first_kernel, (*vector_outs, shape(K, 128), shape(K, 128), shape(8,...]
    ppermute x12 -> x6, starting transfers between devices: 34.4 us -> 13 us  [the longest x2 8.73 us: halo(): down = lax.ppermute(plane, GX, [(i + 1, i) for i in range(N_GX - 1)])]
    unnamed x81 -> x18, local copies, waits for them, and re-layouts: 27.7 us -> 8.5 us
  transfers between devices with their start and end apart: 14 -> 8, of which waited for: 3 -> 6; matrix products, arithmetic and copies ran while one was open for 20% -> 0% of each run, Pallas kernels for 0% -> 3%
where the time goes in v1:
time: 167 us; the launch traced here: 165 us
  waiting for transfers between devices  63.6 us (38%)
  blocking collectives  40.5 us (24%)
  starting transfers between devices  28.3 us (17%)
  Pallas kernels  22.1 us (13%)
  local copies, waits for them, and re-layouts  9.59 us (6%)
    all_to_all x2, waiting for transfers between devices, exchange(): got = lax.all_to_all(shaped, GX_GY, split_axis=0, concat_axis=0, tiled=True)  45.7 us
    all_to_all x3, blocking collectives, exchange(): got = lax.all_to_all(shaped, GX_GY, split_axis=0, concat_axis=0, tiled=True)  40.5 us
    ppermute x2, waiting for transfers between devices, halo(): up = lax.ppermute(plane, GX, [(i, i + 1) for i in range(N_GX - 1)])  15.6 us
    all_to_all x2, starting transfers between devices, exchange(): got = lax.all_to_all(shaped, GX_GY, split_axis=0, concat_axis=0, tiled=True)  15.4 us
    ppermute x2, starting transfers between devices, halo(): down = lax.ppermute(plane, GX, [(i + 1, i) for i in range(N_GX - 1)])  8.73 us
    unnamed x18, local copies, waits for them, and re-layouts  8.5 us
    pallas_call x1, Pallas kernels, body(): call(first_kernel, (*vector_outs, shape(K, 128), shape(K, 128), shape(8,...  6.41 us
    pallas_call x1, Pallas kernels, body(): call(pack_kernel, (shape(PEERS * WIRE, 128), shape(8, ROWS, dtype=jnp.int...  5.37 us
  transfers between devices with their start and end apart: 8, of which 6 were waited for; matrix products, arithmetic and copies ran while one was open for 0% of the time, Pallas kernels for 3%

profile of v1, /device:TPU:2, one launch (start us, length us, event | category | flops | bytes accessed | tf_op | source)
XLA Modules:
  0.0 165.0 jit_solution(3453895704840008978)
XLA Ops:
  0.6 1.2 copy-done.3
  4.3 5.4 %shard_map.68 = (f32[6400,128]{1,0:T(8,128)S(1)}, s32[8,1024]{1,0:T(8,128)S(1)}) custom-call(f32[243,1024]{1,0:T(8,128)S(1)} %copy-done.3, f32[144,1024]{1,0:T(8,128)S(1)} %copy-done.4, f32[3,1024]{1,0:T(4,128)S(1)} %copy-done.6, s32[1,1024]{1,0:T(1,128)S(1)} %bitcast.27), custom_call_target="tpu_custom_call" | custom-call | tf_op jit(solution)/shard_map/pallas_call | solution.py:372
  9.7 1.7 %copy-done.2 = f32[6400,128]{1,0:T(8,128)} copy-done((f32[6400,128]{1,0:T(8,128)}, f32[6400,128]{1,0:T(8,128)S(1)}, u32[]{:S(2)}) %copy-start.2) | copy-done | bytes 3276824
  11.4 10.5 %all-to-all-start = ((f32[128,50,1,128]{3,2,1,0:T(1,128)}), f32[128,50,1,128]{3,2,1,0:T(1,128)S(1)}, u32[]{:S(2)}, u32[]{:S(2)}) async-start(f32[128,50,1,128]{3,2,1,0:T(1,128)} %bitcast.19), calls=%async_computation | async-start | bytes 6553600 | tf_op jit(solution)/shard_map/all_to_all | solution.py:358
  21.9 42.9 %all-to-all-done = f32[128,50,1,128]{3,2,1,0:T(1,128)S(1)} async-done(((f32[128,50,1,128]{3,2,1,0:T(1,128)}), f32[128,50,1,128]{3,2,1,0:T(1,128)S(1)}, u32[]{:S(2)}, u32[]{:S(2)}) %all-to-all-start) | async-done | bytes 3276832 | tf_op jit(solution)/shard_map/all_to_all | solution.py:358
  65.2 1.2 copy-done
  67.1 4.9 %all-to-all-start.1 = ((f32[128,1,1,128]{3,2,1,0:T(1,128)}), f32[128,1,1,128]{3,2,1,0:T(1,128)S(1)}, u32[]{:S(2)}, u32[]{:S(2)}) async-start(f32[128,1,1,128]{3,2,1,0:T(1,128)} %reshape.45), calls=%async_computation.1 | async-start | bytes 131072 | tf_op jit(solution)/shard_map/all_to_all | solution.py:358
  72.0 1.9 %copy-done.1 = f32[128,50,1,128]{3,2,1,0:T(1,128)S(1)} copy-done((f32[128,50,1,128]{3,2,1,0:T(1,128)S(1)}, f32[128,50,1,128]{3,2,1,0:T(1,128)}, u32[]{:S(2)}) %copy-start.1) | copy-done | bytes 3276824
  73.9 4.5 %shard_map.69 = (f32[3072,128]{1,0:T(8,128)S(1)}, f32[48,128]{1,0:T(8,128)S(1)}) custom-call(f32[6400,128]{1,0:T(8,128)S(1)} %bitcast.18), custom_call_target="tpu_custom_call" | custom-call | flops 4000000000 | bytes 5000000 | tf_op jit(solution)/shard_map/pallas_call | solution.py:386
  78.4 2.8 %all-to-all-done.1 = f32[128,1,1,128]{3,2,1,0:T(1,128)S(1)} async-done(((f32[128,1,1,128]{3,2,1,0:T(1,128)}), f32[128,1,1,128]{3,2,1,0:T(1,128)S(1)}, u32[]{:S(2)}, u32[]{:S(2)}) %all-to-all-start.1) | async-done | bytes 65568 | tf_op jit(solution)/shard_map/all_to_all | solution.py:358
  81.2 6.4 %shard_map.70 = (f32[24,128]{1,0:T(8,128)S(1)}, f32[8,128]{1,0:T(8,128)S(1)}, f32[48,128]{1,0:T(8,128)S(1)}, f32[48,128]{1,0:T(8,128)S(1)}, f32[8,128]{1,0:T(8,128)S(1)}) custom-call(s32[1]{0:T(128)} %bitcast.side_ref, f32[128,128]{1,0:T(8,128)S(1)} %bitcast.21, f32[3072,128]{1,0:T(8,128)S(1)} %get-tuple-element.22.main_ref, ...), custom_call_target="tpu_custom_call" | custom-call | tf_op jit(solution)/shard_map/pallas_call | solution.py:394
  87.8 1.1 collective-permute-done.line_ref
  88.9 4.9 %collective-permute-start.2 = (f32[32,128]{1,0:T(8,128)S(1)}, f32[32,128]{1,0:T(8,128)S(1)}, u32[]{:S(2)}, u32[]{:S(2)}) collective-permute-start(f32[32,128]{1,0:T(8,128)S(1)} %constant_dynamic-update-slice_fusion), channel_id=1, source_target_pairs={{2,0},{4,2},{6,4},{8,6},{10,8},{12,10},{14,12},{16,14},{18,16},{20... | collective-permute-start | bytes 49160 | tf_op jit(solution)/shard_map/ppermute | solution.py:366
  93.8 2.1 %collective-permute-start.1 = (f32[32,128]{1,0:T(8,128)S(1)}, f32[32,128]{1,0:T(8,128)S(1)}, u32[]{:S(2)}, u32[]{:S(2)}) collective-permute-start(f32[32,128]{1,0:T(8,128)S(1)} %constant_dynamic-update-slice_fusion), channel_id=1, source_target_pairs={{0,2},{2,4},{4,6},{6,8},{8,10},{10,12},{12,14},{14,16},{16,18},{18... | collective-permute-start | bytes 49160 | tf_op jit(solution)/shard_map/ppermute | solution.py:365
  95.9 7.7 %collective-permute-done.1.up_ref = f32[32,128]{1,0:T(8,128)S(1)} collective-permute-done((f32[32,128]{1,0:T(8,128)S(1)}, f32[32,128]{1,0:T(8,128)S(1)}, u32[]{:S(2)}, u32[]{:S(2)}) %collective-permute-start.1) | collective-permute-done | bytes 16416 | tf_op jit(solution)/shard_map/ppermute | solution.py:365
  104.1 13.4 %all_to_all.25 = f32[128,1,1,128]{3,2,1,0:T(1,128)S(1)} all-to-all(f32[128,1,1,128]{3,2,1,0:T(1,128)S(1)} %bitcast.25), channel_id=1, replica_groups=mesh['gx_0'=4,'gx_1'=4,'gx_2'=4,'gy'=2] {'gx_0','gx_1','gx_2','gy'}, dimensions={0} | all-to-all | bytes 131072 | tf_op jit(solution)/shard_map/all_to_all | solution.py:358
  118.2 1.1 collective-permute-done.3.line_ref
  119.4 3.9 %collective-permute-start.5 = (f32[32,128]{1,0:T(8,128)S(1)}, f32[32,128]{1,0:T(8,128)S(1)}, u32[]{:S(2)}, u32[]{:S(2)}) collective-permute-start(f32[32,128]{1,0:T(8,128)S(1)} %constant_dynamic-update-slice_fusion.2), channel_id=1, source_target_pairs={{2,0},{4,2},{6,4},{8,6},{10,8},{12,10},{14,12},{16,14},{18,16},{20... | collective-permute-start | bytes 49160 | tf_op jit(solution)/shard_map/ppermute | solution.py:366
  123.3 2.0 %collective-permute-start.4 = (f32[32,128]{1,0:T(8,128)S(1)}, f32[32,128]{1,0:T(8,128)S(1)}, u32[]{:S(2)}, u32[]{:S(2)}) collective-permute-start(f32[32,128]{1,0:T(8,128)S(1)} %constant_dynamic-update-slice_fusion.2), channel_id=1, source_target_pairs={{0,2},{2,4},{4,6},{6,8},{8,10},{10,12},{12,14},{14,16},{16,18},{18... | collective-permute-start | bytes 49160 | tf_op jit(solution)/shard_map/ppermute | solution.py:365
  125.2 7.9 %collective-permute-done.4.up_ref = f32[32,128]{1,0:T(8,128)S(1)} collective-permute-done((f32[32,128]{1,0:T(8,128)S(1)}, f32[32,128]{1,0:T(8,128)S(1)}, u32[]{:S(2)}, u32[]{:S(2)}) %collective-permute-start.4) | collective-permute-done | bytes 16416 | tf_op jit(solution)/shard_map/ppermute | solution.py:365
  133.6 12.5 %all_to_all.26 = f32[128,1,1,128]{3,2,1,0:T(1,128)S(1)} all-to-all(f32[128,1,1,128]{3,2,1,0:T(1,128)S(1)} %bitcast.26), channel_id=1, replica_groups=mesh['gx_0'=4,'gx_1'=4,'gx_2'=4,'gy'=2] {'gx_0','gx_1','gx_2','gy'}, dimensions={0} | all-to-all | bytes 131072 | tf_op jit(solution)/shard_map/all_to_all | solution.py:358
  146.0 1.1 shard_map.74
  147.1 14.7 %all_to_all.27 = f32[128,3,1,128]{3,2,1,0:T(1,128)S(1)} all-to-all(f32[128,3,1,128]{3,2,1,0:T(1,128)S(1)} %bitcast.24), channel_id=1, replica_groups=mesh['gx_0'=4,'gx_1'=4,'gx_2'=4,'gy'=2] {'gx_0','gx_1','gx_2','gy'}, dimensions={0} | all-to-all | bytes 393216 | tf_op jit(solution)/shard_map/all_to_all | solution.py:358
  161.8 3.2 %shard_map.75 = (f32[3,1024]{1,0:T(4,128)}, f32[3,1024]{1,0:T(4,128)}) custom-call(s32[1]{0:T(128)} %bitcast.side_ref, f32[384,128]{1,0:T(8,128)S(1)} %bitcast.20, f32[3072,128]{1,0:T(8,128)S(1)} %get-tuple-element.22.main_ref, f32[48,128]{1,0:T(8,128)S(1)} %get-tuple-element.23.ext_ref, f32[8,128]{1,0:T(8,128)S(1)} %get-tuple-element.38.y_ref, ...), custom_call_target="tpu_custom_call" | custom-call | tf_op jit(solution)/shard_map/pallas_call | solution.py:415
  (26 shorter events, 5.3 us)
Async XLA Ops:
  0.6 1.2 copy-start.3
  1.8 1.1 copy-start.4
  2.9 0.7 copy-start.6
  3.6 0.7 copy-start.7
  9.7 1.7 %copy-start.2 = (f32[6400,128]{1,0:T(8,128)}, f32[6400,128]{1,0:T(8,128)S(1)}, u32[]{:S(2)}) copy-start(f32[6400,128]{1,0:T(8,128)S(1)} %get-tuple-element.21) | copy-start | bytes 9830404
  11.4 53.4 %all-to-all-start = ((f32[128,50,1,128]{3,2,1,0:T(1,128)}), f32[128,50,1,128]{3,2,1,0:T(1,128)S(1)}, u32[]{:S(2)}, u32[]{:S(2)}) async-start(f32[128,50,1,128]{3,2,1,0:T(1,128)} %bitcast.19), calls=%async_computation | async-start | bytes 6553600 | tf_op jit(solution)/shard_map/all_to_all | solution.py:358
  64.7 1.7 %copy-start = (f32[128,50,1,128]{3,2,1,0:T(1,128)}, f32[128,50,1,128]{3,2,1,0:T(1,128)S(1)}, u32[]{:S(2)}) copy-start(f32[128,50,1,128]{3,2,1,0:T(1,128)S(1)} %all-to-all-done) | copy-start | bytes 9830404
  67.1 14.1 %all-to-all-start.1 = ((f32[128,1,1,128]{3,2,1,0:T(1,128)}), f32[128,1,1,128]{3,2,1,0:T(1,128)S(1)}, u32[]{:S(2)}, u32[]{:S(2)}) async-start(f32[128,1,1,128]{3,2,1,0:T(1,128)} %reshape.45), calls=%async_computation.1 | async-start | bytes 131072 | tf_op jit(solution)/shard_map/all_to_all | solution.py:358
  72.0 1.9 %copy-start.1 = (f32[128,50,1,128]{3,2,1,0:T(1,128)S(1)}, f32[128,50,1,128]{3,2,1,0:T(1,128)}, u32[]{:S(2)}) copy-start(f32[128,50,1,128]{3,2,1,0:T(1,128)} %copy-done) | copy-start | bytes 9830404
  81.2 64.8 %copy-start.5 = (f32[144,1024]{1,0:T(8,128)S(1)}, f32[144,1024]{1,0:T(8,128)}, u32[]{:S(2)}) copy-start(f32[144,1024]{1,0:T(8,128)} %u_ref.1) | copy-start | bytes 1769476
  87.7 1.2 collective-permute-start
  88.9 7.0 %collective-permute-start.2 = (f32[32,128]{1,0:T(8,128)S(1)}, f32[32,128]{1,0:T(8,128)S(1)}, u32[]{:S(2)}, u32[]{:S(2)}) collective-permute-start(f32[32,128]{1,0:T(8,128)S(1)} %constant_dynamic-update-slice_fusion), channel_id=1, source_target_pairs={{2,0},{4,2},{6,4},{8,6},{10,8},{12,10},{14,12},{16,14},{18,16},{20... | collective-permute-start | bytes 49160 | tf_op jit(solution)/shard_map/ppermute | solution.py:366
  93.8 9.9 %collective-permute-start.1 = (f32[32,128]{1,0:T(8,128)S(1)}, f32[32,128]{1,0:T(8,128)S(1)}, u32[]{:S(2)}, u32[]{:S(2)}) collective-permute-start(f32[32,128]{1,0:T(8,128)S(1)} %constant_dynamic-update-slice_fusion), channel_id=1, source_target_pairs={{0,2},{2,4},{4,6},{6,8},{8,10},{10,12},{12,14},{14,16},{16,18},{18... | collective-permute-start | bytes 49160 | tf_op jit(solution)/shard_map/ppermute | solution.py:365
  118.1 1.2 collective-permute-start.3
  119.4 5.8 %collective-permute-start.5 = (f32[32,128]{1,0:T(8,128)S(1)}, f32[32,128]{1,0:T(8,128)S(1)}, u32[]{:S(2)}, u32[]{:S(2)}) collective-permute-start(f32[32,128]{1,0:T(8,128)S(1)} %constant_dynamic-update-slice_fusion.2), channel_id=1, source_target_pairs={{2,0},{4,2},{6,4},{8,6},{10,8},{12,10},{14,12},{16,14},{18,16},{20... | collective-permute-start | bytes 49160 | tf_op jit(solution)/shard_map/ppermute | solution.py:366
  123.3 9.9 %collective-permute-start.4 = (f32[32,128]{1,0:T(8,128)S(1)}, f32[32,128]{1,0:T(8,128)S(1)}, u32[]{:S(2)}, u32[]{:S(2)}) collective-permute-start(f32[32,128]{1,0:T(8,128)S(1)} %constant_dynamic-update-slice_fusion.2), channel_id=1, source_target_pairs={{0,2},{2,4},{4,6},{6,8},{8,10},{10,12},{12,14},{14,16},{16,18},{18... | collective-permute-start | bytes 49160 | tf_op jit(solution)/shard_map/ppermute | solution.py:365

commit v2 on v1

v2 whole, which is shorter than its diff:
```python
import functools

import jax
import jax.numpy as jnp
from jax import lax
from jax.experimental import pallas as pl
from jax.experimental.pallas import tpu as pltpu
from jax.sharding import Mesh
from jax.sharding import PartitionSpec as P

CY = 8
CZ = 128
K = 48
SLOTS = 16
PEERS = 128
ROWS = 1024
N_GX = 64
GX_GY = ("gx_0", "gx_1", "gx_2", "gy")
GX = ("gx_0", "gx_1", "gx_2")
F32 = jnp.float32
BF16 = jnp.bfloat16
HIGHEST = lax.Precision.HIGHEST
SIDE = K + 1
BANDS = 25
GRAM = 10
WIRE = 49 + GRAM
CHUNKS = 4
NT = (((1,), (1,)), ((), ()))
TN = (((0,), (0,)), ((), ()))
MAIN = 3 * 128


def split(x):
    high = x.astype(BF16)
    return high, (x - high.astype(F32)).astype(BF16)


def exact_dot(x, y, dims=(((1,), (0,)), ((), ()))):
    return lax.dot_general(x, y, dims, precision=HIGHEST, preferred_element_type=F32)


def half_sum(x):
    return x[:, :128] + x[:, 128:]


def folded(rows, start_ref):
    twice = rows + pltpu.roll(rows, SIDE, 1)
    sub = lax.broadcasted_iota(jnp.int32, (8, 128), 0)
    for tile in range(7):
        here = twice[tile * 8 : (tile + 1) * 8]
        total = jnp.zeros((8, 128), F32)
        for r in range(8):
            i = tile * 8 + r
            if i < SIDE:
                moved = pltpu.roll(here, (128 - i + BANDS * (i // GRAM)) % 128, 1)
                total = jnp.where(sub == r, moved, total)
        start_ref[tile * 8 : (tile + 1) * 8, :] = total
    lane = lax.broadcasted_iota(jnp.int32, (GRAM, 128), 1)
    return sum(
        jnp.where(lane // BANDS == g, start_ref[g * GRAM : (g + 1) * GRAM, :], 0.0) for g in range(5)
    )


def unfolded(bands, start_ref):
    sub = lax.broadcasted_iota(jnp.int32, (8, 128), 0)
    lane = lax.broadcasted_iota(jnp.int32, (GRAM, 128), 1)
    start_ref[48:56, :] = jnp.zeros((8, 128), F32)
    for g in range(5):
        start_ref[g * GRAM : (g + 1) * GRAM, :] = jnp.where(lane // BANDS == g, bands, 0.0)
    tiles = []
    for tile in range(7):
        here = start_ref[tile * 8 : (tile + 1) * 8, :]
        total = jnp.zeros((8, 128), F32)
        for r in range(8):
            i = tile * 8 + r
            if i < SIDE:
                moved = pltpu.roll(here, (128 + i - BANDS * (i // GRAM)) % 128, 1)
                total = jnp.where(sub == r, moved, total)
        tiles.append(total)
    half = jnp.concatenate(tiles + [jnp.zeros((72, 128), F32)], axis=0)
    row = lax.broadcasted_iota(jnp.int32, (128, 128), 0)
    lane = lax.broadcasted_iota(jnp.int32, (128, 128), 1)
    half = jnp.where(lane < SIDE, half + pltpu.roll(half, 128 - SIDE, 1), 0.0)
    return half + jnp.where(row == lane, 0.0, half.T)


def pack_kernel(
    op_hbm, c_hbm, b_hbm, rows_hbm, wire_hbm, info_ref,
    op_ref, c_ref, b_ref, rows_ref, p_ref, a_ref, fold_ref, wire_ref, in_sem, out_sem,
):
    copies = [
        pltpu.make_async_copy(source, target, in_sem.at[i])
        for i, (source, target) in enumerate(
            [(rows_hbm, rows_ref), (c_hbm, c_ref), (b_hbm, b_ref), (op_hbm, op_ref)]
        )
    ]
    for copy in copies:
        copy.start()
    copies[0].wait()
    new_rows = rows_ref[...]
    target = new_rows // ROWS
    local = new_rows % ROWS
    onehot = lax.broadcasted_iota(jnp.int32, (PEERS, ROWS), 0) == target
    onehot_f = jnp.where(onehot, 1.0, 0.0).astype(F32)
    onehot_b = onehot_f.astype(BF16)
    before = lax.broadcasted_iota(jnp.int32, (128, 128), 0) < lax.broadcasted_iota(jnp.int32, (128, 128), 1)
    before = jnp.where(before, 1.0, 0.0).astype(BF16)
    ones = jnp.ones((128, 128), BF16)
    seen = jnp.zeros((PEERS, 128), F32)
    ranks = []
    for block in range(ROWS // 128):
        part = onehot_b[:, block * 128 : (block + 1) * 128]
        count = jnp.dot(part, before, preferred_element_type=F32) + seen
        ranks.append(jnp.sum(onehot_f[:, block * 128 : (block + 1) * 128] * count, axis=0, keepdims=True))
        seen = seen + jnp.dot(part, ones, preferred_element_type=F32)
    rank = jnp.concatenate(ranks, axis=1)
    rank_at = jnp.where(onehot, rank, -1.0)
    info_ref[0:1, :] = target
    info_ref[1:2, :] = rank.astype(jnp.int32)
    info_ref[2:3, :] = local
    info_ref[3:8, :] = jnp.zeros((5, ROWS), jnp.int32)

    def put(tile, start, x):
        high, low = split(x)
        p_ref[tile * 256 + start : tile * 256 + start + x.shape[0], :] = high
        p_ref[tile * 256 + 128 + start : tile * 256 + 128 + start + x.shape[0], :] = low

    copies[1].wait()
    copies[2].wait()
    gram = jnp.zeros((64, 128), F32)
    a_ref[48:128, :] = jnp.zeros((80, ROWS), F32)
    for a in range(3):
        a_ref[0:48, :] = c_ref[a * K : (a + 1) * K, :]
        a_ref[48:49, :] = b_ref[a : a + 1, :]
        gram = gram + exact_dot(a_ref[0:64, :], a_ref[...], NT)
    bands = folded(gram, fold_ref)
    for i in range(GRAM):
        wire_ref[pl.ds(49 + i, PEERS, stride=WIRE), :] = jnp.broadcast_to(bands[i : i + 1, :], (PEERS, 128))
    put(0, 0, c_ref[0:128, :])
    put(1, 0, c_ref[128:144, :])
    copies[3].wait()
    put(1, 16, op_ref[0:112, :])
    put(2, 0, op_ref[112:240, :])

    at_rank = lax.broadcasted_iota(jnp.int32, (SLOTS, ROWS), 0).astype(F32) == rank
    rest = [op_ref[240 + i : 241 + i, :] for i in range(3)] + [b_ref[i : i + 1, :] for i in range(3)]
    rest = [jnp.where(at_rank, row, 0.0) for row in rest + [local.astype(F32)]]
    rest = jnp.concatenate(rest + [jnp.zeros((SLOTS, ROWS), F32)], axis=0)
    rest = jnp.concatenate(split(rest), axis=0)
    wire_ref[pl.ds(48, PEERS, stride=WIRE), :] = half_sum(
        lax.dot_general(onehot_b, rest, NT, preferred_element_type=F32)
    )
    sent = []
    count = PEERS // CHUNKS
    for chunk in range(CHUNKS):
        mine = rank_at[chunk * count : (chunk + 1) * count]
        choice = [jnp.where(mine == k, 1.0, 0.0).astype(BF16) for k in range(SLOTS)]
        moved = lax.dot_general(jnp.concatenate(choice, axis=0), p_ref[...], NT, preferred_element_type=F32)
        for tile in range(3):
            both = half_sum(moved[:, tile * 256 : (tile + 1) * 256])
            for k in range(SLOTS):
                wire_ref[pl.ds(chunk * count * WIRE + tile * SLOTS + k, count, stride=WIRE), :] = both[
                    k * count : (k + 1) * count
                ]
        rows = pl.ds(chunk * count * WIRE, count * WIRE)
        sent.append(pltpu.make_async_copy(wire_ref.at[rows], wire_hbm.at[rows], out_sem.at[chunk]))
        sent[-1].start()
    for copy in sent:
        copy.wait()


def two_level(groups, left_ref, right_ref):
    eight = lax.broadcasted_iota(jnp.int32, (CY, 128), 0)
    deep = lax.broadcasted_iota(jnp.int32, (128, 128), 0)
    count = groups[0][0].shape[0] // SLOTS
    for g, (values, labels) in enumerate(groups):
        labels = labels.astype(jnp.int32)
        y, z = labels // CZ, labels % CZ
        for k in range(SLOTS):
            cols = slice(k * 128, (k + 1) * 128)
            right_ref[g * 128 : (g + 1) * 128, cols] = jnp.where(deep == z[k : k + 1], 1.0, 0.0).astype(BF16)
            here = eight == y[k : k + 1]
            for c in range(count):
                row = (g * count + c) * CY
                value = values[c * SLOTS + k : c * SLOTS + k + 1]
                left_ref[row : row + CY, cols] = jnp.where(here, value, 0.0)
    rows = len(groups) * count * CY
    left = jnp.concatenate(split(left_ref[...]), axis=0)
    moved = lax.dot_general(left, right_ref[...], NT, preferred_element_type=F32)
    moved = moved[0:rows] + moved[rows:]
    size = count * CY
    return [moved[g * size : (g + 1) * size, g * 128 : (g + 1) * 128] for g in range(len(groups))]


def minus_combined(start, main_ref, weights):
    result = []
    for a in range(3):
        total = start[a]
        for m in range(K):
            row = (a * K + m) * CY
            total = total - main_ref[row : row + CY, :] * weights[m : m + 1, :]
        result.append(total)
    return result


def put_vector(vector, place_ref, v_ref, line_ref):
    lower = place_ref[0] == 0
    line_ref[...] = jnp.zeros((8, 128), F32)
    v_ref[24:32, :] = jnp.zeros((8, 128), F32)
    for a in range(3):
        v_ref[a * CY : (a + 1) * CY, :] = vector[a]
        line_ref[a : a + 1, :] = jnp.where(lower, vector[a][7:8, :], vector[a][0:1, :])


def swept(work, begin, count):
    row_id = lax.broadcasted_iota(jnp.int32, (K, 128), 0)
    columns = [jnp.broadcast_to(work[:, j : j + 1], (K, 128)) for j in range(begin, begin + count)]
    for s in range(count):
        j = begin + s
        column = columns[s]
        inverse = 1.0 / column[j : j + 1, :]
        here = row_id == j

        def step(x):
            pivot = x[j : j + 1, :] * inverse
            return jnp.where(here, pivot, x - column * pivot)

        work = step(work)
        columns = columns[: s + 1] + [step(c) for c in columns[s + 1 :]]
    return work


def unpack_kernel(
    place_ref, wire_ref, main_ref, ext_ref, v_ref, line_ref, inv_ref, start_ref, beta_ref,
    t_ref, r_ref, left_ref, right_ref, fold_ref,
):
    bands = [
        jnp.sum(wire_ref[pl.ds(49 + i, PEERS, stride=WIRE), :], axis=0, keepdims=True) for i in range(GRAM)
    ]
    gram = unfolded(jnp.concatenate(bands, axis=0), fold_ref)
    load_sq = jnp.broadcast_to(gram[48:49, 48:49], (1, 128))
    row_id = lax.broadcasted_iota(jnp.int32, (K, 128), 0)
    lane = lax.broadcasted_iota(jnp.int32, (K, 128), 1)
    raw = jnp.broadcast_to(gram[0:K, K : K + 1], (K, 128))
    work = jnp.where(lane < K + 1, gram[0:K], jnp.where(lane - 64 == row_id, 1.0, 0.0))

    rest = wire_ref[pl.ds(48, PEERS, stride=WIRE), :].T
    labels = rest[6 * SLOTS : 7 * SLOTS]
    node = lax.broadcasted_iota(jnp.int32, (ROWS, 128), 0).astype(F32)
    for k in range(SLOTS):
        t_ref[:, k * 128 : (k + 1) * 128] = jnp.where(node == labels[k : k + 1], 1.0, 0.0).astype(BF16)
    for tile in range(3):
        work = swept(work, tile * 16, 4)
        work = swept(work, tile * 16 + 4, 4)
        for k in range(SLOTS):
            high, low = split(wire_ref[pl.ds(tile * SLOTS + k, PEERS, stride=WIRE), :])
            r_ref[k * 128 : (k + 1) * 128, 0:128] = high
            r_ref[k * 128 : (k + 1) * 128, 128:256] = low
        work = swept(work, tile * 16 + 8, 4)
        moved = jnp.dot(t_ref[...], r_ref[...], preferred_element_type=F32)
        work = swept(work, tile * 16 + 12, 4)
        for y in range(CY):
            block = half_sum(moved[y * CZ : (y + 1) * CZ])
            main_ref[pl.ds(tile * 128 * CY + y, 128, stride=CY), :] = block.T
    [ext] = two_level([(rest[0 : 6 * SLOTS], labels)], left_ref, right_ref)
    ext_ref[...] = ext

    inverse = jnp.where(lane < K, pltpu.roll(work, 64, 1), 0.0)
    weights = jnp.broadcast_to(work[:, K : K + 1], (K, 128))
    inv_ref[...] = inverse
    start_ref[...] = weights
    beta = jnp.sqrt(load_sq - jnp.sum(raw * weights, axis=0, keepdims=True))
    beta_ref[...] = jnp.broadcast_to(beta, (8, 128))
    load = [ext[24 + a * CY : 24 + (a + 1) * CY, :] for a in range(3)]
    vector = minus_combined(load, main_ref, weights)
    put_vector([v / beta for v in vector], place_ref, v_ref, line_ref)


def put_plane(pad_ref, dx, plane, line, side):
    for a in range(3):
        base = (dx * 3 + a) * 24
        edge = line[a : a + 1, :]
        pad_ref[base + 7 : base + 8, :] = jnp.where(side == 1, edge, 0.0)
        pad_ref[base + 8 : base + 16, :] = plane[a * CY : (a + 1) * CY, :]
        pad_ref[base + 16 : base + 17, :] = jnp.where(side == 0, edge, 0.0)


def stencil(main_ref, ext_ref, pad_ref):
    lane = lax.broadcasted_iota(jnp.int32, (CY, 128), 1)
    total = [jnp.zeros((CY, 128), F32) for _ in range(3)]
    for dx in range(3):
        for dy in range(3):
            for b in range(3):
                start = (dx * 3 + b) * 24 + 7 + dy
                here = pad_ref[start : start + CY, :]
                left = jnp.where(lane == 0, 0.0, pltpu.roll(here, 1, 1))
                right = jnp.where(lane == 127, 0.0, pltpu.roll(here, 127, 1))
                for dz, moved in enumerate((left, here, right)):
                    for a in range(3):
                        q = ((dx * 9 + dy * 3 + dz) * 3 + a) * 3 + b
                        if q < 240:
                            row = (3 * K + q) * CY
                            total[a] = total[a] + main_ref[row : row + CY, :] * moved
                        else:
                            row = (q - 240) * CY
                            total[a] = total[a] + ext_ref[row : row + CY, :] * moved
    return total


def image_kernel(count, place_ref, main_ref, ext_ref, line_ref, first_ref, second_ref, *refs):
    vectors, (image_ref, send_ref, pad_ref, part_ref) = refs[:count], refs[count:]
    side = place_ref[0]
    even = place_ref[1] == 0
    first, second = first_ref[...], second_ref[...]
    up, down = jnp.where(even, second, first), jnp.where(even, first, second)
    put_plane(pad_ref, 0, up[0:24], up[24:32], side)
    put_plane(pad_ref, 1, vectors[-1][0:24, :], line_ref[...], side)
    put_plane(pad_ref, 2, down[0:24], down[24:32], side)
    image = stencil(main_ref, ext_ref, pad_ref)
    for a in range(3):
        image_ref[a * CY : (a + 1) * CY, :] = image[a]
    for m in range(K):
        rows = [(a * K + m) * CY for a in range(3)]
        part_ref[m * CY : (m + 1) * CY, :] = sum(
            main_ref[row : row + CY, :] * image[a] for a, row in enumerate(rows)
        )
    others = [image] + [[ref[a * CY : (a + 1) * CY, :] for a in range(3)] for ref in vectors]
    for i in range(8):
        m = K + i
        if i < len(others):
            part_ref[m * CY : (m + 1) * CY, :] = sum(o * w for o, w in zip(others[i], image))
        else:
            part_ref[m * CY : (m + 1) * CY, :] = jnp.zeros((CY, 128), F32)
    part = sum(part_ref[pl.ds(y, K + 8, stride=CY), :] for y in range(CY))
    part = jnp.concatenate([part, jnp.zeros((128 - K - 8, 128), F32)], axis=0)
    send_ref[...] = exact_dot(jnp.ones((PEERS, 128), F32), part, NT)


def totals(got_ref):
    return exact_dot(got_ref[...], jnp.ones((PEERS, 128), F32), TN)


def next_kernel(place_ref, got_ref, main_ref, image_ref, one_ref, inv_ref, v_ref, line_ref, weights_ref, h_ref):
    sums = totals(got_ref)
    weights = exact_dot(inv_ref[...], sums)
    h11 = sums[K + 1 : K + 2, :]
    along = jnp.sum(sums[0:K] * weights, axis=0, keepdims=True)
    h21 = jnp.sqrt(sums[K : K + 1, :] - along - h11 * h11)
    begin = [
        image_ref[a * CY : (a + 1) * CY, :] - h11 * one_ref[a * CY : (a + 1) * CY, :] for a in range(3)
    ]
    vector = minus_combined(begin, main_ref, weights)
    put_vector([v / h21 for v in vector], place_ref, v_ref, line_ref)
    weights_ref[...] = weights
    h_ref[...] = jnp.zeros((8, 128), F32)
    h_ref[0:1, :] = h11
    h_ref[1:2, :] = h21


def send_kernel(got_ref, inv_ref, start_ref, first_ref, h_ref, beta_ref, u_ref, info_ref, wire_ref, y_ref):
    sums = totals(got_ref)
    weights = exact_dot(inv_ref[...], sums)
    h11, h21 = h_ref[0:1, :], h_ref[1:2, :]
    h12, h22 = sums[K + 1 : K + 2, :], sums[K + 2 : K + 3, :]
    along = jnp.sum(sums[0:K] * weights, axis=0, keepdims=True)
    h32 = jnp.sqrt(sums[K : K + 1, :] - along - h12 * h12 - h22 * h22)
    beta = beta_ref[0:1, :]
    m11 = h11 * h11 + h21 * h21
    m12 = h11 * h12 + h21 * h22
    m22 = h12 * h12 + h22 * h22 + h32 * h32
    g_one = beta * h11
    g_two = beta * h12
    determ = m11 * m22 - m12 * m12
    y_one = (m22 * g_one - m12 * g_two) / determ
    y_two = (m11 * g_two - m12 * g_one) / determ
    y_ref[...] = jnp.zeros((8, 128), F32)
    y_ref[0:1, :] = y_one
    y_ref[1:2, :] = y_two
    weights = start_ref[...] - y_one * first_ref[...] - y_two * weights
    wide = jnp.concatenate([weights] * (ROWS // 128), axis=1)
    target, rank, local = (info_ref[i : i + 1, :] for i in range(3))
    at_rank = lax.broadcasted_iota(jnp.int32, (SLOTS, ROWS), 0) == rank
    rows = [jnp.sum(u_ref[a * K : (a + 1) * K, :] * wide, axis=0, keepdims=True) for a in range(3)]
    rows = jnp.concatenate([jnp.where(at_rank, r, 0.0) for r in rows + [local.astype(F32)]], axis=0)
    rows = jnp.concatenate(split(rows), axis=0)
    onehot = lax.broadcasted_iota(jnp.int32, (PEERS, ROWS), 0) == target
    onehot = jnp.where(onehot, 1.0, 0.0).astype(BF16)
    mine = lax.dot_general(onehot, rows, NT, preferred_element_type=F32)
    mine = mine + pltpu.roll(mine, 64, 1)
    peer = lax.broadcasted_iota(jnp.int32, (PEERS, 128), 0)
    lane = lax.broadcasted_iota(jnp.int32, (PEERS, 128), 1)
    other = jnp.where(peer % 2 == 0, pltpu.roll(mine, PEERS - 1, 0), pltpu.roll(mine, 1, 0))
    pair = jnp.where(lane < 64, mine, other)
    wire_ref[pl.ds(0, PEERS, stride=3), :] = jnp.where(peer < 2, 0.0, pltpu.roll(pair, 2, 0))
    wire_ref[pl.ds(1, PEERS, stride=3), :] = pair
    wire_ref[pl.ds(2, PEERS, stride=3), :] = jnp.where(peer >= PEERS - 2, 0.0, pltpu.roll(pair, PEERS - 2, 0))


def last_kernel(
    place_ref, got_ref, main_ref, ext_ref, y_ref, one_ref, two_ref, im_one_ref, im_two_ref,
    sol_ref, res_ref, left_ref, right_ref, pad_ref,
):
    side = place_ref[0]
    for dx in range(3):
        got = got_ref[pl.ds(dx, PEERS, stride=3), :].T
        own, other = two_level(
            [(got[base : base + 48], got[base + 48 : base + 64]) for base in (0, 64)], left_ref, right_ref
        )
        lines = [
            jnp.where(side == 0, other[a * CY : a * CY + 1, :], other[a * CY + 7 : a * CY + 8, :]) for a in range(3)
        ]
        put_plane(pad_ref, dx, own, jnp.concatenate(lines, axis=0), side)
        if dx == 1:
            term = own
    image = stencil(main_ref, ext_ref, pad_ref)
    y_one, y_two = y_ref[0:1, :], y_ref[1:2, :]
    solution = term + y_one * one_ref[0:24, :] + y_two * two_ref[0:24, :]
    for a in range(3):
        rows = slice(a * CY, (a + 1) * CY)
        residual = ext_ref[24 + a * CY : 24 + (a + 1) * CY, :] - image[a]
        residual = residual - y_one * im_one_ref[rows, :] - y_two * im_two_ref[rows, :]
        for y in range(CY):
            cols = slice(y * CZ, (y + 1) * CZ)
            sol_ref[a : a + 1, cols] = solution[a * CY + y : a * CY + y + 1, :]
            res_ref[a : a + 1, cols] = residual[y : y + 1, :]


def shape(*dims, dtype=F32):
    return jax.ShapeDtypeStruct(dims, dtype)


def specs(*spaces):
    return tuple(pl.BlockSpec(memory_space=space) for space in spaces)


def call(kernel, outs, scratch=(), scalars=0, inputs=0, in_specs=None, out_specs=None, limit=40):
    vmem = pltpu.VMEM
    return pl.pallas_call(
        kernel,
        out_shape=outs,
        in_specs=in_specs or specs(*[pltpu.SMEM] * scalars, *[vmem] * (inputs - scalars)),
        out_specs=out_specs or specs(*[vmem] * len(outs)),
        scratch_shapes=list(scratch),
        compiler_params=pltpu.CompilerParams(vmem_limit_bytes=limit * 2**20),
    )


def exchange(rows):
    count = rows.shape[0] // PEERS
    shaped = rows.reshape(PEERS, count, 1, 128)
    got = lax.all_to_all(shaped, GX_GY, split_axis=0, concat_axis=0, tiled=True)
    return got.reshape(PEERS * count, 128)


def swap(plane, first):
    pairs = [(i, i + 1) for i in range(first, N_GX - 1, 2)]
    return lax.ppermute(plane, GX, pairs + [(j, i) for i, j in pairs])


def halo(vector, line):
    other = lax.ppermute(line, "gy", [(0, 1), (1, 0)])
    plane = lax.dynamic_update_slice(vector, other, (24, 0))
    return other, swap(plane, 0), swap(plane, 1)


def body(operator, basis_u, basis_c, right_side, new_rows):
    place = jnp.stack([lax.axis_index("gy"), lax.axis_index(GX) % 2]).astype(jnp.int32)
    vmem, hbm = pltpu.VMEM, pltpu.HBM
    wire, info = call(
        pack_kernel,
        (shape(PEERS * WIRE, 128), shape(8, ROWS, dtype=jnp.int32)),
        [
            vmem((243, ROWS), F32),
            vmem((144, ROWS), F32),
            vmem((3, ROWS), F32),
            vmem((1, ROWS), jnp.int32),
            vmem((2 * MAIN, ROWS), BF16),
            vmem((128, ROWS), F32),
            vmem((56, 128), F32),
            vmem((PEERS * WIRE, 128), F32),
            pltpu.SemaphoreType.DMA((4,)),
            pltpu.SemaphoreType.DMA((CHUNKS,)),
        ],
        in_specs=specs(hbm, hbm, hbm, hbm),
        out_specs=specs(hbm, vmem),
    )(operator, basis_c, right_side, new_rows.reshape(1, ROWS))
    got = exchange(wire)
    vector_outs = (shape(32, 128), shape(8, 128))
    main, ext, one, line, inverse, start, beta = call(
        unpack_kernel,
        (shape(MAIN * CY, 128), shape(48, 128), *vector_outs, shape(K, 128), shape(K, 128), shape(8, 128)),
        [
            vmem((ROWS, SLOTS * PEERS), BF16),
            vmem((SLOTS * PEERS, 256), BF16),
            vmem((48, SLOTS * PEERS), F32),
            vmem((128, SLOTS * PEERS), BF16),
            vmem((56, 128), F32),
        ],
        scalars=1,
        inputs=2,
    )(place, got)
    pad = vmem((9 * 24, 128), F32)
    image_scratch = [pad, vmem(((K + 8) * CY, 128), F32)]
    image_outs = (shape(3 * CY, 128), shape(PEERS, 128))
    image_one, send = call(functools.partial(image_kernel, 1), image_outs, image_scratch, scalars=1, inputs=7)(
        place, main, ext, *halo(one, line), one
    )
    sums = exchange(send)
    two, line, weights, h_one = call(
        next_kernel, (*vector_outs, shape(K, 128), shape(8, 128)), scalars=1, inputs=6
    )(place, sums, main, image_one, one, inverse)
    image_two, send = call(functools.partial(image_kernel, 2), image_outs, image_scratch, scalars=1, inputs=8)(
        place, main, ext, *halo(two, line), one, two
    )
    sums = exchange(send)
    wire, y = call(send_kernel, (shape(PEERS * 3, 128), shape(8, 128)), inputs=8)(
        sums, inverse, start, weights, h_one, beta, basis_u, info
    )
    got = exchange(wire)
    return call(
        last_kernel,
        (shape(3, ROWS), shape(3, ROWS)),
        [vmem((48, SLOTS * PEERS), F32), vmem((256, SLOTS * PEERS), BF16), pad],
        scalars=1,
        inputs=9,
    )(place, got, main, ext, y, one, two, image_one, image_two)


def solution(mesh):
    torus = Mesh(mesh.devices.reshape(4, 4, 4, mesh.shape["gy"]), ("gx_0", "gx_1", "gx_2", "gy"))
    placed = (P(None, GX_GY), P(None, GX_GY), P(None, GX_GY), P(None, GX_GY), P(GX_GY))
    return jax.shard_map(
        body,
        mesh=torus,
        in_specs=placed,
        out_specs=(P(None, GX_GY), P(None, GX_GY)),
        check_vma=False,
    )
```

time: 167 us -> 158 us (0.946)
  starting transfers between devices: 28.3 us -> 19.2 us
  local copies, waits for them, and re-layouts: 9.59 us -> 5.55 us
  Pallas kernels: 22.1 us -> 24.8 us
  blocking collectives: 40.5 us -> 42.6 us
    pallas_call x1, Pallas kernels: 5.37 us -> 10.9 us  [body(): call(pack_kernel, (shape(PEERS * WIRE, 128), shape(8, ROWS, dtype=jnp.int...]
    ppermute x4, starting transfers between devices: 12.8 us -> 8.05 us  [swap(): return lax.ppermute(plane, GX, pairs + [(j, i) for i, j in pairs])]
    all_to_all x2 -> x1, starting transfers between devices: 15.4 us -> 10.9 us  [exchange(): got = lax.all_to_all(shaped, GX_GY, split_axis=0, concat_axis=0, tiled=True)]
    pallas_call x3 -> x2, Pallas kernels: 14.1 us -> 10 us  [the longest x1 6.82 us: body(): call(unpack_kernel, (shape(MAIN * CY, 128), shape(48, 128), *vector_outs,...]
    ppermute x4, waiting for transfers between devices: 15.6 us -> 11.6 us  [swap(): return lax.ppermute(plane, GX, pairs + [(j, i) for i, j in pairs])]
    all_to_all x2 -> x1, waiting for transfers between devices: 45.7 us -> 48.8 us  [exchange(): got = lax.all_to_all(shaped, GX_GY, split_axis=0, concat_axis=0, tiled=True)]
    unnamed x18 -> x14, local copies, waits for them, and re-layouts: 8.5 us -> 5.54 us
    all_to_all x3, blocking collectives: 40.5 us -> 42.6 us  [exchange(): got = lax.all_to_all(shaped, GX_GY, split_axis=0, concat_axis=0, tiled=True)]
  transfers between devices with their start and end apart: 8 -> 7, of which waited for: 6 -> 5; matrix products, arithmetic and copies ran while one was open for 0% -> 0% of each run, Pallas kernels for 3% -> 0%
where the time goes in v2:
time: 158 us; the launch traced here: 156 us
  waiting for transfers between devices  62.7 us (40%)
  blocking collectives  42.6 us (27%)
  Pallas kernels  24.8 us (16%)
  starting transfers between devices  19.2 us (12%)
  local copies, waits for them, and re-layouts  5.55 us (4%)
    all_to_all x1, waiting for transfers between devices, exchange(): got = lax.all_to_all(shaped, GX_GY, split_axis=0, concat_axis=0, tiled=True)  48.8 us
    all_to_all x3, blocking collectives, exchange(): got = lax.all_to_all(shaped, GX_GY, split_axis=0, concat_axis=0, tiled=True)  42.6 us
    ppermute x4, waiting for transfers between devices, swap(): return lax.ppermute(plane, GX, pairs + [(j, i) for i, j in pairs])  11.6 us
    all_to_all x1, starting transfers between devices, exchange(): got = lax.all_to_all(shaped, GX_GY, split_axis=0, concat_axis=0, tiled=True)  10.9 us
    pallas_call x1, Pallas kernels, body(): call(pack_kernel, (shape(PEERS * WIRE, 128), shape(8, ROWS, dtype=jnp.int...  10.9 us
    ppermute x4, starting transfers between devices, swap(): return lax.ppermute(plane, GX, pairs + [(j, i) for i, j in pairs])  8.05 us
    pallas_call x1, Pallas kernels, body(): call(unpack_kernel, (shape(MAIN * CY, 128), shape(48, 128), *vector_outs,...  6.82 us
    unnamed x14, local copies, waits for them, and re-layouts  5.54 us
  transfers between devices with their start and end apart: 7, of which 5 were waited for; matrix products, arithmetic and copies ran while one was open for 0% of the time, Pallas kernels for 0%

profile of v2, /device:TPU:2, one launch (start us, length us, event | category | flops | bytes accessed | tf_op | source)
XLA Modules:
  0.0 155.7 jit_solution(21675804684870396)
XLA Ops:
  0.6 1.2 copy-done.1
  1.8 1.1 copy-done.2
  2.9 0.7 copy-done.4
  3.6 0.7 copy-done.5
  4.3 10.9 %shard_map.68 = (f32[7552,128]{1,0:T(8,128)S(1)}, s32[8,1024]{1,0:T(8,128)S(1)}) custom-call(f32[243,1024]{1,0:T(8,128)S(1)} %copy-done.1, f32[144,1024]{1,0:T(8,128)S(1)} %copy-done.2, f32[3,1024]{1,0:T(4,128)S(1)} %copy-done.4, s32[1,1024]{1,0:T(1,128)S(1)} %bitcast.22), custom_call_target="tpu_custom_call" | custom-call | tf_op jit(solution)/shard_map/pallas_call | solution.py:469
  15.2 1.9 %copy-done = f32[7552,128]{1,0:T(8,128)} copy-done((f32[7552,128]{1,0:T(8,128)}, f32[7552,128]{1,0:T(8,128)S(1)}, u32[]{:S(2)}) %copy-start) | copy-done | bytes 3866648
  17.1 10.9 %all-to-all-start = ((f32[128,59,1,128]{3,2,1,0:T(1,128)}), f32[128,59,1,128]{3,2,1,0:T(1,128)}, u32[]{:S(2)}, u32[]{:S(2)}) async-start(f32[128,59,1,128]{3,2,1,0:T(1,128)} %bitcast.15), calls=%async_computation | async-start | bytes 7733248 | tf_op jit(solution)/shard_map/all_to_all | solution.py:451
  28.1 48.8 %all-to-all-done = f32[128,59,1,128]{3,2,1,0:T(1,128)} async-done(((f32[128,59,1,128]{3,2,1,0:T(1,128)}), f32[128,59,1,128]{3,2,1,0:T(1,128)}, u32[]{:S(2)}, u32[]{:S(2)}) %all-to-all-start) | async-done | bytes 3866656 | tf_op jit(solution)/shard_map/all_to_all | solution.py:451
  76.9 6.8 %shard_map.69 = (f32[3072,128]{1,0:T(8,128)S(1)}, f32[48,128]{1,0:T(8,128)S(1)}, f32[32,128]{1,0:T(8,128)S(1)}, f32[8,128]{1,0:T(8,128)S(1)}, f32[48,128]{1,0:T(...) custom-call(s32[2]{0:T(128)S(1)} %pad_add_fusion.place_ref, f32[7552,128]{1,0:T(8,128)} %bitcast.4.wire_ref), custom_call_target="tpu_custom_call" | custom-call | tf_op jit(solution)/shard_map/pallas_call | solution.py:489
  83.8 1.1 collective-permute-done.line_ref
  85.0 4.0 %collective-permute-start.2 = (f32[32,128]{1,0:T(8,128)S(1)}, f32[32,128]{1,0:T(8,128)S(1)}, u32[]{:S(2)}, u32[]{:S(2)}) collective-permute-start(f32[32,128]{1,0:T(8,128)S(1)} %constant_dynamic-update-slice_fusion.1), channel_id=1, source_target_pairs={{2,4},{6,8},{10,12},{14,16},{18,20},{22,24},{26,28},{30,32},{34,36... | collective-permute-start | bytes 49160 | tf_op jit(solution)/shard_map/ppermute | solution.py:457
  89.0 0.1 collective-permute-start.1
  89.1 5.7 %collective-permute-done.2.second_ref = f32[32,128]{1,0:T(8,128)S(1)} collective-permute-done((f32[32,128]{1,0:T(8,128)S(1)}, f32[32,128]{1,0:T(8,128)S(1)}, u32[]{:S(2)}, u32[]{:S(2)}) %collective-permute-start.2) | collective-permute-done | bytes 16416 | tf_op jit(solution)/shard_map/ppermute | solution.py:457
  94.8 1.0 shard_map.70
  95.8 14.0 %all_to_all.20 = f32[128,1,1,128]{3,2,1,0:T(1,128)S(1)} all-to-all(f32[128,1,1,128]{3,2,1,0:T(1,128)S(1)} %bitcast.20), channel_id=1, replica_groups=mesh['gx_0'=4,'gx_1'=4,'gx_2'=4,'gy'=2] {'gx_0','gx_1','gx_2','gy'}, dimensions={0} | all-to-all | bytes 131072 | tf_op jit(solution)/shard_map/all_to_all | solution.py:451
  109.8 1.1 shard_map.71
  111.0 1.1 collective-permute-done.3.line_ref
  112.1 3.9 %collective-permute-start.5 = (f32[32,128]{1,0:T(8,128)S(1)}, f32[32,128]{1,0:T(8,128)S(1)}, u32[]{:S(2)}, u32[]{:S(2)}) collective-permute-start(f32[32,128]{1,0:T(8,128)S(1)} %constant_dynamic-update-slice_fusion), channel_id=1, source_target_pairs={{2,4},{6,8},{10,12},{14,16},{18,20},{22,24},{26,28},{30,32},{34,36... | collective-permute-start | bytes 49160 | tf_op jit(solution)/shard_map/ppermute | solution.py:457
  116.1 5.9 %collective-permute-done.5.second_ref = f32[32,128]{1,0:T(8,128)S(1)} collective-permute-done((f32[32,128]{1,0:T(8,128)S(1)}, f32[32,128]{1,0:T(8,128)S(1)}, u32[]{:S(2)}, u32[]{:S(2)}) %collective-permute-start.5) | collective-permute-done | bytes 16416 | tf_op jit(solution)/shard_map/ppermute | solution.py:457
  121.9 1.0 shard_map.72
  122.9 14.0 %all_to_all.21 = f32[128,1,1,128]{3,2,1,0:T(1,128)S(1)} all-to-all(f32[128,1,1,128]{3,2,1,0:T(1,128)S(1)} %bitcast.21), channel_id=1, replica_groups=mesh['gx_0'=4,'gx_1'=4,'gx_2'=4,'gy'=2] {'gx_0','gx_1','gx_2','gy'}, dimensions={0} | all-to-all | bytes 131072 | tf_op jit(solution)/shard_map/all_to_all | solution.py:451
  136.9 0.9 shard_map.73
  137.8 14.7 %all_to_all.22 = f32[128,3,1,128]{3,2,1,0:T(1,128)S(1)} all-to-all(f32[128,3,1,128]{3,2,1,0:T(1,128)S(1)} %bitcast.19), channel_id=1, replica_groups=mesh['gx_0'=4,'gx_1'=4,'gx_2'=4,'gy'=2] {'gx_0','gx_1','gx_2','gy'}, dimensions={0} | all-to-all | bytes 393216 | tf_op jit(solution)/shard_map/all_to_all | solution.py:451
  152.4 3.2 %shard_map.74 = (f32[3,1024]{1,0:T(4,128)}, f32[3,1024]{1,0:T(4,128)}) custom-call(s32[2]{0:T(128)S(1)} %pad_add_fusion.place_ref, f32[384,128]{1,0:T(8,128)S(1)} %bitcast.16, f32[3072,128]{1,0:T(8,128)S(1)} %get-tuple-element.22.main_ref, f32[48,128]{1,0:T(8,128)S(1)} %get-tuple-element.23.ext_ref, f32[8,128]{1,0:T(8,128)S(1)} %get-tuple-element.38.y_ref, ...), custom_call_target="tpu_custom_call" | custom-call | tf_op jit(solution)/shard_map/pallas_call | solution.py:520
  (17 shorter events, 0.4 us)
Async XLA Ops:
  0.6 1.2 copy-start.1
  1.8 1.1 copy-start.2
  2.9 0.7 copy-start.4
  3.6 0.7 copy-start.5
  15.2 1.9 %copy-start = (f32[7552,128]{1,0:T(8,128)}, f32[7552,128]{1,0:T(8,128)S(1)}, u32[]{:S(2)}) copy-start(f32[7552,128]{1,0:T(8,128)S(1)} %get-tuple-element.21) | copy-start | bytes 11599876
  17.1 59.8 %all-to-all-start = ((f32[128,59,1,128]{3,2,1,0:T(1,128)}), f32[128,59,1,128]{3,2,1,0:T(1,128)}, u32[]{:S(2)}, u32[]{:S(2)}) async-start(f32[128,59,1,128]{3,2,1,0:T(1,128)} %bitcast.15), calls=%async_computation | async-start | bytes 7733248 | tf_op jit(solution)/shard_map/all_to_all | solution.py:451
  76.9 60.0 %copy-start.3 = (f32[144,1024]{1,0:T(8,128)S(1)}, f32[144,1024]{1,0:T(8,128)}, u32[]{:S(2)}) copy-start(f32[144,1024]{1,0:T(8,128)} %u_ref.1) | copy-start | bytes 1769476
  83.7 1.2 collective-permute-start
  85.0 9.8 %collective-permute-start.2 = (f32[32,128]{1,0:T(8,128)S(1)}, f32[32,128]{1,0:T(8,128)S(1)}, u32[]{:S(2)}, u32[]{:S(2)}) collective-permute-start(f32[32,128]{1,0:T(8,128)S(1)} %constant_dynamic-update-slice_fusion.1), channel_id=1, source_target_pairs={{2,4},{6,8},{10,12},{14,16},{18,20},{22,24},{26,28},{30,32},{34,36... | collective-permute-start | bytes 49160 | tf_op jit(solution)/shard_map/ppermute | solution.py:457
  89.0 5.8 %collective-permute-start.1 = (f32[32,128]{1,0:T(8,128)S(1)}, f32[32,128]{1,0:T(8,128)S(1)}, u32[]{:S(2)}, u32[]{:S(2)}) collective-permute-start(f32[32,128]{1,0:T(8,128)S(1)} %constant_dynamic-update-slice_fusion.1), channel_id=1, source_target_pairs={{0,2},{4,6},{8,10},{12,14},{16,18},{20,22},{24,26},{28,30},{32,34}... | collective-permute-start | bytes 49160 | tf_op jit(solution)/shard_map/ppermute | solution.py:457
  110.8 1.2 collective-permute-start.3
  112.1 9.8 %collective-permute-start.5 = (f32[32,128]{1,0:T(8,128)S(1)}, f32[32,128]{1,0:T(8,128)S(1)}, u32[]{:S(2)}, u32[]{:S(2)}) collective-permute-start(f32[32,128]{1,0:T(8,128)S(1)} %constant_dynamic-update-slice_fusion), channel_id=1, source_target_pairs={{2,4},{6,8},{10,12},{14,16},{18,20},{22,24},{26,28},{30,32},{34,36... | collective-permute-start | bytes 49160 | tf_op jit(solution)/shard_map/ppermute | solution.py:457
  116.0 6.0 %collective-permute-start.4 = (f32[32,128]{1,0:T(8,128)S(1)}, f32[32,128]{1,0:T(8,128)S(1)}, u32[]{:S(2)}, u32[]{:S(2)}) collective-permute-start(f32[32,128]{1,0:T(8,128)S(1)} %constant_dynamic-update-slice_fusion), channel_id=1, source_target_pairs={{0,2},{4,6},{8,10},{12,14},{16,18},{20,22},{24,26},{28,30},{32,34}... | collective-permute-start | bytes 49160 | tf_op jit(solution)/shard_map/ppermute | solution.py:457

commit v3 on v2

--- a/solution.py
+++ b/solution.py
@@ -24,7 +24,7 @@
 BANDS = 25
 GRAM = 10
 WIRE = 49 + GRAM
-CHUNKS = 4
+CHUNKS = 8
 NT = (((1,), (1,)), ((), ()))
 TN = (((0,), (0,)), ((), ()))
 MAIN = 3 * 128
@@ -119,14 +119,11 @@
     info_ref[1:2, :] = rank.astype(jnp.int32)
     info_ref[2:3, :] = local
     info_ref[3:8, :] = jnp.zeros((5, ROWS), jnp.int32)
-
-    def put(tile, start, x):
-        high, low = split(x)
-        p_ref[tile * 256 + start : tile * 256 + start + x.shape[0], :] = high
-        p_ref[tile * 256 + 128 + start : tile * 256 + 128 + start + x.shape[0], :] = low
-
-    copies[1].wait()
-    copies[2].wait()
+    for copy in copies[1:]:
+        copy.wait()
+    middle = jnp.concatenate([c_ref[128:144, :], op_ref[0:112, :]], axis=0)
+    for tile, x in enumerate((c_ref[0:128, :], middle, op_ref[112:240, :])):
+        p_ref[:, tile * 256 : tile * 256 + 128], p_ref[:, tile * 256 + 128 : (tile + 1) * 256] = split(x.T)
     gram = jnp.zeros((64, 128), F32)
     a_ref[48:128, :] = jnp.zeros((80, ROWS), F32)
     for a in range(3):
@@ -136,11 +133,6 @@
     bands = folded(gram, fold_ref)
     for i in range(GRAM):
         wire_ref[pl.ds(49 + i, PEERS, stride=WIRE), :] = jnp.broadcast_to(bands[i : i + 1, :], (PEERS, 128))
-    put(0, 0, c_ref[0:128, :])
-    put(1, 0, c_ref[128:144, :])
-    copies[3].wait()
-    put(1, 16, op_ref[0:112, :])
-    put(2, 0, op_ref[112:240, :])
 
     at_rank = lax.broadcasted_iota(jnp.int32, (SLOTS, ROWS), 0).astype(F32) == rank
     rest = [op_ref[240 + i : 241 + i, :] for i in range(3)] + [b_ref[i : i + 1, :] for i in range(3)]
@@ -155,7 +147,7 @@
     for chunk in range(CHUNKS):
         mine = rank_at[chunk * count : (chunk + 1) * count]
         choice = [jnp.where(mine == k, 1.0, 0.0).astype(BF16) for k in range(SLOTS)]
-        moved = lax.dot_general(jnp.concatenate(choice, axis=0), p_ref[...], NT, preferred_element_type=F32)
+        moved = jnp.dot(jnp.concatenate(choice, axis=0), p_ref[...], preferred_element_type=F32)
         for tile in range(3):
             both = half_sum(moved[:, tile * 256 : (tile + 1) * 256])
             for k in range(SLOTS):
@@ -204,7 +196,7 @@
 
 
 def put_vector(vector, place_ref, v_ref, line_ref):
-    lower = place_ref[0] == 0
+    lower = place_ref[0:1, :] == 0
     line_ref[...] = jnp.zeros((8, 128), F32)
     v_ref[24:32, :] = jnp.zeros((8, 128), F32)
     for a in range(3):
@@ -231,37 +223,50 @@
 
 
 def unpack_kernel(
-    place_ref, wire_ref, main_ref, ext_ref, v_ref, line_ref, inv_ref, start_ref, beta_ref,
-    t_ref, r_ref, left_ref, right_ref, fold_ref,
+    place_ref, wire_hbm, main_ref, ext_ref, v_ref, line_ref, inv_ref, start_ref, beta_ref,
+    wire_ref, t_ref, r_ref, part_ref, left_ref, right_ref, fold_ref, in_sem,
 ):
-    bands = [
-        jnp.sum(wire_ref[pl.ds(49 + i, PEERS, stride=WIRE), :], axis=0, keepdims=True) for i in range(GRAM)
-    ]
-    gram = unfolded(jnp.concatenate(bands, axis=0), fold_ref)
-    load_sq = jnp.broadcast_to(gram[48:49, 48:49], (1, 128))
-    row_id = lax.broadcasted_iota(jnp.int32, (K, 128), 0)
-    lane = lax.broadcasted_iota(jnp.int32, (K, 128), 1)
-    raw = jnp.broadcast_to(gram[0:K, K : K + 1], (K, 128))
-    work = jnp.where(lane < K + 1, gram[0:K], jnp.where(lane - 64 == row_id, 1.0, 0.0))
-
+    half = PEERS // 2
+    copies = []
+    for part in range(2):
+        rows = pl.ds(part * half * WIRE, half * WIRE)
+        copies.append(pltpu.make_async_copy(wire_hbm.at[rows], wire_ref.at[rows], in_sem.at[part]))
+        copies[-1].start()
+    node = lax.broadcasted_iota(jnp.int32, (ROWS, 128), 0).astype(F32)
+    for part in range(2):
+        copies[part].wait()
+        if part == 1:
+            bands = [
+                jnp.sum(wire_ref[pl.ds(49 + i, PEERS, stride=WIRE), :], axis=0, keepdims=True) for i in range(GRAM)
+            ]
+            gram = unfolded(jnp.concatenate(bands, axis=0), fold_ref)
+            load_sq = jnp.broadcast_to(gram[48:49, 48:49], (1, 128))
+            row_id = lax.broadcasted_iota(jnp.int32, (K, 128), 0)
+            lane = lax.broadcasted_iota(jnp.int32, (K, 128), 1)
+            raw = jnp.broadcast_to(gram[0:K, K : K + 1], (K, 128))
+            work = jnp.where(lane < K + 1, gram[0:K], jnp.where(lane - 64 == row_id, 1.0, 0.0))
+            for begin in range(0, K, 4):
+                work = swept(work, begin, 4)
+        first = part * half * WIRE
+        labels = wire_ref[pl.ds(first + 48, half, stride=WIRE), :].T[6 * SLOTS : 7 * SLOTS]
+        labels = jnp.concatenate([labels[0:8], labels[8:16]], axis=1)
+        for i in range(8):
+            t_ref[part, :, i * 128 : (i + 1) * 128] = jnp.where(node == labels[i : i + 1], 1.0, 0.0).astype(BF16)
+        for tile in range(3):
+            for k in range(SLOTS):
+                high, low = split(wire_ref[pl.ds(first + tile * SLOTS + k, half, stride=WIRE), :])
+                row = k % 8 * 128 + k // 8 * half
+                r_ref[part, tile, row : row + half, 0:128] = high
+                r_ref[part, tile, row : row + half, 128:256] = low
+            moved = half_sum(jnp.dot(t_ref[part], r_ref[part, tile], preferred_element_type=F32))
+            if part == 0:
+                part_ref[tile] = moved
+                continue
+            moved = moved + part_ref[tile]
+            for y in range(CY):
+                main_ref[pl.ds(tile * 128 * CY + y, 128, stride=CY), :] = moved[y * CZ : (y + 1) * CZ].T
     rest = wire_ref[pl.ds(48, PEERS, stride=WIRE), :].T
     labels = rest[6 * SLOTS : 7 * SLOTS]
-    node = lax.broadcasted_iota(jnp.int32, (ROWS, 128), 0).astype(F32)
-    for k in range(SLOTS):
-        t_ref[:, k * 128 : (k + 1) * 128] = jnp.where(node == labels[k : k + 1], 1.0, 0.0).astype(BF16)
-    for tile in range(3):
-        work = swept(work, tile * 16, 4)
-        work = swept(work, tile * 16 + 4, 4)
-        for k in range(SLOTS):
-            high, low = split(wire_ref[pl.ds(tile * SLOTS + k, PEERS, stride=WIRE), :])
-            r_ref[k * 128 : (k + 1) * 128, 0:128] = high
-            r_ref[k * 128 : (k + 1) * 128, 128:256] = low
-        work = swept(work, tile * 16 + 8, 4)
-        moved = jnp.dot(t_ref[...], r_ref[...], preferred_element_type=F32)
-        work = swept(work, tile * 16 + 12, 4)
-        for y in range(CY):
-            block = half_sum(moved[y * CZ : (y + 1) * CZ])
-            main_ref[pl.ds(tile * 128 * CY + y, 128, stride=CY), :] = block.T
     [ext] = two_level([(rest[0 : 6 * SLOTS], labels)], left_ref, right_ref)
     ext_ref[...] = ext
 
@@ -309,8 +314,8 @@
 
 def image_kernel(count, place_ref, main_ref, ext_ref, line_ref, first_ref, second_ref, *refs):
     vectors, (image_ref, send_ref, pad_ref, part_ref) = refs[:count], refs[count:]
-    side = place_ref[0]
-    even = place_ref[1] == 0
+    side = place_ref[0:1, :]
+    even = place_ref[1:2, :] == 0
     first, second = first_ref[...], second_ref[...]
     up, down = jnp.where(even, second, first), jnp.where(even, first, second)
     put_plane(pad_ref, 0, up[0:24], up[24:32], side)
@@ -400,11 +405,13 @@
     place_ref, got_ref, main_ref, ext_ref, y_ref, one_ref, two_ref, im_one_ref, im_two_ref,
     sol_ref, res_ref, left_ref, right_ref, pad_ref,
 ):
-    side = place_ref[0]
+    side = place_ref[0:1, :]
     for dx in range(3):
         got = got_ref[pl.ds(dx, PEERS, stride=3), :].T
         own, other = two_level(
-            [(got[base : base + 48], got[base + 48 : base + 64]) for base in (0, 64)], left_ref, right_ref
+            [(got[base : base + 48], got[base + 48 : base + 64]) for base in (0, 64)],
+            left_ref.at[dx],
+            right_ref.at[dx],
         )
         lines = [
             jnp.where(side == 0, other[a * CY : a * CY + 1, :], other[a * CY + 7 : a * CY + 8, :]) for a in range(3)
@@ -433,12 +440,12 @@
     return tuple(pl.BlockSpec(memory_space=space) for space in spaces)
 
 
-def call(kernel, outs, scratch=(), scalars=0, inputs=0, in_specs=None, out_specs=None, limit=40):
+def call(kernel, outs, scratch=(), inputs=0, in_specs=None, out_specs=None, limit=40):
     vmem = pltpu.VMEM
     return pl.pallas_call(
         kernel,
         out_shape=outs,
-        in_specs=in_specs or specs(*[pltpu.SMEM] * scalars, *[vmem] * (inputs - scalars)),
+        in_specs=in_specs or specs(*[vmem] * inputs),
         out_specs=out_specs or specs(*[vmem] * len(outs)),
         scratch_shapes=list(scratch),
         compiler_params=pltpu.CompilerParams(vmem_limit_bytes=limit * 2**20),
@@ -464,7 +471,8 @@
 
 
 def body(operator, basis_u, basis_c, right_side, new_rows):
-    place = jnp.stack([lax.axis_index("gy"), lax.axis_index(GX) % 2]).astype(jnp.int32)
+    row = lax.broadcasted_iota(jnp.int32, (8, 128), 0)
+    place = jnp.where(row == 0, lax.axis_index("gy"), lax.axis_index(GX) % 2).astype(jnp.int32)
     vmem, hbm = pltpu.VMEM, pltpu.HBM
     wire, info = call(
         pack_kernel,
@@ -474,7 +482,7 @@
             vmem((144, ROWS), F32),
             vmem((3, ROWS), F32),
             vmem((1, ROWS), jnp.int32),
-            vmem((2 * MAIN, ROWS), BF16),
+            vmem((ROWS, 2 * MAIN), BF16),
             vmem((128, ROWS), F32),
             vmem((56, 128), F32),
             vmem((PEERS * WIRE, 128), F32),
@@ -483,6 +491,7 @@
         ],
         in_specs=specs(hbm, hbm, hbm, hbm),
         out_specs=specs(hbm, vmem),
+        limit=56,
     )(operator, basis_c, right_side, new_rows.reshape(1, ROWS))
     got = exchange(wire)
     vector_outs = (shape(32, 128), shape(8, 128))
@@ -490,26 +499,29 @@
         unpack_kernel,
         (shape(MAIN * CY, 128), shape(48, 128), *vector_outs, shape(K, 128), shape(K, 128), shape(8, 128)),
         [
-            vmem((ROWS, SLOTS * PEERS), BF16),
-            vmem((SLOTS * PEERS, 256), BF16),
+            vmem((PEERS * WIRE, 128), F32),
+            vmem((2, ROWS, SLOTS * PEERS // 2), BF16),
+            vmem((2, 3, SLOTS * PEERS // 2, 256), BF16),
+            vmem((3, ROWS, 128), F32),
             vmem((48, SLOTS * PEERS), F32),
             vmem((128, SLOTS * PEERS), BF16),
             vmem((56, 128), F32),
+            pltpu.SemaphoreType.DMA((2,)),
         ],
-        scalars=1,
-        inputs=2,
+        in_specs=specs(vmem, hbm),
+        limit=40,
     )(place, got)
     pad = vmem((9 * 24, 128), F32)
     image_scratch = [pad, vmem(((K + 8) * CY, 128), F32)]
     image_outs = (shape(3 * CY, 128), shape(PEERS, 128))
-    image_one, send = call(functools.partial(image_kernel, 1), image_outs, image_scratch, scalars=1, inputs=7)(
+    image_one, send = call(functools.partial(image_kernel, 1), image_outs, image_scratch, inputs=7)(
         place, main, ext, *halo(one, line), one
     )
     sums = exchange(send)
     two, line, weights, h_one = call(
-        next_kernel, (*vector_outs, shape(K, 128), shape(8, 128)), scalars=1, inputs=6
+        next_kernel, (*vector_outs, shape(K, 128), shape(8, 128)), inputs=6
     )(place, sums, main, image_one, one, inverse)
-    image_two, send = call(functools.partial(image_kernel, 2), image_outs, image_scratch, scalars=1, inputs=8)(
+    image_two, send = call(functools.partial(image_kernel, 2), image_outs, image_scratch, inputs=8)(
         place, main, ext, *halo(two, line), one, two
     )
     sums = exchange(send)
@@ -520,8 +532,7 @@
     return call(
         last_kernel,
         (shape(3, ROWS), shape(3, ROWS)),
-        [vmem((48, SLOTS * PEERS), F32), vmem((256, SLOTS * PEERS), BF16), pad],
-        scalars=1,
+        [vmem((3, 48, SLOTS * PEERS), F32), vmem((3, 256, SLOTS * PEERS), BF16), pad],
         inputs=9,
     )(place, got, main, ext, y, one, two, image_one, image_two)
 

time: 158 us -> 147 us (0.930)
  local copies, waits for them, and re-layouts: 5.55 us -> 0.09 us
  Pallas kernels: 24.8 us -> 20.1 us
    unnamed x14 -> x6, local copies, waits for them, and re-layouts: 5.54 us -> 0.01 us
    pallas_call x1, Pallas kernels: 10.9 us -> 8.14 us  [body(): call(pack_kernel, (shape(PEERS * WIRE, 128), shape(8, ROWS, dtype=jnp.int...]
    pallas_call x4, Pallas kernels: 6.21 us -> 4.04 us  [the longest x1 2.66 us: body(): call(last_kernel, (shape(3, ROWS), shape(3, ROWS)), [vmem((3, 48, SLOTS *...]
where the time goes in v3:
time: 147 us; the launch traced here: 146 us
  waiting for transfers between devices  62.8 us (43%)
  blocking collectives  42.6 us (29%)
  Pallas kernels  20.1 us (14%)
  starting transfers between devices  19.2 us (13%)
    all_to_all x1, waiting for transfers between devices, exchange(): got = lax.all_to_all(shaped, GX_GY, split_axis=0, concat_axis=0, tiled=True)  48.9 us
    all_to_all x3, blocking collectives, exchange(): got = lax.all_to_all(shaped, GX_GY, split_axis=0, concat_axis=0, tiled=True)  42.6 us
    ppermute x4, waiting for transfers between devices, swap(): return lax.ppermute(plane, GX, pairs + [(j, i) for i, j in pairs])  11.6 us
    all_to_all x1, starting transfers between devices, exchange(): got = lax.all_to_all(shaped, GX_GY, split_axis=0, concat_axis=0, tiled=True)  10.9 us
    pallas_call x1, Pallas kernels, body(): call(pack_kernel, (shape(PEERS * WIRE, 128), shape(8, ROWS, dtype=jnp.int...  8.14 us
    ppermute x4, starting transfers between devices, swap(): return lax.ppermute(plane, GX, pairs + [(j, i) for i, j in pairs])  8.05 us
    pallas_call x1, Pallas kernels, body(): call(unpack_kernel, (shape(MAIN * CY, 128), shape(48, 128), *vector_outs,...  7.05 us
  transfers between devices with their start and end apart: 7, of which 5 were waited for; matrix products, arithmetic and copies ran while one was open for 0% of the time, Pallas kernels for 0%

profile of v3, /device:TPU:2, one launch (start us, length us, event | category | flops | bytes accessed | tf_op | source)
XLA Modules:
  0.0 145.5 jit_solution(9143665813723878399)
XLA Ops:
  0.6 8.1 %shard_map.68 = (f32[7552,128]{1,0:T(8,128)}, s32[8,1024]{1,0:T(8,128)}) custom-call(f32[243,1024]{1,0:T(8,128)} %op_hbm.1, f32[144,1024]{1,0:T(8,128)} %c_hbm.1, f32[3,1024]{1,0:T(4,128)} %b_hbm.1, s32[1,1024]{1,0:T(1,128)} %bitcast.20), custom_call_target="tpu_custom_call" | custom-call | tf_op jit(solution)/shard_map/pallas_call | solution.py:477
  8.8 10.9 %all-to-all-start = ((f32[128,59,1,128]{3,2,1,0:T(1,128)}), f32[128,59,1,128]{3,2,1,0:T(1,128)}, u32[]{:S(2)}, u32[]{:S(2)}) async-start(f32[128,59,1,128]{3,2,1,0:T(1,128)} %bitcast.19), calls=%async_computation | async-start | bytes 7733248 | tf_op jit(solution)/shard_map/all_to_all | solution.py:458
  19.8 48.9 %all-to-all-done = f32[128,59,1,128]{3,2,1,0:T(1,128)} async-done(((f32[128,59,1,128]{3,2,1,0:T(1,128)}), f32[128,59,1,128]{3,2,1,0:T(1,128)}, u32[]{:S(2)}, u32[]{:S(2)}) %all-to-all-start) | async-done | bytes 3866656 | tf_op jit(solution)/shard_map/all_to_all | solution.py:458
  68.6 0.1 iota.7.place_ref
  68.7 7.1 %shard_map.69 = (f32[3072,128]{1,0:T(8,128)S(1)}, f32[48,128]{1,0:T(8,128)S(1)}, f32[32,128]{1,0:T(8,128)S(1)}, f32[8,128]{1,0:T(8,128)S(1)}, f32[48,128]{1,0:T(...) custom-call(s32[8,128]{1,0:T(8,128)S(1)} %iota.7.place_ref, f32[7552,128]{1,0:T(8,128)} %bitcast.2.wire_hbm), custom_call_target="tpu_custom_call" | custom-call | tf_op jit(solution)/shard_map/pallas_call | solution.py:498
  75.8 0.1 collective-permute-start
  75.9 1.1 collective-permute-done.line_ref
  77.0 4.0 %collective-permute-start.2 = (f32[32,128]{1,0:T(8,128)S(1)}, f32[32,128]{1,0:T(8,128)S(1)}, u32[]{:S(2)}, u32[]{:S(2)}) collective-permute-start(f32[32,128]{1,0:T(8,128)S(1)} %constant_dynamic-update-slice_fusion.1), channel_id=1, source_target_pairs={{2,4},{6,8},{10,12},{14,16},{18,20},{22,24},{26,28},{30,32},{34,36... | collective-permute-start | bytes 49160 | tf_op jit(solution)/shard_map/ppermute | solution.py:464
  81.0 0.1 collective-permute-start.1
  81.1 5.7 %collective-permute-done.2.second_ref = f32[32,128]{1,0:T(8,128)S(1)} collective-permute-done((f32[32,128]{1,0:T(8,128)S(1)}, f32[32,128]{1,0:T(8,128)S(1)}, u32[]{:S(2)}, u32[]{:S(2)}) %collective-permute-start.2) | collective-permute-done | bytes 16416 | tf_op jit(solution)/shard_map/ppermute | solution.py:464
  86.8 0.0 collective-permute-done.1.first_ref
  86.8 0.4 shard_map.70
  87.3 14.0 %all_to_all.20 = f32[128,1,1,128]{3,2,1,0:T(1,128)S(1)} all-to-all(f32[128,1,1,128]{3,2,1,0:T(1,128)S(1)} %bitcast.17), channel_id=1, replica_groups=mesh['gx_0'=4,'gx_1'=4,'gx_2'=4,'gy'=2] {'gx_0','gx_1','gx_2','gy'}, dimensions={0} | all-to-all | bytes 131072 | tf_op jit(solution)/shard_map/all_to_all | solution.py:458
  101.3 0.5 shard_map.71
  101.8 0.1 collective-permute-start.3
  101.9 1.1 collective-permute-done.3.line_ref
  103.0 3.9 %collective-permute-start.5 = (f32[32,128]{1,0:T(8,128)S(1)}, f32[32,128]{1,0:T(8,128)S(1)}, u32[]{:S(2)}, u32[]{:S(2)}) collective-permute-start(f32[32,128]{1,0:T(8,128)S(1)} %constant_dynamic-update-slice_fusion), channel_id=1, source_target_pairs={{2,4},{6,8},{10,12},{14,16},{18,20},{22,24},{26,28},{30,32},{34,36... | collective-permute-start | bytes 49160 | tf_op jit(solution)/shard_map/ppermute | solution.py:464
  106.9 0.1 collective-permute-start.4
  107.0 5.9 %collective-permute-done.5.second_ref = f32[32,128]{1,0:T(8,128)S(1)} collective-permute-done((f32[32,128]{1,0:T(8,128)S(1)}, f32[32,128]{1,0:T(8,128)S(1)}, u32[]{:S(2)}, u32[]{:S(2)}) %collective-permute-start.5) | collective-permute-done | bytes 16416 | tf_op jit(solution)/shard_map/ppermute | solution.py:464
  112.9 0.4 shard_map.72
  113.3 14.0 %all_to_all.21 = f32[128,1,1,128]{3,2,1,0:T(1,128)S(1)} all-to-all(f32[128,1,1,128]{3,2,1,0:T(1,128)S(1)} %bitcast.18), channel_id=1, replica_groups=mesh['gx_0'=4,'gx_1'=4,'gx_2'=4,'gy'=2] {'gx_0','gx_1','gx_2','gy'}, dimensions={0} | all-to-all | bytes 131072 | tf_op jit(solution)/shard_map/all_to_all | solution.py:458
  127.3 0.9 shard_map.73
  128.2 14.7 %all_to_all.22 = f32[128,3,1,128]{3,2,1,0:T(1,128)S(1)} all-to-all(f32[128,3,1,128]{3,2,1,0:T(1,128)S(1)} %bitcast.16), channel_id=1, replica_groups=mesh['gx_0'=4,'gx_1'=4,'gx_2'=4,'gy'=2] {'gx_0','gx_1','gx_2','gy'}, dimensions={0} | all-to-all | bytes 393216 | tf_op jit(solution)/shard_map/all_to_all | solution.py:458
  142.9 2.7 %shard_map.74 = (f32[3,1024]{1,0:T(4,128)}, f32[3,1024]{1,0:T(4,128)}) custom-call(s32[8,128]{1,0:T(8,128)S(1)} %iota.7.place_ref, f32[384,128]{1,0:T(8,128)S(1)} %bitcast.13, f32[3072,128]{1,0:T(8,128)S(1)} %get-tuple-element.22.main_ref, f32[48,128]{1,0:T(8,128)S(1)} %get-tuple-element.23.ext_ref, f32[8,128]{1,0:T(8,128)S(1)} %get-tuple-element.38.y_ref, ...), custom_call_target="tpu_custom_call" | custom-call | tf_op jit(solution)/shard_map/pallas_call | solution.py:532
  (10 shorter events, 0.0 us)
Async XLA Ops:
  8.8 59.8 %all-to-all-start = ((f32[128,59,1,128]{3,2,1,0:T(1,128)}), f32[128,59,1,128]{3,2,1,0:T(1,128)}, u32[]{:S(2)}, u32[]{:S(2)}) async-start(f32[128,59,1,128]{3,2,1,0:T(1,128)} %bitcast.19), calls=%async_computation | async-start | bytes 7733248 | tf_op jit(solution)/shard_map/all_to_all | solution.py:458
  68.7 58.6 %copy-start = (f32[144,1024]{1,0:T(8,128)S(1)}, f32[144,1024]{1,0:T(8,128)}, u32[]{:S(2)}) copy-start(f32[144,1024]{1,0:T(8,128)} %u_ref.1) | copy-start | bytes 1769476
  68.7 58.6 %copy-start.1 = (s32[8,1024]{1,0:T(8,128)S(1)}, s32[8,1024]{1,0:T(8,128)}, u32[]{:S(2)}) copy-start(s32[8,1024]{1,0:T(8,128)} %get-tuple-element.36.info_ref) | copy-start | bytes 98308
  75.8 1.2 collective-permute-start
  77.0 9.8 %collective-permute-start.2 = (f32[32,128]{1,0:T(8,128)S(1)}, f32[32,128]{1,0:T(8,128)S(1)}, u32[]{:S(2)}, u32[]{:S(2)}) collective-permute-start(f32[32,128]{1,0:T(8,128)S(1)} %constant_dynamic-update-slice_fusion.1), channel_id=1, source_target_pairs={{2,4},{6,8},{10,12},{14,16},{18,20},{22,24},{26,28},{30,32},{34,36... | collective-permute-start | bytes 49160 | tf_op jit(solution)/shard_map/ppermute | solution.py:464
  81.0 5.8 %collective-permute-start.1 = (f32[32,128]{1,0:T(8,128)S(1)}, f32[32,128]{1,0:T(8,128)S(1)}, u32[]{:S(2)}, u32[]{:S(2)}) collective-permute-start(f32[32,128]{1,0:T(8,128)S(1)} %constant_dynamic-update-slice_fusion.1), channel_id=1, source_target_pairs={{0,2},{4,6},{8,10},{12,14},{16,18},{20,22},{24,26},{28,30},{32,34}... | collective-permute-start | bytes 49160 | tf_op jit(solution)/shard_map/ppermute | solution.py:464
  101.8 1.2 collective-permute-start.3
  103.0 9.8 %collective-permute-start.5 = (f32[32,128]{1,0:T(8,128)S(1)}, f32[32,128]{1,0:T(8,128)S(1)}, u32[]{:S(2)}, u32[]{:S(2)}) collective-permute-start(f32[32,128]{1,0:T(8,128)S(1)} %constant_dynamic-update-slice_fusion), channel_id=1, source_target_pairs={{2,4},{6,8},{10,12},{14,16},{18,20},{22,24},{26,28},{30,32},{34,36... | collective-permute-start | bytes 49160 | tf_op jit(solution)/shard_map/ppermute | solution.py:464
  106.9 6.0 %collective-permute-start.4 = (f32[32,128]{1,0:T(8,128)S(1)}, f32[32,128]{1,0:T(8,128)S(1)}, u32[]{:S(2)}, u32[]{:S(2)}) collective-permute-start(f32[32,128]{1,0:T(8,128)S(1)} %constant_dynamic-update-slice_fusion), channel_id=1, source_target_pairs={{0,2},{4,6},{8,10},{12,14},{16,18},{20,22},{24,26},{28,30},{32,34}... | collective-permute-start | bytes 49160 | tf_op jit(solution)/shard_map/ppermute | solution.py:464

commit v4 on v3

--- a/solution.py
+++ b/solution.py
@@ -39,8 +39,17 @@
     return lax.dot_general(x, y, dims, precision=HIGHEST, preferred_element_type=F32)
 
 
+def chosen(mask):
+    return jnp.where(mask, jnp.ones(mask.shape, BF16), jnp.zeros(mask.shape, BF16))
+
+
 def half_sum(x):
     return x[:, :128] + x[:, 128:]
+
+
+def squared(x):
+    x = jnp.concatenate([x, jnp.zeros((64, 64), F32)], axis=1)
+    return jnp.concatenate([x, jnp.zeros((64, 128), F32)], axis=0)
 
 
 def folded(rows, start_ref):
@@ -84,6 +93,12 @@
     return half + jnp.where(row == lane, 0.0, half.T)
 
 
+def pieces(source, target, size):
+    count = source.shape[0]
+    parts = [pl.ds(i, min(size, count - i)) for i in range(0, count, size)]
+    return [(source.at[part], target.at[part]) for part in parts]
+
+
 def pack_kernel(
     op_hbm, c_hbm, b_hbm, rows_hbm, wire_hbm, info_ref,
     op_ref, c_ref, b_ref, rows_ref, p_ref, a_ref, fold_ref, wire_ref, in_sem, out_sem,
@@ -91,7 +106,7 @@
     copies = [
         pltpu.make_async_copy(source, target, in_sem.at[i])
         for i, (source, target) in enumerate(
-            [(rows_hbm, rows_ref), (c_hbm, c_ref), (b_hbm, b_ref), (op_hbm, op_ref)]
+            [(rows_hbm, rows_ref), (b_hbm, b_ref), *pieces(c_hbm, c_ref, 72), *pieces(op_hbm, op_ref, 128)]
         )
     ]
     for copy in copies:
@@ -114,7 +129,7 @@
         ranks.append(jnp.sum(onehot_f[:, block * 128 : (block + 1) * 128] * count, axis=0, keepdims=True))
         seen = seen + jnp.dot(part, ones, preferred_element_type=F32)
     rank = jnp.concatenate(ranks, axis=1)
-    rank_at = jnp.where(onehot, rank, -1.0)
+    rank_at = jnp.where(onehot, rank, -1.0).astype(BF16)
     info_ref[0:1, :] = target
     info_ref[1:2, :] = rank.astype(jnp.int32)
     info_ref[2:3, :] = local
@@ -124,13 +139,19 @@
     middle = jnp.concatenate([c_ref[128:144, :], op_ref[0:112, :]], axis=0)
     for tile, x in enumerate((c_ref[0:128, :], middle, op_ref[112:240, :])):
         p_ref[:, tile * 256 : tile * 256 + 128], p_ref[:, tile * 256 + 128 : (tile + 1) * 256] = split(x.T)
-    gram = jnp.zeros((64, 128), F32)
-    a_ref[48:128, :] = jnp.zeros((80, ROWS), F32)
-    for a in range(3):
-        a_ref[0:48, :] = c_ref[a * K : (a + 1) * K, :]
-        a_ref[48:49, :] = b_ref[a : a + 1, :]
-        gram = gram + exact_dot(a_ref[0:64, :], a_ref[...], NT)
-    bands = folded(gram, fold_ref)
+    sums, low = jnp.zeros((192, 64), F32), jnp.zeros((64, 64), F32)
+    for a in range(3):
+        a_ref[a, 48:64, :] = jnp.zeros((16, ROWS), F32)
+        a_ref[a, 0:48, :] = c_ref[a * K : (a + 1) * K, :]
+        a_ref[a, 48:49, :] = b_ref[a : a + 1, :]
+        one, two = split(a_ref[a])
+        three = (a_ref[a] - one.astype(F32) - two.astype(F32)).astype(BF16)
+        terms = jnp.concatenate([one, two, three], axis=0)
+        sums = sums + lax.dot_general(terms, one, NT, preferred_element_type=F32)
+        low = low + lax.dot_general(two, two, NT, preferred_element_type=F32)
+    cross = squared(sums[64:128] + sums[128:192])
+    gram = squared(sums[0:64] + low) + cross + cross.T
+    bands = folded(gram[0:64], fold_ref)
     for i in range(GRAM):
         wire_ref[pl.ds(49 + i, PEERS, stride=WIRE), :] = jnp.broadcast_to(bands[i : i + 1, :], (PEERS, 128))
 
@@ -146,7 +167,7 @@
     count = PEERS // CHUNKS
     for chunk in range(CHUNKS):
         mine = rank_at[chunk * count : (chunk + 1) * count]
-        choice = [jnp.where(mine == k, 1.0, 0.0).astype(BF16) for k in range(SLOTS)]
+        choice = [chosen(mine == k) for k in range(SLOTS)]
         moved = jnp.dot(jnp.concatenate(choice, axis=0), p_ref[...], preferred_element_type=F32)
         for tile in range(3):
             both = half_sum(moved[:, tile * 256 : (tile + 1) * 256])
@@ -163,14 +184,15 @@
 
 def two_level(groups, left_ref, right_ref):
     eight = lax.broadcasted_iota(jnp.int32, (CY, 128), 0)
-    deep = lax.broadcasted_iota(jnp.int32, (128, 128), 0)
+    deep = lax.broadcasted_iota(jnp.int32, (128, 128), 0).astype(F32).astype(BF16)
     count = groups[0][0].shape[0] // SLOTS
     for g, (values, labels) in enumerate(groups):
         labels = labels.astype(jnp.int32)
-        y, z = labels // CZ, labels % CZ
+        y, z = labels // CZ, (labels % CZ).astype(F32)
         for k in range(SLOTS):
             cols = slice(k * 128, (k + 1) * 128)
-            right_ref[g * 128 : (g + 1) * 128, cols] = jnp.where(deep == z[k : k + 1], 1.0, 0.0).astype(BF16)
+            row = jnp.broadcast_to(z[k : k + 1], (128, 128)).astype(BF16)
+            right_ref[g * 128 : (g + 1) * 128, cols] = chosen(deep == row)
             here = eight == y[k : k + 1]
             for c in range(count):
                 row = (g * count + c) * CY
@@ -195,13 +217,11 @@
     return result
 
 
-def put_vector(vector, place_ref, v_ref, line_ref):
-    lower = place_ref[0:1, :] == 0
-    line_ref[...] = jnp.zeros((8, 128), F32)
+def put_vector(vector, lines, v_ref):
     v_ref[24:32, :] = jnp.zeros((8, 128), F32)
     for a in range(3):
         v_ref[a * CY : (a + 1) * CY, :] = vector[a]
-        line_ref[a : a + 1, :] = jnp.where(lower, vector[a][7:8, :], vector[a][0:1, :])
+        v_ref[24 + a : 25 + a, :] = lines[a]
 
 
 def swept(work, begin, count):
@@ -223,7 +243,7 @@
 
 
 def unpack_kernel(
-    place_ref, wire_hbm, main_ref, ext_ref, v_ref, line_ref, inv_ref, start_ref, beta_ref,
+    place_ref, wire_hbm, main_ref, ext_ref, v_ref, inv_ref, start_ref, beta_ref,
     wire_ref, t_ref, r_ref, part_ref, left_ref, right_ref, fold_ref, in_sem,
 ):
     half = PEERS // 2
@@ -232,7 +252,7 @@
         rows = pl.ds(part * half * WIRE, half * WIRE)
         copies.append(pltpu.make_async_copy(wire_hbm.at[rows], wire_ref.at[rows], in_sem.at[part]))
         copies[-1].start()
-    node = lax.broadcasted_iota(jnp.int32, (ROWS, 128), 0).astype(F32)
+    deep = lax.broadcasted_iota(jnp.int32, (CZ, 128), 0).astype(F32).astype(BF16)
     for part in range(2):
         copies[part].wait()
         if part == 1:
@@ -249,9 +269,16 @@
                 work = swept(work, begin, 4)
         first = part * half * WIRE
         labels = wire_ref[pl.ds(first + 48, half, stride=WIRE), :].T[6 * SLOTS : 7 * SLOTS]
-        labels = jnp.concatenate([labels[0:8], labels[8:16]], axis=1)
+        labels = jnp.concatenate([labels[0:8], labels[8:16]], axis=1).astype(jnp.int32)
+        label_y, label_z = (labels // CZ).astype(F32), (labels % CZ).astype(F32)
         for i in range(8):
-            t_ref[part, :, i * 128 : (i + 1) * 128] = jnp.where(node == labels[i : i + 1], 1.0, 0.0).astype(BF16)
+            here = deep == jnp.broadcast_to(label_z[i : i + 1], (CZ, 128)).astype(BF16)
+            here = chosen(here)
+            row = jnp.broadcast_to(label_y[i : i + 1], (CZ, 128)).astype(BF16)
+            for y in range(CY):
+                t_ref[part, y * CZ : (y + 1) * CZ, i * 128 : (i + 1) * 128] = jnp.where(
+                    row == y, here, jnp.zeros((CZ, 128), BF16)
+                )
         for tile in range(3):
             for k in range(SLOTS):
                 high, low = split(wire_ref[pl.ds(first + tile * SLOTS + k, half, stride=WIRE), :])
@@ -277,8 +304,9 @@
     beta = jnp.sqrt(load_sq - jnp.sum(raw * weights, axis=0, keepdims=True))
     beta_ref[...] = jnp.broadcast_to(beta, (8, 128))
     load = [ext[24 + a * CY : 24 + (a + 1) * CY, :] for a in range(3)]
-    vector = minus_combined(load, main_ref, weights)
-    put_vector([v / beta for v in vector], place_ref, v_ref, line_ref)
+    vector = [v / beta for v in minus_combined(load, main_ref, weights)]
+    lower = place_ref[0:1, :] == 0
+    put_vector(vector, [jnp.where(lower, v[CY - 1 : CY], v[0:1]) for v in vector], v_ref)
 
 
 def put_plane(pad_ref, dx, plane, line, side):
@@ -312,18 +340,25 @@
     return total
 
 
-def image_kernel(count, place_ref, main_ref, ext_ref, line_ref, first_ref, second_ref, *refs):
-    vectors, (image_ref, send_ref, pad_ref, part_ref) = refs[:count], refs[count:]
+def image_kernel(count, place_ref, main_ref, ext_ref, first_ref, second_ref, *refs):
+    vectors, (image_ref, send_ref, *edges, pad_ref, part_ref) = refs[:count], refs[count:]
     side = place_ref[0:1, :]
     even = place_ref[1:2, :] == 0
     first, second = first_ref[...], second_ref[...]
     up, down = jnp.where(even, second, first), jnp.where(even, first, second)
     put_plane(pad_ref, 0, up[0:24], up[24:32], side)
-    put_plane(pad_ref, 1, vectors[-1][0:24, :], line_ref[...], side)
+    put_plane(pad_ref, 1, vectors[-1][0:24, :], vectors[-1][24:32, :], side)
     put_plane(pad_ref, 2, down[0:24], down[24:32], side)
     image = stencil(main_ref, ext_ref, pad_ref)
     for a in range(3):
         image_ref[a * CY : (a + 1) * CY, :] = image[a]
+    for edge_ref in edges:
+        last = main_ref[pl.ds(CY - 1, 3 * K, stride=CY), :]
+        edge_ref[0 : 3 * K, :] = jnp.where(side == 0, last, main_ref[pl.ds(0, 3 * K, stride=CY), :])
+        edge_ref[3 * K :, :] = jnp.zeros((8, 128), F32)
+        for a in range(3):
+            row = 3 * K + a
+            edge_ref[row : row + 1, :] = jnp.where(side == 0, image[a][CY - 1 : CY], image[a][0:1])
     for m in range(K):
         rows = [(a * K + m) * CY for a in range(3)]
         part_ref[m * CY : (m + 1) * CY, :] = sum(
@@ -345,7 +380,7 @@
     return exact_dot(got_ref[...], jnp.ones((PEERS, 128), F32), TN)
 
 
-def next_kernel(place_ref, got_ref, main_ref, image_ref, one_ref, inv_ref, v_ref, line_ref, weights_ref, h_ref):
+def next_kernel(got_ref, main_ref, image_ref, one_ref, other_ref, inv_ref, v_ref, weights_ref, h_ref):
     sums = totals(got_ref)
     weights = exact_dot(inv_ref[...], sums)
     h11 = sums[K + 1 : K + 2, :]
@@ -354,8 +389,13 @@
     begin = [
         image_ref[a * CY : (a + 1) * CY, :] - h11 * one_ref[a * CY : (a + 1) * CY, :] for a in range(3)
     ]
-    vector = minus_combined(begin, main_ref, weights)
-    put_vector([v / h21 for v in vector], place_ref, v_ref, line_ref)
+    vector = [v / h21 for v in minus_combined(begin, main_ref, weights)]
+    lines = []
+    for a in range(3):
+        along_line = jnp.sum(other_ref[a * K : (a + 1) * K, :] * weights, axis=0, keepdims=True)
+        line = other_ref[3 * K + a : 3 * K + a + 1, :] - along_line - h11 * one_ref[24 + a : 25 + a, :]
+        lines.append(line / h21)
+    put_vector(vector, lines, v_ref)
     weights_ref[...] = weights
     h_ref[...] = jnp.zeros((8, 128), F32)
     h_ref[0:1, :] = h11
@@ -464,10 +504,8 @@
     return lax.ppermute(plane, GX, pairs + [(j, i) for i, j in pairs])
 
 
-def halo(vector, line):
-    other = lax.ppermute(line, "gy", [(0, 1), (1, 0)])
-    plane = lax.dynamic_update_slice(vector, other, (24, 0))
-    return other, swap(plane, 0), swap(plane, 1)
+def other_core(x):
+    return lax.ppermute(x, "gy", [(0, 1), (1, 0)])
 
 
 def body(operator, basis_u, basis_c, right_side, new_rows):
@@ -483,10 +521,10 @@
             vmem((3, ROWS), F32),
             vmem((1, ROWS), jnp.int32),
             vmem((ROWS, 2 * MAIN), BF16),
-            vmem((128, ROWS), F32),
+            vmem((3, 64, ROWS), F32),
             vmem((56, 128), F32),
             vmem((PEERS * WIRE, 128), F32),
-            pltpu.SemaphoreType.DMA((4,)),
+            pltpu.SemaphoreType.DMA((6,)),
             pltpu.SemaphoreType.DMA((CHUNKS,)),
         ],
         in_specs=specs(hbm, hbm, hbm, hbm),
@@ -494,10 +532,10 @@
         limit=56,
     )(operator, basis_c, right_side, new_rows.reshape(1, ROWS))
     got = exchange(wire)
-    vector_outs = (shape(32, 128), shape(8, 128))
-    main, ext, one, line, inverse, start, beta = call(
+    plane = shape(32, 128)
+    main, ext, one, inverse, start, beta = call(
         unpack_kernel,
-        (shape(MAIN * CY, 128), shape(48, 128), *vector_outs, shape(K, 128), shape(K, 128), shape(8, 128)),
+        (shape(MAIN * CY, 128), shape(48, 128), plane, shape(K, 128), shape(K, 128), shape(8, 128)),
         [
             vmem((PEERS * WIRE, 128), F32),
             vmem((2, ROWS, SLOTS * PEERS // 2), BF16),
@@ -514,15 +552,17 @@
     pad = vmem((9 * 24, 128), F32)
     image_scratch = [pad, vmem(((K + 8) * CY, 128), F32)]
     image_outs = (shape(3 * CY, 128), shape(PEERS, 128))
-    image_one, send = call(functools.partial(image_kernel, 1), image_outs, image_scratch, inputs=7)(
-        place, main, ext, *halo(one, line), one
-    )
+    one = lax.dynamic_update_slice(one, other_core(one[24:32]), (24, 0))
+    image_one, send, edge = call(
+        functools.partial(image_kernel, 1), (*image_outs, shape(3 * K + 8, 128)), image_scratch, inputs=6
+    )(place, main, ext, swap(one, 0), swap(one, 1), one)
+    other = other_core(edge)
     sums = exchange(send)
-    two, line, weights, h_one = call(
-        next_kernel, (*vector_outs, shape(K, 128), shape(8, 128)), inputs=6
-    )(place, sums, main, image_one, one, inverse)
-    image_two, send = call(functools.partial(image_kernel, 2), image_outs, image_scratch, inputs=8)(
-        place, main, ext, *halo(two, line), one, two
+    two, weights, h_one = call(next_kernel, (plane, shape(K, 128), shape(8, 128)), inputs=6)(
+        sums, main, image_one, one, other, inverse
+    )
+    image_two, send = call(functools.partial(image_kernel, 2), image_outs, image_scratch, inputs=7)(
+        place, main, ext, swap(two, 0), swap(two, 1), one, two
     )
     sums = exchange(send)
     wire, y = call(send_kernel, (shape(PEERS * 3, 128), shape(8, 128)), inputs=8)(

time: 147 us -> 145 us (0.986)
  Pallas kernels: 20.1 us -> 18.5 us
  transfers between devices with their start and end apart: 7 -> 7, of which waited for: 5 -> 4; matrix products, arithmetic and copies ran while one was open for 0% -> 0% of each run, Pallas kernels for 0% -> 0%
where the time goes in v4:
time: 145 us; the launch traced here: 143 us
  waiting for transfers between devices  61.6 us (42%)
  blocking collectives  42.7 us (29%)
  starting transfers between devices  19.2 us (13%)
  Pallas kernels  18.5 us (13%)
    all_to_all x1, waiting for transfers between devices, exchange(): got = lax.all_to_all(shaped, GX_GY, split_axis=0, concat_axis=0, tiled=True)  48.9 us
    all_to_all x3, blocking collectives, exchange(): got = lax.all_to_all(shaped, GX_GY, split_axis=0, concat_axis=0, tiled=True)  42.7 us
    ppermute x4, waiting for transfers between devices, swap(): return lax.ppermute(plane, GX, pairs + [(j, i) for i, j in pairs])  11.6 us
    all_to_all x1, starting transfers between devices, exchange(): got = lax.all_to_all(shaped, GX_GY, split_axis=0, concat_axis=0, tiled=True)  10.9 us
    ppermute x4, starting transfers between devices, swap(): return lax.ppermute(plane, GX, pairs + [(j, i) for i, j in pairs])  8.07 us
    pallas_call x1, Pallas kernels, body(): call(unpack_kernel, (shape(MAIN * CY, 128), shape(48, 128), plane, shape(...  7.01 us
    pallas_call x1, Pallas kernels, body(): call(pack_kernel, (shape(PEERS * WIRE, 128), shape(8, ROWS, dtype=jnp.int...  6.92 us
  transfers between devices with their start and end apart: 7, of which 4 were waited for; matrix products, arithmetic and copies ran while one was open for 0% of the time, Pallas kernels for 0%

profile of v4, /device:TPU:2, one launch (start us, length us, event | category | flops | bytes accessed | tf_op | source)
XLA Modules:
  0.0 142.8 jit_solution(7582256645941019250)
XLA Ops:
  0.6 6.9 %shard_map.68 = (f32[7552,128]{1,0:T(8,128)}, s32[8,1024]{1,0:T(8,128)}) custom-call(f32[243,1024]{1,0:T(8,128)} %op_hbm.1, f32[144,1024]{1,0:T(8,128)} %c_hbm.1, f32[3,1024]{1,0:T(4,128)} %b_hbm.1, s32[1,1024]{1,0:T(1,128)} %bitcast.20), custom_call_target="tpu_custom_call" | custom-call | tf_op jit(solution)/shard_map/pallas_call | solution.py:515
  7.6 10.9 %all-to-all-start = ((f32[128,59,1,128]{3,2,1,0:T(1,128)}), f32[128,59,1,128]{3,2,1,0:T(1,128)}, u32[]{:S(2)}, u32[]{:S(2)}) async-start(f32[128,59,1,128]{3,2,1,0:T(1,128)} %bitcast.19), calls=%async_computation | async-start | bytes 7733248 | tf_op jit(solution)/shard_map/all_to_all | solution.py:498
  18.5 48.9 %all-to-all-done = f32[128,59,1,128]{3,2,1,0:T(1,128)} async-done(((f32[128,59,1,128]{3,2,1,0:T(1,128)}), f32[128,59,1,128]{3,2,1,0:T(1,128)}, u32[]{:S(2)}, u32[]{:S(2)}) %all-to-all-start) | async-done | bytes 3866656 | tf_op jit(solution)/shard_map/all_to_all | solution.py:498
  67.4 0.1 iota.7.place_ref
  67.5 7.0 %shard_map.69 = (f32[3072,128]{1,0:T(8,128)S(1)}, f32[48,128]{1,0:T(8,128)S(1)}, f32[32,128]{1,0:T(8,128)S(1)}, f32[48,128]{1,0:T(8,128)S(1)}, f32[48,128]{1,0:T(8,128)S(1)}, /*index=5*/f32[8,128]{1,0:T(8,128)S(1)}) custom-call(s32[8,128]{1,0:T(8,128)S(1)} %iota.7.place_ref, f32[7552,128]{1,0:T(8,128)} %bitcast.2.wire_hbm), custom_call_target="tpu_custom_call" | custom-call | tf_op jit(solution)/shard_map/pallas_call | solution.py:536
  74.5 0.1 collective-permute-start
  74.6 1.2 collective-permute-done
  75.7 4.0 %collective-permute-start.2 = (f32[32,128]{1,0:T(8,128)S(1)}, f32[32,128]{1,0:T(8,128)S(1)}, u32[]{:S(2)}, u32[]{:S(2)}) collective-permute-start(f32[32,128]{1,0:T(8,128)S(1)} %constant_dynamic-update-slice_fusion.refs_0_.one_ref), channel_id=1, source_target_pairs={{2,4},{6,8},{10,12},{14,16},{18,20},{22,24},{26,28},{30,32},{34,36... | collective-permute-start | bytes 49160 | tf_op jit(solution)/shard_map/ppermute | solution.py:504
  79.8 0.1 collective-permute-start.1
  79.9 5.7 %collective-permute-done.2.second_ref = f32[32,128]{1,0:T(8,128)S(1)} collective-permute-done((f32[32,128]{1,0:T(8,128)S(1)}, f32[32,128]{1,0:T(8,128)S(1)}, u32[]{:S(2)}, u32[]{:S(2)}) %collective-permute-start.2) | collective-permute-done | bytes 16416 | tf_op jit(solution)/shard_map/ppermute | solution.py:504
  85.6 0.0 collective-permute-done.1.first_ref
  85.6 0.4 shard_map.70
  86.0 0.1 collective-permute-start.3
  86.1 14.1 %all_to_all.20 = f32[128,1,1,128]{3,2,1,0:T(1,128)S(1)} all-to-all(f32[128,1,1,128]{3,2,1,0:T(1,128)S(1)} %bitcast.17), channel_id=1, replica_groups=mesh['gx_0'=4,'gx_1'=4,'gx_2'=4,'gy'=2] {'gx_0','gx_1','gx_2','gy'}, dimensions={0} | all-to-all | bytes 131072 | tf_op jit(solution)/shard_map/all_to_all | solution.py:498
  100.2 0.0 collective-permute-done.3.other_ref
  100.2 0.5 shard_map.71
  100.7 3.9 %collective-permute-start.5 = (f32[32,128]{1,0:T(8,128)S(1)}, f32[32,128]{1,0:T(8,128)S(1)}, u32[]{:S(2)}, u32[]{:S(2)}) collective-permute-start(f32[32,128]{1,0:T(8,128)S(1)} %get-tuple-element.28.refs_1_.two_ref), channel_id=1, source_target_pairs={{2,4},{6,8},{10,12},{14,16},{18,20},{22,24},{26,28},{30,32},{34,36... | collective-permute-start | bytes 49160 | tf_op jit(solution)/shard_map/ppermute | solution.py:504
  104.6 0.1 collective-permute-start.4
  104.7 5.9 %collective-permute-done.5.second_ref = f32[32,128]{1,0:T(8,128)S(1)} collective-permute-done((f32[32,128]{1,0:T(8,128)S(1)}, f32[32,128]{1,0:T(8,128)S(1)}, u32[]{:S(2)}, u32[]{:S(2)}) %collective-permute-start.5) | collective-permute-done | bytes 16416 | tf_op jit(solution)/shard_map/ppermute | solution.py:504
  110.6 0.4 shard_map.72
  111.0 14.0 %all_to_all.21 = f32[128,1,1,128]{3,2,1,0:T(1,128)S(1)} all-to-all(f32[128,1,1,128]{3,2,1,0:T(1,128)S(1)} %bitcast.18), channel_id=1, replica_groups=mesh['gx_0'=4,'gx_1'=4,'gx_2'=4,'gy'=2] {'gx_0','gx_1','gx_2','gy'}, dimensions={0} | all-to-all | bytes 131072 | tf_op jit(solution)/shard_map/all_to_all | solution.py:498
  125.0 0.9 shard_map.73
  125.9 14.7 %all_to_all.22 = f32[128,3,1,128]{3,2,1,0:T(1,128)S(1)} all-to-all(f32[128,3,1,128]{3,2,1,0:T(1,128)S(1)} %bitcast.16), channel_id=1, replica_groups=mesh['gx_0'=4,'gx_1'=4,'gx_2'=4,'gy'=2] {'gx_0','gx_1','gx_2','gy'}, dimensions={0} | all-to-all | bytes 393216 | tf_op jit(solution)/shard_map/all_to_all | solution.py:498
  140.6 2.2 %shard_map.74 = (f32[3,1024]{1,0:T(4,128)}, f32[3,1024]{1,0:T(4,128)}) custom-call(s32[8,128]{1,0:T(8,128)S(1)} %iota.7.place_ref, f32[384,128]{1,0:T(8,128)S(1)} %bitcast.13, f32[3072,128]{1,0:T(8,128)S(1)} %get-tuple-element.21.main_ref, f32[48,128]{1,0:T(8,128)S(1)} %get-tuple-element.22.ext_ref, f32[8,128]{1,0:T(8,128)S(1)} %get-tuple-element.36.y_ref, ...), custom_call_target="tpu_custom_call" | custom-call | tf_op jit(solution)/shard_map/pallas_call | solution.py:572
  (8 shorter events, 0.0 us)
Async XLA Ops:
  7.6 59.8 %all-to-all-start = ((f32[128,59,1,128]{3,2,1,0:T(1,128)}), f32[128,59,1,128]{3,2,1,0:T(1,128)}, u32[]{:S(2)}, u32[]{:S(2)}) async-start(f32[128,59,1,128]{3,2,1,0:T(1,128)} %bitcast.19), calls=%async_computation | async-start | bytes 7733248 | tf_op jit(solution)/shard_map/all_to_all | solution.py:498
  67.5 57.5 %copy-start = (f32[144,1024]{1,0:T(8,128)S(1)}, f32[144,1024]{1,0:T(8,128)}, u32[]{:S(2)}) copy-start(f32[144,1024]{1,0:T(8,128)} %u_ref.1) | copy-start | bytes 1769476
  67.5 57.5 %copy-start.1 = (s32[8,1024]{1,0:T(8,128)S(1)}, s32[8,1024]{1,0:T(8,128)}, u32[]{:S(2)}) copy-start(s32[8,1024]{1,0:T(8,128)} %get-tuple-element.34.info_ref) | copy-start | bytes 98308
  74.5 1.2 collective-permute-start
  75.7 9.8 %collective-permute-start.2 = (f32[32,128]{1,0:T(8,128)S(1)}, f32[32,128]{1,0:T(8,128)S(1)}, u32[]{:S(2)}, u32[]{:S(2)}) collective-permute-start(f32[32,128]{1,0:T(8,128)S(1)} %constant_dynamic-update-slice_fusion.refs_0_.one_ref), channel_id=1, source_target_pairs={{2,4},{6,8},{10,12},{14,16},{18,20},{22,24},{26,28},{30,32},{34,36... | collective-permute-start | bytes 49160 | tf_op jit(solution)/shard_map/ppermute | solution.py:504
  79.8 5.8 %collective-permute-start.1 = (f32[32,128]{1,0:T(8,128)S(1)}, f32[32,128]{1,0:T(8,128)S(1)}, u32[]{:S(2)}, u32[]{:S(2)}) collective-permute-start(f32[32,128]{1,0:T(8,128)S(1)} %constant_dynamic-update-slice_fusion.refs_0_.one_ref), channel_id=1, source_target_pairs={{0,2},{4,6},{8,10},{12,14},{16,18},{20,22},{24,26},{28,30},{32,34}... | collective-permute-start | bytes 49160 | tf_op jit(solution)/shard_map/ppermute | solution.py:504
  86.0 14.2 %collective-permute-start.3 = (f32[152,128]{1,0:T(8,128)S(1)}, f32[152,128]{1,0:T(8,128)S(1)}, u32[]{:S(2)}, u32[]{:S(2)}) collective-permute-start(f32[152,128]{1,0:T(8,128)S(1)} %get-tuple-element.26), channel_id=1, source_target_pairs={{0,1},{1,0},{2,3},{3,2},{4,5},{5,4},{6,7},{7,6},{8,9},{9,8},{10,11... | collective-permute-start | bytes 233480 | tf_op jit(solution)/shard_map/ppermute | solution.py:508
  100.7 9.9 %collective-permute-start.5 = (f32[32,128]{1,0:T(8,128)S(1)}, f32[32,128]{1,0:T(8,128)S(1)}, u32[]{:S(2)}, u32[]{:S(2)}) collective-permute-start(f32[32,128]{1,0:T(8,128)S(1)} %get-tuple-element.28.refs_1_.two_ref), channel_id=1, source_target_pairs={{2,4},{6,8},{10,12},{14,16},{18,20},{22,24},{26,28},{30,32},{34,36... | collective-permute-start | bytes 49160 | tf_op jit(solution)/shard_map/ppermute | solution.py:504
  104.6 6.0 %collective-permute-start.4 = (f32[32,128]{1,0:T(8,128)S(1)}, f32[32,128]{1,0:T(8,128)S(1)}, u32[]{:S(2)}, u32[]{:S(2)}) collective-permute-start(f32[32,128]{1,0:T(8,128)S(1)} %get-tuple-element.28.refs_1_.two_ref), channel_id=1, source_target_pairs={{0,2},{4,6},{8,10},{12,14},{16,18},{20,22},{24,26},{28,30},{32,34}... | collective-permute-start | bytes 49160 | tf_op jit(solution)/shard_map/ppermute | solution.py:504

commit v5 on v4

--- a/solution.py
+++ b/solution.py
@@ -24,6 +24,7 @@
 BANDS = 25
 GRAM = 10
 WIRE = 49 + GRAM
+PARTS = 1
 CHUNKS = 8
 NT = (((1,), (1,)), ((), ()))
 TN = (((0,), (0,)), ((), ()))
@@ -244,56 +245,45 @@
 
 def unpack_kernel(
     place_ref, wire_hbm, main_ref, ext_ref, v_ref, inv_ref, start_ref, beta_ref,
-    wire_ref, t_ref, r_ref, part_ref, left_ref, right_ref, fold_ref, in_sem,
+    wire_ref, t_ref, r_ref, left_ref, right_ref, fold_ref, in_sem,
 ):
-    half = PEERS // 2
     copies = []
-    for part in range(2):
-        rows = pl.ds(part * half * WIRE, half * WIRE)
-        copies.append(pltpu.make_async_copy(wire_hbm.at[rows], wire_ref.at[rows], in_sem.at[part]))
+    for part, (source, target) in enumerate(pieces(wire_hbm, wire_ref, PEERS * WIRE // PARTS)):
+        copies.append(pltpu.make_async_copy(source, target, in_sem.at[part]))
         copies[-1].start()
     deep = lax.broadcasted_iota(jnp.int32, (CZ, 128), 0).astype(F32).astype(BF16)
-    for part in range(2):
-        copies[part].wait()
-        if part == 1:
-            bands = [
-                jnp.sum(wire_ref[pl.ds(49 + i, PEERS, stride=WIRE), :], axis=0, keepdims=True) for i in range(GRAM)
-            ]
-            gram = unfolded(jnp.concatenate(bands, axis=0), fold_ref)
-            load_sq = jnp.broadcast_to(gram[48:49, 48:49], (1, 128))
-            row_id = lax.broadcasted_iota(jnp.int32, (K, 128), 0)
-            lane = lax.broadcasted_iota(jnp.int32, (K, 128), 1)
-            raw = jnp.broadcast_to(gram[0:K, K : K + 1], (K, 128))
-            work = jnp.where(lane < K + 1, gram[0:K], jnp.where(lane - 64 == row_id, 1.0, 0.0))
-            for begin in range(0, K, 4):
-                work = swept(work, begin, 4)
-        first = part * half * WIRE
-        labels = wire_ref[pl.ds(first + 48, half, stride=WIRE), :].T[6 * SLOTS : 7 * SLOTS]
-        labels = jnp.concatenate([labels[0:8], labels[8:16]], axis=1).astype(jnp.int32)
-        label_y, label_z = (labels // CZ).astype(F32), (labels % CZ).astype(F32)
-        for i in range(8):
-            here = deep == jnp.broadcast_to(label_z[i : i + 1], (CZ, 128)).astype(BF16)
-            here = chosen(here)
-            row = jnp.broadcast_to(label_y[i : i + 1], (CZ, 128)).astype(BF16)
-            for y in range(CY):
-                t_ref[part, y * CZ : (y + 1) * CZ, i * 128 : (i + 1) * 128] = jnp.where(
-                    row == y, here, jnp.zeros((CZ, 128), BF16)
-                )
-        for tile in range(3):
-            for k in range(SLOTS):
-                high, low = split(wire_ref[pl.ds(first + tile * SLOTS + k, half, stride=WIRE), :])
-                row = k % 8 * 128 + k // 8 * half
-                r_ref[part, tile, row : row + half, 0:128] = high
-                r_ref[part, tile, row : row + half, 128:256] = low
-            moved = half_sum(jnp.dot(t_ref[part], r_ref[part, tile], preferred_element_type=F32))
-            if part == 0:
-                part_ref[tile] = moved
-                continue
-            moved = moved + part_ref[tile]
-            for y in range(CY):
-                main_ref[pl.ds(tile * 128 * CY + y, 128, stride=CY), :] = moved[y * CZ : (y + 1) * CZ].T
+    for copy in copies:
+        copy.wait()
+    bands = [
+        jnp.sum(wire_ref[pl.ds(49 + i, PEERS, stride=WIRE), :], axis=0, keepdims=True) for i in range(GRAM)
+    ]
+    gram = unfolded(jnp.concatenate(bands, axis=0), fold_ref)
+    load_sq = jnp.broadcast_to(gram[48:49, 48:49], (1, 128))
+    row_id = lax.broadcasted_iota(jnp.int32, (K, 128), 0)
+    lane = lax.broadcasted_iota(jnp.int32, (K, 128), 1)
+    raw = jnp.broadcast_to(gram[0:K, K : K + 1], (K, 128))
+    work = jnp.where(lane < K + 1, gram[0:K], jnp.where(lane - 64 == row_id, 1.0, 0.0))
+    for begin in range(0, K, 4):
+        work = swept(work, begin, 4)
     rest = wire_ref[pl.ds(48, PEERS, stride=WIRE), :].T
     labels = rest[6 * SLOTS : 7 * SLOTS]
+    whole = labels.astype(jnp.int32)
+    label_y, label_z = (whole // CZ).astype(F32), (whole % CZ).astype(F32)
+    for k in range(SLOTS):
+        here = chosen(deep == jnp.broadcast_to(label_z[k : k + 1], (CZ, 128)).astype(BF16))
+        row = jnp.broadcast_to(label_y[k : k + 1], (CZ, 128)).astype(BF16)
+        for y in range(CY):
+            t_ref[y * CZ : (y + 1) * CZ, k * 128 : (k + 1) * 128] = jnp.where(
+                row == y, here, jnp.zeros((CZ, 128), BF16)
+            )
+    for tile in range(3):
+        for k in range(SLOTS):
+            high, low = split(wire_ref[pl.ds(tile * SLOTS + k, PEERS, stride=WIRE), :])
+            r_ref[tile, k * 128 : (k + 1) * 128, 0:128] = high
+            r_ref[tile, k * 128 : (k + 1) * 128, 128:256] = low
+        moved = half_sum(jnp.dot(t_ref[...], r_ref[tile], preferred_element_type=F32))
+        for y in range(CY):
+            main_ref[pl.ds(tile * 128 * CY + y, 128, stride=CY), :] = moved[y * CZ : (y + 1) * CZ].T
     [ext] = two_level([(rest[0 : 6 * SLOTS], labels)], left_ref, right_ref)
     ext_ref[...] = ext
 
@@ -538,13 +528,12 @@
         (shape(MAIN * CY, 128), shape(48, 128), plane, shape(K, 128), shape(K, 128), shape(8, 128)),
         [
             vmem((PEERS * WIRE, 128), F32),
-            vmem((2, ROWS, SLOTS * PEERS // 2), BF16),
-            vmem((2, 3, SLOTS * PEERS // 2, 256), BF16),
-            vmem((3, ROWS, 128), F32),
+            vmem((ROWS, SLOTS * PEERS), BF16),
+            vmem((3, SLOTS * PEERS, 256), BF16),
             vmem((48, SLOTS * PEERS), F32),
             vmem((128, SLOTS * PEERS), BF16),
             vmem((56, 128), F32),
-            pltpu.SemaphoreType.DMA((2,)),
+            pltpu.SemaphoreType.DMA((PARTS,)),
         ],
         in_specs=specs(vmem, hbm),
         limit=40,

time: 145 us -> 144 us (level)
  no operation moved by 1% of the time
where the time goes in v5:
time: 144 us; the launch traced here: 142 us
  waiting for transfers between devices  61.6 us (43%)
  blocking collectives  42.7 us (30%)
  starting transfers between devices  19.2 us (13%)
  Pallas kernels  18 us (12%)
    all_to_all x1, waiting for transfers between devices, exchange(): got = lax.all_to_all(shaped, GX_GY, split_axis=0, concat_axis=0, tiled=True)  48.9 us
    all_to_all x3, blocking collectives, exchange(): got = lax.all_to_all(shaped, GX_GY, split_axis=0, concat_axis=0, tiled=True)  42.7 us
    ppermute x4, waiting for transfers between devices, swap(): return lax.ppermute(plane, GX, pairs + [(j, i) for i, j in pairs])  11.6 us
    all_to_all x1, starting transfers between devices, exchange(): got = lax.all_to_all(shaped, GX_GY, split_axis=0, concat_axis=0, tiled=True)  10.9 us
    ppermute x4, starting transfers between devices, swap(): return lax.ppermute(plane, GX, pairs + [(j, i) for i, j in pairs])  8.06 us
    pallas_call x1, Pallas kernels, body(): call(pack_kernel, (shape(PEERS * WIRE, 128), shape(8, ROWS, dtype=jnp.int...  6.92 us
    pallas_call x1, Pallas kernels, body(): call(unpack_kernel, (shape(MAIN * CY, 128), shape(48, 128), plane, shape(...  6.52 us
  transfers between devices with their start and end apart: 7, of which 4 were waited for; matrix products, arithmetic and copies ran while one was open for 0% of the time, Pallas kernels for 0%

profile of v5, /device:TPU:2, one launch (start us, length us, event | category | flops | bytes accessed | tf_op | source)
XLA Modules:
  0.0 142.3 jit_solution(3518803312191186054)
XLA Ops:
  0.6 6.9 %shard_map.68 = (f32[7552,128]{1,0:T(8,128)}, s32[8,1024]{1,0:T(8,128)}) custom-call(f32[243,1024]{1,0:T(8,128)} %op_hbm.1, f32[144,1024]{1,0:T(8,128)} %c_hbm.1, f32[3,1024]{1,0:T(4,128)} %b_hbm.1, s32[1,1024]{1,0:T(1,128)} %bitcast.20), custom_call_target="tpu_custom_call" | custom-call | tf_op jit(solution)/shard_map/pallas_call | solution.py:505
  7.6 10.9 %all-to-all-start = ((f32[128,59,1,128]{3,2,1,0:T(1,128)}), f32[128,59,1,128]{3,2,1,0:T(1,128)}, u32[]{:S(2)}, u32[]{:S(2)}) async-start(f32[128,59,1,128]{3,2,1,0:T(1,128)} %bitcast.19), calls=%async_computation | async-start | bytes 7733248 | tf_op jit(solution)/shard_map/all_to_all | solution.py:488
  18.5 48.9 %all-to-all-done = f32[128,59,1,128]{3,2,1,0:T(1,128)} async-done(((f32[128,59,1,128]{3,2,1,0:T(1,128)}), f32[128,59,1,128]{3,2,1,0:T(1,128)}, u32[]{:S(2)}, u32[]{:S(2)}) %all-to-all-start) | async-done | bytes 3866656 | tf_op jit(solution)/shard_map/all_to_all | solution.py:488
  67.4 0.1 iota.7.place_ref
  67.5 6.5 %shard_map.69 = (f32[3072,128]{1,0:T(8,128)S(1)}, f32[48,128]{1,0:T(8,128)S(1)}, f32[32,128]{1,0:T(8,128)S(1)}, f32[48,128]{1,0:T(8,128)S(1)}, f32[48,128]{1,0:T(8,128)S(1)}, /*index=5*/f32[8,128]{1,0:T(8,128)S(1)}) custom-call(s32[8,128]{1,0:T(8,128)S(1)} %iota.7.place_ref, f32[7552,128]{1,0:T(8,128)} %bitcast.2.wire_hbm), custom_call_target="tpu_custom_call" | custom-call | tf_op jit(solution)/shard_map/pallas_call | solution.py:526
  74.0 0.1 collective-permute-start
  74.1 1.2 collective-permute-done
  75.3 4.0 %collective-permute-start.2 = (f32[32,128]{1,0:T(8,128)S(1)}, f32[32,128]{1,0:T(8,128)S(1)}, u32[]{:S(2)}, u32[]{:S(2)}) collective-permute-start(f32[32,128]{1,0:T(8,128)S(1)} %constant_dynamic-update-slice_fusion.refs_0_.one_ref), channel_id=1, source_target_pairs={{2,4},{6,8},{10,12},{14,16},{18,20},{22,24},{26,28},{30,32},{34,36... | collective-permute-start | bytes 49160 | tf_op jit(solution)/shard_map/ppermute | solution.py:494
  79.3 0.1 collective-permute-start.1
  79.4 5.7 %collective-permute-done.2.second_ref = f32[32,128]{1,0:T(8,128)S(1)} collective-permute-done((f32[32,128]{1,0:T(8,128)S(1)}, f32[32,128]{1,0:T(8,128)S(1)}, u32[]{:S(2)}, u32[]{:S(2)}) %collective-permute-start.2) | collective-permute-done | bytes 16416 | tf_op jit(solution)/shard_map/ppermute | solution.py:494
  85.1 0.0 collective-permute-done.1.first_ref
  85.1 0.4 shard_map.70
  85.6 0.1 collective-permute-start.3
  85.6 14.1 %all_to_all.20 = f32[128,1,1,128]{3,2,1,0:T(1,128)S(1)} all-to-all(f32[128,1,1,128]{3,2,1,0:T(1,128)S(1)} %bitcast.17), channel_id=1, replica_groups=mesh['gx_0'=4,'gx_1'=4,'gx_2'=4,'gy'=2] {'gx_0','gx_1','gx_2','gy'}, dimensions={0} | all-to-all | bytes 131072 | tf_op jit(solution)/shard_map/all_to_all | solution.py:488
  99.7 0.0 collective-permute-done.3.other_ref
  99.7 0.5 shard_map.71
  100.3 3.9 %collective-permute-start.5 = (f32[32,128]{1,0:T(8,128)S(1)}, f32[32,128]{1,0:T(8,128)S(1)}, u32[]{:S(2)}, u32[]{:S(2)}) collective-permute-start(f32[32,128]{1,0:T(8,128)S(1)} %get-tuple-element.28.refs_1_.two_ref), channel_id=1, source_target_pairs={{2,4},{6,8},{10,12},{14,16},{18,20},{22,24},{26,28},{30,32},{34,36... | collective-permute-start | bytes 49160 | tf_op jit(solution)/shard_map/ppermute | solution.py:494
  104.1 0.1 collective-permute-start.4
  104.2 5.9 %collective-permute-done.5.second_ref = f32[32,128]{1,0:T(8,128)S(1)} collective-permute-done((f32[32,128]{1,0:T(8,128)S(1)}, f32[32,128]{1,0:T(8,128)S(1)}, u32[]{:S(2)}, u32[]{:S(2)}) %collective-permute-start.5) | collective-permute-done | bytes 16416 | tf_op jit(solution)/shard_map/ppermute | solution.py:494
  110.1 0.4 shard_map.72
  110.5 14.0 %all_to_all.21 = f32[128,1,1,128]{3,2,1,0:T(1,128)S(1)} all-to-all(f32[128,1,1,128]{3,2,1,0:T(1,128)S(1)} %bitcast.18), channel_id=1, replica_groups=mesh['gx_0'=4,'gx_1'=4,'gx_2'=4,'gy'=2] {'gx_0','gx_1','gx_2','gy'}, dimensions={0} | all-to-all | bytes 131072 | tf_op jit(solution)/shard_map/all_to_all | solution.py:488
  124.5 0.9 shard_map.73
  125.4 14.7 %all_to_all.22 = f32[128,3,1,128]{3,2,1,0:T(1,128)S(1)} all-to-all(f32[128,3,1,128]{3,2,1,0:T(1,128)S(1)} %bitcast.16), channel_id=1, replica_groups=mesh['gx_0'=4,'gx_1'=4,'gx_2'=4,'gy'=2] {'gx_0','gx_1','gx_2','gy'}, dimensions={0} | all-to-all | bytes 393216 | tf_op jit(solution)/shard_map/all_to_all | solution.py:488
  140.1 2.2 %shard_map.74 = (f32[3,1024]{1,0:T(4,128)}, f32[3,1024]{1,0:T(4,128)}) custom-call(s32[8,128]{1,0:T(8,128)S(1)} %iota.7.place_ref, f32[384,128]{1,0:T(8,128)S(1)} %bitcast.13, f32[3072,128]{1,0:T(8,128)S(1)} %get-tuple-element.21.main_ref, f32[48,128]{1,0:T(8,128)S(1)} %get-tuple-element.22.ext_ref, f32[8,128]{1,0:T(8,128)S(1)} %get-tuple-element.36.y_ref, ...), custom_call_target="tpu_custom_call" | custom-call | tf_op jit(solution)/shard_map/pallas_call | solution.py:561
  (8 shorter events, 0.0 us)
Async XLA Ops:
  7.6 59.8 %all-to-all-start = ((f32[128,59,1,128]{3,2,1,0:T(1,128)}), f32[128,59,1,128]{3,2,1,0:T(1,128)}, u32[]{:S(2)}, u32[]{:S(2)}) async-start(f32[128,59,1,128]{3,2,1,0:T(1,128)} %bitcast.19), calls=%async_computation | async-start | bytes 7733248 | tf_op jit(solution)/shard_map/all_to_all | solution.py:488
  67.5 57.0 %copy-start = (f32[144,1024]{1,0:T(8,128)S(1)}, f32[144,1024]{1,0:T(8,128)}, u32[]{:S(2)}) copy-start(f32[144,1024]{1,0:T(8,128)} %u_ref.1) | copy-start | bytes 1769476
  67.5 57.0 %copy-start.1 = (s32[8,1024]{1,0:T(8,128)S(1)}, s32[8,1024]{1,0:T(8,128)}, u32[]{:S(2)}) copy-start(s32[8,1024]{1,0:T(8,128)} %get-tuple-element.34.info_ref) | copy-start | bytes 98308
  74.0 1.2 collective-permute-start
  75.3 9.8 %collective-permute-start.2 = (f32[32,128]{1,0:T(8,128)S(1)}, f32[32,128]{1,0:T(8,128)S(1)}, u32[]{:S(2)}, u32[]{:S(2)}) collective-permute-start(f32[32,128]{1,0:T(8,128)S(1)} %constant_dynamic-update-slice_fusion.refs_0_.one_ref), channel_id=1, source_target_pairs={{2,4},{6,8},{10,12},{14,16},{18,20},{22,24},{26,28},{30,32},{34,36... | collective-permute-start | bytes 49160 | tf_op jit(solution)/shard_map/ppermute | solution.py:494
  79.3 5.8 %collective-permute-start.1 = (f32[32,128]{1,0:T(8,128)S(1)}, f32[32,128]{1,0:T(8,128)S(1)}, u32[]{:S(2)}, u32[]{:S(2)}) collective-permute-start(f32[32,128]{1,0:T(8,128)S(1)} %constant_dynamic-update-slice_fusion.refs_0_.one_ref), channel_id=1, source_target_pairs={{0,2},{4,6},{8,10},{12,14},{16,18},{20,22},{24,26},{28,30},{32,34}... | collective-permute-start | bytes 49160 | tf_op jit(solution)/shard_map/ppermute | solution.py:494
  85.6 14.2 %collective-permute-start.3 = (f32[152,128]{1,0:T(8,128)S(1)}, f32[152,128]{1,0:T(8,128)S(1)}, u32[]{:S(2)}, u32[]{:S(2)}) collective-permute-start(f32[152,128]{1,0:T(8,128)S(1)} %get-tuple-element.26), channel_id=1, source_target_pairs={{0,1},{1,0},{2,3},{3,2},{4,5},{5,4},{6,7},{7,6},{8,9},{9,8},{10,11... | collective-permute-start | bytes 233480 | tf_op jit(solution)/shard_map/ppermute | solution.py:498
  100.3 9.9 %collective-permute-start.5 = (f32[32,128]{1,0:T(8,128)S(1)}, f32[32,128]{1,0:T(8,128)S(1)}, u32[]{:S(2)}, u32[]{:S(2)}) collective-permute-start(f32[32,128]{1,0:T(8,128)S(1)} %get-tuple-element.28.refs_1_.two_ref), channel_id=1, source_target_pairs={{2,4},{6,8},{10,12},{14,16},{18,20},{22,24},{26,28},{30,32},{34,36... | collective-permute-start | bytes 49160 | tf_op jit(solution)/shard_map/ppermute | solution.py:494
  104.1 6.0 %collective-permute-start.4 = (f32[32,128]{1,0:T(8,128)S(1)}, f32[32,128]{1,0:T(8,128)S(1)}, u32[]{:S(2)}, u32[]{:S(2)}) collective-permute-start(f32[32,128]{1,0:T(8,128)S(1)} %get-tuple-element.28.refs_1_.two_ref), channel_id=1, source_target_pairs={{0,2},{4,6},{8,10},{12,14},{16,18},{20,22},{24,26},{28,30},{32,34}... | collective-permute-start | bytes 49160 | tf_op jit(solution)/shard_map/ppermute | solution.py:494

commit v6 on v5

--- a/solution.py
+++ b/solution.py
@@ -23,8 +23,8 @@
 SIDE = K + 1
 BANDS = 25
 GRAM = 10
-WIRE = 49 + GRAM
-PARTS = 1
+HALF = GRAM // 2
+WIRE = 49 + HALF
 CHUNKS = 8
 NT = (((1,), (1,)), ((), ()))
 TN = (((0,), (0,)), ((), ()))
@@ -135,11 +135,13 @@
     info_ref[1:2, :] = rank.astype(jnp.int32)
     info_ref[2:3, :] = local
     info_ref[3:8, :] = jnp.zeros((5, ROWS), jnp.int32)
-    for copy in copies[1:]:
+    for copy in copies[1:4]:
         copy.wait()
-    middle = jnp.concatenate([c_ref[128:144, :], op_ref[0:112, :]], axis=0)
-    for tile, x in enumerate((c_ref[0:128, :], middle, op_ref[112:240, :])):
+
+    def put(tile, x):
         p_ref[:, tile * 256 : tile * 256 + 128], p_ref[:, tile * 256 + 128 : (tile + 1) * 256] = split(x.T)
+
+    put(0, c_ref[0:128, :])
     sums, low = jnp.zeros((192, 64), F32), jnp.zeros((64, 64), F32)
     for a in range(3):
         a_ref[a, 48:64, :] = jnp.zeros((16, ROWS), F32)
@@ -153,9 +155,15 @@
     cross = squared(sums[64:128] + sums[128:192])
     gram = squared(sums[0:64] + low) + cross + cross.T
     bands = folded(gram[0:64], fold_ref)
-    for i in range(GRAM):
-        wire_ref[pl.ds(49 + i, PEERS, stride=WIRE), :] = jnp.broadcast_to(bands[i : i + 1, :], (PEERS, 128))
-
+    second = lax.broadcasted_iota(jnp.int32, (PEERS, 128), 0) % 2 == 1
+    for i in range(HALF):
+        wire_ref[pl.ds(49 + i, PEERS, stride=WIRE), :] = jnp.where(
+            second, bands[HALF + i : HALF + i + 1, :], bands[i : i + 1, :]
+        )
+    for copy in copies[4:]:
+        copy.wait()
+    put(1, jnp.concatenate([c_ref[128:144, :], op_ref[0:112, :]], axis=0))
+    put(2, op_ref[112:240, :])
     at_rank = lax.broadcasted_iota(jnp.int32, (SLOTS, ROWS), 0).astype(F32) == rank
     rest = [op_ref[240 + i : 241 + i, :] for i in range(3)] + [b_ref[i : i + 1, :] for i in range(3)]
     rest = [jnp.where(at_rank, row, 0.0) for row in rest + [local.astype(F32)]]
@@ -244,20 +252,14 @@
 
 
 def unpack_kernel(
-    place_ref, wire_hbm, main_ref, ext_ref, v_ref, inv_ref, start_ref, beta_ref,
-    wire_ref, t_ref, r_ref, left_ref, right_ref, fold_ref, in_sem,
+    place_ref, wire_ref, mine_ref, other_ref, main_ref, ext_ref, v_ref, inv_ref, start_ref, beta_ref,
+    t_ref, r_ref, left_ref, right_ref, fold_ref,
 ):
-    copies = []
-    for part, (source, target) in enumerate(pieces(wire_hbm, wire_ref, PEERS * WIRE // PARTS)):
-        copies.append(pltpu.make_async_copy(source, target, in_sem.at[part]))
-        copies[-1].start()
     deep = lax.broadcasted_iota(jnp.int32, (CZ, 128), 0).astype(F32).astype(BF16)
-    for copy in copies:
-        copy.wait()
-    bands = [
-        jnp.sum(wire_ref[pl.ds(49 + i, PEERS, stride=WIRE), :], axis=0, keepdims=True) for i in range(GRAM)
-    ]
-    gram = unfolded(jnp.concatenate(bands, axis=0), fold_ref)
+    lower = place_ref[0:1, :] == 0
+    mine, other = mine_ref[0:HALF, :], other_ref[0:HALF, :]
+    bands = jnp.concatenate([jnp.where(lower, mine, other), jnp.where(lower, other, mine)], axis=0)
+    gram = unfolded(bands, fold_ref)
     load_sq = jnp.broadcast_to(gram[48:49, 48:49], (1, 128))
     row_id = lax.broadcasted_iota(jnp.int32, (K, 128), 0)
     lane = lax.broadcasted_iota(jnp.int32, (K, 128), 1)
@@ -295,7 +297,6 @@
     beta_ref[...] = jnp.broadcast_to(beta, (8, 128))
     load = [ext[24 + a * CY : 24 + (a + 1) * CY, :] for a in range(3)]
     vector = [v / beta for v in minus_combined(load, main_ref, weights)]
-    lower = place_ref[0:1, :] == 0
     put_vector(vector, [jnp.where(lower, v[CY - 1 : CY], v[0:1]) for v in vector], v_ref)
 
 
@@ -522,22 +523,20 @@
         limit=56,
     )(operator, basis_c, right_side, new_rows.reshape(1, ROWS))
     got = exchange(wire)
+    mine = jnp.sum(got.reshape(PEERS, WIRE, 128)[:, 49:], axis=0)
     plane = shape(32, 128)
     main, ext, one, inverse, start, beta = call(
         unpack_kernel,
         (shape(MAIN * CY, 128), shape(48, 128), plane, shape(K, 128), shape(K, 128), shape(8, 128)),
         [
-            vmem((PEERS * WIRE, 128), F32),
             vmem((ROWS, SLOTS * PEERS), BF16),
             vmem((3, SLOTS * PEERS, 256), BF16),
             vmem((48, SLOTS * PEERS), F32),
             vmem((128, SLOTS * PEERS), BF16),
             vmem((56, 128), F32),
-            pltpu.SemaphoreType.DMA((PARTS,)),
         ],
-        in_specs=specs(vmem, hbm),
-        limit=40,
-    )(place, got)
+        inputs=4,
+    )(place, got, mine, other_core(mine))
     pad = vmem((9 * 24, 128), F32)
     image_scratch = [pad, vmem(((K + 8) * CY, 128), F32)]
     image_outs = (shape(3 * CY, 128), shape(PEERS, 128))

time: 144 us -> 141 us (0.979)
  waiting for transfers between devices: 61.6 us -> 59.5 us
    all_to_all x1, waiting for transfers between devices: 48.9 us -> 45.7 us  [exchange(): got = lax.all_to_all(shaped, GX_GY, split_axis=0, concat_axis=0, tiled=True)]
    pallas_call x1, Pallas kernels: 6.52 us -> 4.33 us  [body(): call(unpack_kernel, (shape(MAIN * CY, 128), shape(48, 128), plane, shape(...]
  transfers between devices with their start and end apart: 7 -> 8, of which waited for: 4 -> 5; matrix products, arithmetic and copies ran while one was open for 0% -> 0% of each run, Pallas kernels for 0% -> 0%
where the time goes in v6:
time: 141 us; the launch traced here: 139 us
  waiting for transfers between devices  59.5 us (42%)
  blocking collectives  42.9 us (30%)
  starting transfers between devices  19 us (13%)
  Pallas kernels  16.6 us (12%)
    all_to_all x1, waiting for transfers between devices, exchange(): got = lax.all_to_all(shaped, GX_GY, split_axis=0, concat_axis=0, tiled=True)  45.7 us
    all_to_all x3, blocking collectives, exchange(): got = lax.all_to_all(shaped, GX_GY, split_axis=0, concat_axis=0, tiled=True)  42.9 us
    ppermute x4, waiting for transfers between devices, swap(): return lax.ppermute(plane, GX, pairs + [(j, i) for i, j in pairs])  11.7 us
    all_to_all x1, starting transfers between devices, exchange(): got = lax.all_to_all(shaped, GX_GY, split_axis=0, concat_axis=0, tiled=True)  10.5 us
    ppermute x4, starting transfers between devices, swap(): return lax.ppermute(plane, GX, pairs + [(j, i) for i, j in pairs])  8.01 us
    pallas_call x1, Pallas kernels, body(): call(pack_kernel, (shape(PEERS * WIRE, 128), shape(8, ROWS, dtype=jnp.int...  7.71 us
    pallas_call x1, Pallas kernels, body(): call(unpack_kernel, (shape(MAIN * CY, 128), shape(48, 128), plane, shape(...  4.33 us
  transfers between devices with their start and end apart: 8, of which 5 were waited for; matrix products, arithmetic and copies ran while one was open for 0% of the time, Pallas kernels for 0%

profile of v6, /device:TPU:2, one launch (start us, length us, event | category | flops | bytes accessed | tf_op | source)
XLA Modules:
  0.0 139.2 jit_solution(4579929971908299711)
XLA Ops:
  0.6 7.7 %shard_map.68 = (f32[6912,128]{1,0:T(8,128)}, s32[8,1024]{1,0:T(8,128)}) custom-call(f32[243,1024]{1,0:T(8,128)} %op_hbm.1, f32[144,1024]{1,0:T(8,128)} %c_hbm.1, f32[3,1024]{1,0:T(4,128)} %b_hbm.1, s32[1,1024]{1,0:T(1,128)} %bitcast.25), custom_call_target="tpu_custom_call" | custom-call | tf_op jit(solution)/shard_map/pallas_call | solution.py:506
  8.3 10.5 %all-to-all-start = ((f32[128,54,1,128]{3,2,1,0:T(1,128)}), f32[128,54,1,128]{3,2,1,0:T(1,128)S(1)}, u32[]{:S(2)}, u32[]{:S(2)}) async-start(f32[128,54,1,128]{3,2,1,0:T(1,128)} %bitcast.24), calls=%async_computation | async-start | bytes 7077888 | tf_op jit(solution)/shard_map/all_to_all | solution.py:489
  18.9 45.7 %all-to-all-done = f32[128,54,1,128]{3,2,1,0:T(1,128)S(1)} async-done(((f32[128,54,1,128]{3,2,1,0:T(1,128)}), f32[128,54,1,128]{3,2,1,0:T(1,128)S(1)}, u32[]{:S(2)}, u32[]{:S(2)}) %all-to-all-start) | async-done | bytes 3538976 | tf_op jit(solution)/shard_map/all_to_all | solution.py:489
  64.6 0.5 copy.17
  65.1 0.1 collective-permute-start
  65.2 1.1 collective-permute-done.other_ref
  66.4 4.3 %shard_map.69 = (f32[3072,128]{1,0:T(8,128)S(1)}, f32[48,128]{1,0:T(8,128)S(1)}, f32[32,128]{1,0:T(8,128)S(1)}, f32[48,128]{1,0:T(8,128)S(1)}, f32[48,128]{1,0:T(8,128)S(1)}, /*index=5*/f32[8,128]{1,0:T(8,128)S(1)}) custom-call(s32[8,128]{1,0:T(8,128)S(1)} %iota.7.place_ref, f32[6912,128]{1,0:T(8,128)S(1)} %bitcast.16, ...), custom_call_target="tpu_custom_call" | custom-call | tf_op jit(solution)/shard_map/pallas_call | solution.py:528
  70.8 0.2 collective-permute-start.1
  71.0 1.0 collective-permute-done.1
  72.0 3.8 %collective-permute-start.3 = (f32[32,128]{1,0:T(8,128)S(1)}, f32[32,128]{1,0:T(8,128)S(1)}, u32[]{:S(2)}, u32[]{:S(2)}) collective-permute-start(f32[32,128]{1,0:T(8,128)S(1)} %constant_dynamic-update-slice_fusion.refs_0_.one_ref), channel_id=1, source_target_pairs={{2,4},{6,8},{10,12},{14,16},{18,20},{22,24},{26,28},{30,32},{34,36... | collective-permute-start | bytes 49160 | tf_op jit(solution)/shard_map/ppermute | solution.py:495
  75.8 0.1 collective-permute-start.2
  75.9 6.0 %collective-permute-done.3.second_ref = f32[32,128]{1,0:T(8,128)S(1)} collective-permute-done((f32[32,128]{1,0:T(8,128)S(1)}, f32[32,128]{1,0:T(8,128)S(1)}, u32[]{:S(2)}, u32[]{:S(2)}) %collective-permute-start.3) | collective-permute-done | bytes 16416 | tf_op jit(solution)/shard_map/ppermute | solution.py:495
  81.8 0.4 shard_map.70
  82.3 0.1 collective-permute-start.4
  82.4 14.1 %all_to_all.20 = f32[128,1,1,128]{3,2,1,0:T(1,128)S(1)} all-to-all(f32[128,1,1,128]{3,2,1,0:T(1,128)S(1)} %bitcast.21), channel_id=1, replica_groups=mesh['gx_0'=4,'gx_1'=4,'gx_2'=4,'gy'=2] {'gx_0','gx_1','gx_2','gy'}, dimensions={0} | all-to-all | bytes 131072 | tf_op jit(solution)/shard_map/all_to_all | solution.py:489
  96.5 0.5 shard_map.71
  97.0 3.9 %collective-permute-start.6 = (f32[32,128]{1,0:T(8,128)S(1)}, f32[32,128]{1,0:T(8,128)S(1)}, u32[]{:S(2)}, u32[]{:S(2)}) collective-permute-start(f32[32,128]{1,0:T(8,128)S(1)} %get-tuple-element.28.refs_1_.two_ref), channel_id=1, source_target_pairs={{2,4},{6,8},{10,12},{14,16},{18,20},{22,24},{26,28},{30,32},{34,36... | collective-permute-start | bytes 49160 | tf_op jit(solution)/shard_map/ppermute | solution.py:495
  100.9 0.3 collective-permute-start.5
  101.2 5.7 %collective-permute-done.6.second_ref = f32[32,128]{1,0:T(8,128)S(1)} collective-permute-done((f32[32,128]{1,0:T(8,128)S(1)}, f32[32,128]{1,0:T(8,128)S(1)}, u32[]{:S(2)}, u32[]{:S(2)}) %collective-permute-start.6) | collective-permute-done | bytes 16416 | tf_op jit(solution)/shard_map/ppermute | solution.py:495
  106.9 0.4 shard_map.72
  107.3 14.1 %all_to_all.21 = f32[128,1,1,128]{3,2,1,0:T(1,128)S(1)} all-to-all(f32[128,1,1,128]{3,2,1,0:T(1,128)S(1)} %bitcast.22), channel_id=1, replica_groups=mesh['gx_0'=4,'gx_1'=4,'gx_2'=4,'gy'=2] {'gx_0','gx_1','gx_2','gy'}, dimensions={0} | all-to-all | bytes 131072 | tf_op jit(solution)/shard_map/all_to_all | solution.py:489
  121.4 0.9 shard_map.73
  122.4 14.7 %all_to_all.22 = f32[128,3,1,128]{3,2,1,0:T(1,128)S(1)} all-to-all(f32[128,3,1,128]{3,2,1,0:T(1,128)S(1)} %bitcast.20), channel_id=1, replica_groups=mesh['gx_0'=4,'gx_1'=4,'gx_2'=4,'gy'=2] {'gx_0','gx_1','gx_2','gy'}, dimensions={0} | all-to-all | bytes 393216 | tf_op jit(solution)/shard_map/all_to_all | solution.py:489
  137.0 2.2 %shard_map.74 = (f32[3,1024]{1,0:T(4,128)}, f32[3,1024]{1,0:T(4,128)}) custom-call(s32[8,128]{1,0:T(8,128)S(1)} %iota.7.place_ref, f32[384,128]{1,0:T(8,128)S(1)} %bitcast.17, f32[3072,128]{1,0:T(8,128)S(1)} %get-tuple-element.21.main_ref, f32[48,128]{1,0:T(8,128)S(1)} %get-tuple-element.22.ext_ref, f32[8,128]{1,0:T(8,128)S(1)} %get-tuple-element.36.y_ref, ...), custom_call_target="tpu_custom_call" | custom-call | tf_op jit(solution)/shard_map/pallas_call | solution.py:560
  (12 shorter events, 0.1 us)
Async XLA Ops:
  8.3 56.2 %all-to-all-start = ((f32[128,54,1,128]{3,2,1,0:T(1,128)}), f32[128,54,1,128]{3,2,1,0:T(1,128)S(1)}, u32[]{:S(2)}, u32[]{:S(2)}) async-start(f32[128,54,1,128]{3,2,1,0:T(1,128)} %bitcast.24), calls=%async_computation | async-start | bytes 7077888 | tf_op jit(solution)/shard_map/all_to_all | solution.py:489
  65.1 1.2 collective-permute-start
  70.7 50.7 %copy-start = (f32[144,1024]{1,0:T(8,128)S(1)}, f32[144,1024]{1,0:T(8,128)}, u32[]{:S(2)}) copy-start(f32[144,1024]{1,0:T(8,128)} %u_ref.1) | copy-start | bytes 1769476
  70.7 50.7 %copy-start.1 = (s32[8,1024]{1,0:T(8,128)S(1)}, s32[8,1024]{1,0:T(8,128)}, u32[]{:S(2)}) copy-start(s32[8,1024]{1,0:T(8,128)} %get-tuple-element.34.info_ref) | copy-start | bytes 98308
  70.8 1.2 collective-permute-start.1
  72.0 9.8 %collective-permute-start.3 = (f32[32,128]{1,0:T(8,128)S(1)}, f32[32,128]{1,0:T(8,128)S(1)}, u32[]{:S(2)}, u32[]{:S(2)}) collective-permute-start(f32[32,128]{1,0:T(8,128)S(1)} %constant_dynamic-update-slice_fusion.refs_0_.one_ref), channel_id=1, source_target_pairs={{2,4},{6,8},{10,12},{14,16},{18,20},{22,24},{26,28},{30,32},{34,36... | collective-permute-start | bytes 49160 | tf_op jit(solution)/shard_map/ppermute | solution.py:495
  75.8 6.1 %collective-permute-start.2 = (f32[32,128]{1,0:T(8,128)S(1)}, f32[32,128]{1,0:T(8,128)S(1)}, u32[]{:S(2)}, u32[]{:S(2)}) collective-permute-start(f32[32,128]{1,0:T(8,128)S(1)} %constant_dynamic-update-slice_fusion.refs_0_.one_ref), channel_id=1, source_target_pairs={{0,2},{4,6},{8,10},{12,14},{16,18},{20,22},{24,26},{28,30},{32,34}... | collective-permute-start | bytes 49160 | tf_op jit(solution)/shard_map/ppermute | solution.py:495
  82.3 14.2 %collective-permute-start.4 = (f32[152,128]{1,0:T(8,128)S(1)}, f32[152,128]{1,0:T(8,128)S(1)}, u32[]{:S(2)}, u32[]{:S(2)}) collective-permute-start(f32[152,128]{1,0:T(8,128)S(1)} %get-tuple-element.26), channel_id=1, source_target_pairs={{0,1},{1,0},{2,3},{3,2},{4,5},{5,4},{6,7},{7,6},{8,9},{9,8},{10,11... | collective-permute-start | bytes 233480 | tf_op jit(solution)/shard_map/ppermute | solution.py:499
  97.0 9.9 %collective-permute-start.6 = (f32[32,128]{1,0:T(8,128)S(1)}, f32[32,128]{1,0:T(8,128)S(1)}, u32[]{:S(2)}, u32[]{:S(2)}) collective-permute-start(f32[32,128]{1,0:T(8,128)S(1)} %get-tuple-element.28.refs_1_.two_ref), channel_id=1, source_target_pairs={{2,4},{6,8},{10,12},{14,16},{18,20},{22,24},{26,28},{30,32},{34,36... | collective-permute-start | bytes 49160 | tf_op jit(solution)/shard_map/ppermute | solution.py:495
  100.9 6.0 %collective-permute-start.5 = (f32[32,128]{1,0:T(8,128)S(1)}, f32[32,128]{1,0:T(8,128)S(1)}, u32[]{:S(2)}, u32[]{:S(2)}) collective-permute-start(f32[32,128]{1,0:T(8,128)S(1)} %get-tuple-element.28.refs_1_.two_ref), channel_id=1, source_target_pairs={{0,2},{4,6},{8,10},{12,14},{16,18},{20,22},{24,26},{28,30},{32,34}... | collective-permute-start | bytes 49160 | tf_op jit(solution)/shard_map/ppermute | solution.py:495

commit v7 on v6

--- a/solution.py
+++ b/solution.py
@@ -135,13 +135,15 @@
     info_ref[1:2, :] = rank.astype(jnp.int32)
     info_ref[2:3, :] = local
     info_ref[3:8, :] = jnp.zeros((5, ROWS), jnp.int32)
-    for copy in copies[1:4]:
+    for copy in copies[1:]:
         copy.wait()
 
     def put(tile, x):
         p_ref[:, tile * 256 : tile * 256 + 128], p_ref[:, tile * 256 + 128 : (tile + 1) * 256] = split(x.T)
 
     put(0, c_ref[0:128, :])
+    put(1, jnp.concatenate([c_ref[128:144, :], op_ref[0:112, :]], axis=0))
+    put(2, op_ref[112:240, :])
     sums, low = jnp.zeros((192, 64), F32), jnp.zeros((64, 64), F32)
     for a in range(3):
         a_ref[a, 48:64, :] = jnp.zeros((16, ROWS), F32)
@@ -160,10 +162,6 @@
         wire_ref[pl.ds(49 + i, PEERS, stride=WIRE), :] = jnp.where(
             second, bands[HALF + i : HALF + i + 1, :], bands[i : i + 1, :]
         )
-    for copy in copies[4:]:
-        copy.wait()
-    put(1, jnp.concatenate([c_ref[128:144, :], op_ref[0:112, :]], axis=0))
-    put(2, op_ref[112:240, :])
     at_rank = lax.broadcasted_iota(jnp.int32, (SLOTS, ROWS), 0).astype(F32) == rank
     rest = [op_ref[240 + i : 241 + i, :] for i in range(3)] + [b_ref[i : i + 1, :] for i in range(3)]
     rest = [jnp.where(at_rank, row, 0.0) for row in rest + [local.astype(F32)]]
@@ -267,7 +265,7 @@
     work = jnp.where(lane < K + 1, gram[0:K], jnp.where(lane - 64 == row_id, 1.0, 0.0))
     for begin in range(0, K, 4):
         work = swept(work, begin, 4)
-    rest = wire_ref[pl.ds(48, PEERS, stride=WIRE), :].T
+    rest = wire_ref[48].T
     labels = rest[6 * SLOTS : 7 * SLOTS]
     whole = labels.astype(jnp.int32)
     label_y, label_z = (whole // CZ).astype(F32), (whole % CZ).astype(F32)
@@ -280,7 +278,7 @@
             )
     for tile in range(3):
         for k in range(SLOTS):
-            high, low = split(wire_ref[pl.ds(tile * SLOTS + k, PEERS, stride=WIRE), :])
+            high, low = split(wire_ref[tile * SLOTS + k])
             r_ref[tile, k * 128 : (k + 1) * 128, 0:128] = high
             r_ref[tile, k * 128 : (k + 1) * 128, 128:256] = low
         moved = half_sum(jnp.dot(t_ref[...], r_ref[tile], preferred_element_type=F32))
@@ -523,7 +521,8 @@
         limit=56,
     )(operator, basis_c, right_side, new_rows.reshape(1, ROWS))
     got = exchange(wire)
-    mine = jnp.sum(got.reshape(PEERS, WIRE, 128)[:, 49:], axis=0)
+    got = got.reshape(PEERS, WIRE, 128).transpose(1, 0, 2)
+    mine = jnp.sum(got[49:], axis=1)
     plane = shape(32, 128)
     main, ext, one, inverse, start, beta = call(
         unpack_kernel,

time: 141 us -> 140 us (level)
  no operation moved by 1% of the time
where the time goes in v7:
time: 140 us; the launch traced here: 138 us
  waiting for transfers between devices  59.6 us (43%)
  blocking collectives  42.7 us (30%)
  starting transfers between devices  18.8 us (13%)
  Pallas kernels  15.7 us (11%)
    all_to_all x1, waiting for transfers between devices, exchange(): got = lax.all_to_all(shaped, GX_GY, split_axis=0, concat_axis=0, tiled=True)  45.7 us
    all_to_all x3, blocking collectives, exchange(): got = lax.all_to_all(shaped, GX_GY, split_axis=0, concat_axis=0, tiled=True)  42.7 us
    ppermute x4, waiting for transfers between devices, swap(): return lax.ppermute(plane, GX, pairs + [(j, i) for i, j in pairs])  11.8 us
    all_to_all x1, starting transfers between devices, exchange(): got = lax.all_to_all(shaped, GX_GY, split_axis=0, concat_axis=0, tiled=True)  10.5 us
    ppermute x4, starting transfers between devices, swap(): return lax.ppermute(plane, GX, pairs + [(j, i) for i, j in pairs])  7.83 us
    pallas_call x1, Pallas kernels, body(): call(pack_kernel, (shape(PEERS * WIRE, 128), shape(8, ROWS, dtype=jnp.int...  6.89 us
    pallas_call x1, Pallas kernels, body(): call(unpack_kernel, (shape(MAIN * CY, 128), shape(48, 128), plane, shape(...  4.31 us
  transfers between devices with their start and end apart: 8, of which 5 were waited for; matrix products, arithmetic and copies ran while one was open for 0% of the time, Pallas kernels for 0%

profile of v7, /device:TPU:2, one launch (start us, length us, event | category | flops | bytes accessed | tf_op | source)
XLA Modules:
  0.0 138.2 jit_solution(6165498804439382260)
XLA Ops:
  0.6 6.9 %shard_map.68 = (f32[6912,128]{1,0:T(8,128)}, s32[8,1024]{1,0:T(8,128)}) custom-call(f32[243,1024]{1,0:T(8,128)} %op_hbm.1, f32[144,1024]{1,0:T(8,128)} %c_hbm.1, f32[3,1024]{1,0:T(4,128)} %b_hbm.1, s32[1,1024]{1,0:T(1,128)} %bitcast.26), custom_call_target="tpu_custom_call" | custom-call | tf_op jit(solution)/shard_map/pallas_call | solution.py:504
  7.5 10.5 %all-to-all-start = ((f32[128,54,1,128]{3,2,1,0:T(1,128)}), f32[128,54,1,128]{3,2,1,0:T(1,128)S(1)}, u32[]{:S(2)}, u32[]{:S(2)}) async-start(f32[128,54,1,128]{3,2,1,0:T(1,128)} %bitcast.25), calls=%async_computation | async-start | bytes 7077888 | tf_op jit(solution)/shard_map/all_to_all | solution.py:487
  18.1 45.7 %all-to-all-done = f32[128,54,1,128]{3,2,1,0:T(1,128)S(1)} async-done(((f32[128,54,1,128]{3,2,1,0:T(1,128)}), f32[128,54,1,128]{3,2,1,0:T(1,128)S(1)}, u32[]{:S(2)}, u32[]{:S(2)}) %all-to-all-start) | async-done | bytes 3538976 | tf_op jit(solution)/shard_map/all_to_all | solution.py:487
  63.7 0.5 copy.19
  64.3 0.1 collective-permute-start
  64.4 1.1 collective-permute-done.other_ref
  65.6 4.3 %shard_map.69 = (f32[3072,128]{1,0:T(8,128)S(1)}, f32[48,128]{1,0:T(8,128)S(1)}, f32[32,128]{1,0:T(8,128)S(1)}, f32[48,128]{1,0:T(8,128)S(1)}, f32[48,128]{1,0:T(8,128)S(1)}, /*index=5*/f32[8,128]{1,0:T(8,128)S(1)}) custom-call(s32[8,128]{1,0:T(8,128)S(1)} %iota.7.place_ref, f32[54,128,128]{2,1,0:T(8,128)S(1)} %bitcast.18, ...), custom_call_target="tpu_custom_call" | custom-call | tf_op jit(solution)/shard_map/pallas_call | solution.py:527
  69.9 0.2 collective-permute-start.1
  70.2 1.0 collective-permute-done.1
  71.2 3.8 %collective-permute-start.3 = (f32[32,128]{1,0:T(8,128)S(1)}, f32[32,128]{1,0:T(8,128)S(1)}, u32[]{:S(2)}, u32[]{:S(2)}) collective-permute-start(f32[32,128]{1,0:T(8,128)S(1)} %constant_dynamic-update-slice_fusion.refs_0_.one_ref), channel_id=1, source_target_pairs={{2,4},{6,8},{10,12},{14,16},{18,20},{22,24},{26,28},{30,32},{34,36... | collective-permute-start | bytes 49160 | tf_op jit(solution)/shard_map/ppermute | solution.py:493
  74.9 0.1 collective-permute-start.2
  75.0 6.0 %collective-permute-done.3.second_ref = f32[32,128]{1,0:T(8,128)S(1)} collective-permute-done((f32[32,128]{1,0:T(8,128)S(1)}, f32[32,128]{1,0:T(8,128)S(1)}, u32[]{:S(2)}, u32[]{:S(2)}) %collective-permute-start.3) | collective-permute-done | bytes 16416 | tf_op jit(solution)/shard_map/ppermute | solution.py:493
  81.0 0.4 shard_map.70
  81.5 0.1 collective-permute-start.4
  81.6 14.1 %all_to_all.20 = f32[128,1,1,128]{3,2,1,0:T(1,128)S(1)} all-to-all(f32[128,1,1,128]{3,2,1,0:T(1,128)S(1)} %bitcast.23), channel_id=1, replica_groups=mesh['gx_0'=4,'gx_1'=4,'gx_2'=4,'gy'=2] {'gx_0','gx_1','gx_2','gy'}, dimensions={0} | all-to-all | bytes 131072 | tf_op jit(solution)/shard_map/all_to_all | solution.py:487
  95.6 0.5 shard_map.71
  96.2 3.9 %collective-permute-start.6 = (f32[32,128]{1,0:T(8,128)S(1)}, f32[32,128]{1,0:T(8,128)S(1)}, u32[]{:S(2)}, u32[]{:S(2)}) collective-permute-start(f32[32,128]{1,0:T(8,128)S(1)} %get-tuple-element.28.refs_1_.two_ref), channel_id=1, source_target_pairs={{2,4},{6,8},{10,12},{14,16},{18,20},{22,24},{26,28},{30,32},{34,36... | collective-permute-start | bytes 49160 | tf_op jit(solution)/shard_map/ppermute | solution.py:493
  100.1 0.1 collective-permute-start.5
  100.1 5.9 %collective-permute-done.6.second_ref = f32[32,128]{1,0:T(8,128)S(1)} collective-permute-done((f32[32,128]{1,0:T(8,128)S(1)}, f32[32,128]{1,0:T(8,128)S(1)}, u32[]{:S(2)}, u32[]{:S(2)}) %collective-permute-start.6) | collective-permute-done | bytes 16416 | tf_op jit(solution)/shard_map/ppermute | solution.py:493
  106.0 0.4 shard_map.72
  106.4 14.0 %all_to_all.21 = f32[128,1,1,128]{3,2,1,0:T(1,128)S(1)} all-to-all(f32[128,1,1,128]{3,2,1,0:T(1,128)S(1)} %bitcast.24), channel_id=1, replica_groups=mesh['gx_0'=4,'gx_1'=4,'gx_2'=4,'gy'=2] {'gx_0','gx_1','gx_2','gy'}, dimensions={0} | all-to-all | bytes 131072 | tf_op jit(solution)/shard_map/all_to_all | solution.py:487
  120.4 0.9 shard_map.73
  121.3 14.7 %all_to_all.22 = f32[128,3,1,128]{3,2,1,0:T(1,128)S(1)} all-to-all(f32[128,3,1,128]{3,2,1,0:T(1,128)S(1)} %bitcast.22), channel_id=1, replica_groups=mesh['gx_0'=4,'gx_1'=4,'gx_2'=4,'gy'=2] {'gx_0','gx_1','gx_2','gy'}, dimensions={0} | all-to-all | bytes 393216 | tf_op jit(solution)/shard_map/all_to_all | solution.py:487
  136.0 2.2 %shard_map.74 = (f32[3,1024]{1,0:T(4,128)}, f32[3,1024]{1,0:T(4,128)}) custom-call(s32[8,128]{1,0:T(8,128)S(1)} %iota.7.place_ref, f32[384,128]{1,0:T(8,128)S(1)} %bitcast.19, f32[3072,128]{1,0:T(8,128)S(1)} %get-tuple-element.21.main_ref, f32[48,128]{1,0:T(8,128)S(1)} %get-tuple-element.22.ext_ref, f32[8,128]{1,0:T(8,128)S(1)} %get-tuple-element.36.y_ref, ...), custom_call_target="tpu_custom_call" | custom-call | tf_op jit(solution)/shard_map/pallas_call | solution.py:559
  (12 shorter events, 0.1 us)
Async XLA Ops:
  7.5 56.2 %all-to-all-start = ((f32[128,54,1,128]{3,2,1,0:T(1,128)}), f32[128,54,1,128]{3,2,1,0:T(1,128)S(1)}, u32[]{:S(2)}, u32[]{:S(2)}) async-start(f32[128,54,1,128]{3,2,1,0:T(1,128)} %bitcast.25), calls=%async_computation | async-start | bytes 7077888 | tf_op jit(solution)/shard_map/all_to_all | solution.py:487
  64.3 1.2 collective-permute-start
  69.9 50.5 %copy-start = (f32[144,1024]{1,0:T(8,128)S(1)}, f32[144,1024]{1,0:T(8,128)}, u32[]{:S(2)}) copy-start(f32[144,1024]{1,0:T(8,128)} %u_ref.1) | copy-start | bytes 1769476
  69.9 50.5 %copy-start.1 = (s32[8,1024]{1,0:T(8,128)S(1)}, s32[8,1024]{1,0:T(8,128)}, u32[]{:S(2)}) copy-start(s32[8,1024]{1,0:T(8,128)} %get-tuple-element.34.info_ref) | copy-start | bytes 98308
  69.9 1.2 collective-permute-start.1
  71.2 9.8 %collective-permute-start.3 = (f32[32,128]{1,0:T(8,128)S(1)}, f32[32,128]{1,0:T(8,128)S(1)}, u32[]{:S(2)}, u32[]{:S(2)}) collective-permute-start(f32[32,128]{1,0:T(8,128)S(1)} %constant_dynamic-update-slice_fusion.refs_0_.one_ref), channel_id=1, source_target_pairs={{2,4},{6,8},{10,12},{14,16},{18,20},{22,24},{26,28},{30,32},{34,36... | collective-permute-start | bytes 49160 | tf_op jit(solution)/shard_map/ppermute | solution.py:493
  74.9 6.1 %collective-permute-start.2 = (f32[32,128]{1,0:T(8,128)S(1)}, f32[32,128]{1,0:T(8,128)S(1)}, u32[]{:S(2)}, u32[]{:S(2)}) collective-permute-start(f32[32,128]{1,0:T(8,128)S(1)} %constant_dynamic-update-slice_fusion.refs_0_.one_ref), channel_id=1, source_target_pairs={{0,2},{4,6},{8,10},{12,14},{16,18},{20,22},{24,26},{28,30},{32,34}... | collective-permute-start | bytes 49160 | tf_op jit(solution)/shard_map/ppermute | solution.py:493
  81.5 14.2 %collective-permute-start.4 = (f32[152,128]{1,0:T(8,128)S(1)}, f32[152,128]{1,0:T(8,128)S(1)}, u32[]{:S(2)}, u32[]{:S(2)}) collective-permute-start(f32[152,128]{1,0:T(8,128)S(1)} %get-tuple-element.26), channel_id=1, source_target_pairs={{0,1},{1,0},{2,3},{3,2},{4,5},{5,4},{6,7},{7,6},{8,9},{9,8},{10,11... | collective-permute-start | bytes 233480 | tf_op jit(solution)/shard_map/ppermute | solution.py:497
  96.2 9.9 %collective-permute-start.6 = (f32[32,128]{1,0:T(8,128)S(1)}, f32[32,128]{1,0:T(8,128)S(1)}, u32[]{:S(2)}, u32[]{:S(2)}) collective-permute-start(f32[32,128]{1,0:T(8,128)S(1)} %get-tuple-element.28.refs_1_.two_ref), channel_id=1, source_target_pairs={{2,4},{6,8},{10,12},{14,16},{18,20},{22,24},{26,28},{30,32},{34,36... | collective-permute-start | bytes 49160 | tf_op jit(solution)/shard_map/ppermute | solution.py:493
  100.1 6.0 %collective-permute-start.5 = (f32[32,128]{1,0:T(8,128)S(1)}, f32[32,128]{1,0:T(8,128)S(1)}, u32[]{:S(2)}, u32[]{:S(2)}) collective-permute-start(f32[32,128]{1,0:T(8,128)S(1)} %get-tuple-element.28.refs_1_.two_ref), channel_id=1, source_target_pairs={{0,2},{4,6},{8,10},{12,14},{16,18},{20,22},{24,26},{28,30},{32,34}... | collective-permute-start | bytes 49160 | tf_op jit(solution)/shard_map/ppermute | solution.py:493

commit v8 on v7

--- a/solution.py
+++ b/solution.py
@@ -29,6 +29,7 @@
 NT = (((1,), (1,)), ((), ()))
 TN = (((0,), (0,)), ((), ()))
 MAIN = 3 * 128
+EARLY = 2 * 128 - 3 * K
 
 
 def split(x):
@@ -249,11 +250,38 @@
     return work
 
 
+def put_table(labels, t_ref):
+    deep = lax.broadcasted_iota(jnp.int32, (CZ, 128), 0).astype(F32).astype(BF16)
+    whole = labels.astype(jnp.int32)
+    label_y, label_z = (whole // CZ).astype(F32), (whole % CZ).astype(F32)
+    for k in range(SLOTS):
+        here = chosen(deep == jnp.broadcast_to(label_z[k : k + 1], (CZ, 128)).astype(BF16))
+        row = jnp.broadcast_to(label_y[k : k + 1], (CZ, 128)).astype(BF16)
+        for y in range(CY):
+            t_ref[y * CZ : (y + 1) * CZ, k * 128 : (k + 1) * 128] = jnp.where(
+                row == y, here, jnp.zeros((CZ, 128), BF16)
+            )
+
+
+def put_tile(wire_ref, tile, t_ref, r_ref, out_ref, first):
+    for k in range(SLOTS):
+        high, low = split(wire_ref[tile * SLOTS + k])
+        r_ref[k * 128 : (k + 1) * 128, 0:128] = high
+        r_ref[k * 128 : (k + 1) * 128, 128:256] = low
+    moved = half_sum(jnp.dot(t_ref[...], r_ref[...], preferred_element_type=F32))
+    for y in range(CY):
+        out_ref[pl.ds(first * CY + y, 128, stride=CY), :] = moved[y * CZ : (y + 1) * CZ].T
+
+
+def late_kernel(wire_ref, late_ref, t_ref, r_ref):
+    put_table(wire_ref[48].T[6 * SLOTS : 7 * SLOTS], t_ref)
+    put_tile(wire_ref, 2, t_ref, r_ref, late_ref, 0)
+
+
 def unpack_kernel(
     place_ref, wire_ref, mine_ref, other_ref, main_ref, ext_ref, v_ref, inv_ref, start_ref, beta_ref,
     t_ref, r_ref, left_ref, right_ref, fold_ref,
 ):
-    deep = lax.broadcasted_iota(jnp.int32, (CZ, 128), 0).astype(F32).astype(BF16)
     lower = place_ref[0:1, :] == 0
     mine, other = mine_ref[0:HALF, :], other_ref[0:HALF, :]
     bands = jnp.concatenate([jnp.where(lower, mine, other), jnp.where(lower, other, mine)], axis=0)
@@ -267,23 +295,9 @@
         work = swept(work, begin, 4)
     rest = wire_ref[48].T
     labels = rest[6 * SLOTS : 7 * SLOTS]
-    whole = labels.astype(jnp.int32)
-    label_y, label_z = (whole // CZ).astype(F32), (whole % CZ).astype(F32)
-    for k in range(SLOTS):
-        here = chosen(deep == jnp.broadcast_to(label_z[k : k + 1], (CZ, 128)).astype(BF16))
-        row = jnp.broadcast_to(label_y[k : k + 1], (CZ, 128)).astype(BF16)
-        for y in range(CY):
-            t_ref[y * CZ : (y + 1) * CZ, k * 128 : (k + 1) * 128] = jnp.where(
-                row == y, here, jnp.zeros((CZ, 128), BF16)
-            )
-    for tile in range(3):
-        for k in range(SLOTS):
-            high, low = split(wire_ref[tile * SLOTS + k])
-            r_ref[tile, k * 128 : (k + 1) * 128, 0:128] = high
-            r_ref[tile, k * 128 : (k + 1) * 128, 128:256] = low
-        moved = half_sum(jnp.dot(t_ref[...], r_ref[tile], preferred_element_type=F32))
-        for y in range(CY):
-            main_ref[pl.ds(tile * 128 * CY + y, 128, stride=CY), :] = moved[y * CZ : (y + 1) * CZ].T
+    put_table(labels, t_ref)
+    for tile in range(2):
+        put_tile(wire_ref, tile, t_ref, r_ref.at[tile], main_ref, tile * 128)
     [ext] = two_level([(rest[0 : 6 * SLOTS], labels)], left_ref, right_ref)
     ext_ref[...] = ext
 
@@ -307,7 +321,7 @@
         pad_ref[base + 16 : base + 17, :] = jnp.where(side == 0, edge, 0.0)
 
 
-def stencil(main_ref, ext_ref, pad_ref):
+def stencil(main_ref, late_ref, ext_ref, pad_ref):
     lane = lax.broadcasted_iota(jnp.int32, (CY, 128), 1)
     total = [jnp.zeros((CY, 128), F32) for _ in range(3)]
     for dx in range(3):
@@ -320,16 +334,17 @@
                 for dz, moved in enumerate((left, here, right)):
                     for a in range(3):
                         q = ((dx * 9 + dy * 3 + dz) * 3 + a) * 3 + b
-                        if q < 240:
-                            row = (3 * K + q) * CY
-                            total[a] = total[a] + main_ref[row : row + CY, :] * moved
+                        if q < EARLY:
+                            source, row = main_ref, (3 * K + q) * CY
+                        elif q < 240:
+                            source, row = late_ref, (q - EARLY) * CY
                         else:
-                            row = (q - 240) * CY
-                            total[a] = total[a] + ext_ref[row : row + CY, :] * moved
+                            source, row = ext_ref, (q - 240) * CY
+                        total[a] = total[a] + source[row : row + CY, :] * moved
     return total
 
 
-def image_kernel(count, place_ref, main_ref, ext_ref, first_ref, second_ref, *refs):
+def image_kernel(count, place_ref, main_ref, late_ref, ext_ref, first_ref, second_ref, *refs):
     vectors, (image_ref, send_ref, *edges, pad_ref, part_ref) = refs[:count], refs[count:]
     side = place_ref[0:1, :]
     even = place_ref[1:2, :] == 0
@@ -338,7 +353,7 @@
     put_plane(pad_ref, 0, up[0:24], up[24:32], side)
     put_plane(pad_ref, 1, vectors[-1][0:24, :], vectors[-1][24:32, :], side)
     put_plane(pad_ref, 2, down[0:24], down[24:32], side)
-    image = stencil(main_ref, ext_ref, pad_ref)
+    image = stencil(main_ref, late_ref, ext_ref, pad_ref)
     for a in range(3):
         image_ref[a * CY : (a + 1) * CY, :] = image[a]
     for edge_ref in edges:
@@ -431,7 +446,7 @@
 
 
 def last_kernel(
-    place_ref, got_ref, main_ref, ext_ref, y_ref, one_ref, two_ref, im_one_ref, im_two_ref,
+    place_ref, got_ref, main_ref, late_ref, ext_ref, y_ref, one_ref, two_ref, im_one_ref, im_two_ref,
     sol_ref, res_ref, left_ref, right_ref, pad_ref,
 ):
     side = place_ref[0:1, :]
@@ -448,7 +463,7 @@
         put_plane(pad_ref, dx, own, jnp.concatenate(lines, axis=0), side)
         if dx == 1:
             term = own
-    image = stencil(main_ref, ext_ref, pad_ref)
+    image = stencil(main_ref, late_ref, ext_ref, pad_ref)
     y_one, y_two = y_ref[0:1, :], y_ref[1:2, :]
     solution = term + y_one * one_ref[0:24, :] + y_two * two_ref[0:24, :]
     for a in range(3):
@@ -469,7 +484,7 @@
     return tuple(pl.BlockSpec(memory_space=space) for space in spaces)
 
 
-def call(kernel, outs, scratch=(), inputs=0, in_specs=None, out_specs=None, limit=40):
+def call(kernel, outs, scratch=(), inputs=0, in_specs=None, out_specs=None, limit=40, cost=None):
     vmem = pltpu.VMEM
     return pl.pallas_call(
         kernel,
@@ -478,6 +493,7 @@
         out_specs=out_specs or specs(*[vmem] * len(outs)),
         scratch_shapes=list(scratch),
         compiler_params=pltpu.CompilerParams(vmem_limit_bytes=limit * 2**20),
+        cost_estimate=cost,
     )
 
 
@@ -526,30 +542,37 @@
     plane = shape(32, 128)
     main, ext, one, inverse, start, beta = call(
         unpack_kernel,
-        (shape(MAIN * CY, 128), shape(48, 128), plane, shape(K, 128), shape(K, 128), shape(8, 128)),
+        (shape(2 * 128 * CY, 128), shape(48, 128), plane, shape(K, 128), shape(K, 128), shape(8, 128)),
         [
             vmem((ROWS, SLOTS * PEERS), BF16),
-            vmem((3, SLOTS * PEERS, 256), BF16),
+            vmem((2, SLOTS * PEERS, 256), BF16),
             vmem((48, SLOTS * PEERS), F32),
             vmem((128, SLOTS * PEERS), BF16),
             vmem((56, 128), F32),
         ],
         inputs=4,
     )(place, got, mine, other_core(mine))
+    [late] = call(
+        late_kernel,
+        (shape(128 * CY, 128),),
+        [vmem((ROWS, SLOTS * PEERS), BF16), vmem((SLOTS * PEERS, 256), BF16)],
+        inputs=1,
+        cost=pl.CostEstimate(flops=2 * ROWS * SLOTS * PEERS * 256, bytes_accessed=5 * 10**6, transcendentals=0),
+    )(got)
     pad = vmem((9 * 24, 128), F32)
     image_scratch = [pad, vmem(((K + 8) * CY, 128), F32)]
     image_outs = (shape(3 * CY, 128), shape(PEERS, 128))
     one = lax.dynamic_update_slice(one, other_core(one[24:32]), (24, 0))
     image_one, send, edge = call(
-        functools.partial(image_kernel, 1), (*image_outs, shape(3 * K + 8, 128)), image_scratch, inputs=6
-    )(place, main, ext, swap(one, 0), swap(one, 1), one)
+        functools.partial(image_kernel, 1), (*image_outs, shape(3 * K + 8, 128)), image_scratch, inputs=7
+    )(place, main, late, ext, swap(one, 0), swap(one, 1), one)
     other = other_core(edge)
     sums = exchange(send)
     two, weights, h_one = call(next_kernel, (plane, shape(K, 128), shape(8, 128)), inputs=6)(
         sums, main, image_one, one, other, inverse
     )
-    image_two, send = call(functools.partial(image_kernel, 2), image_outs, image_scratch, inputs=7)(
-        place, main, ext, swap(two, 0), swap(two, 1), one, two
+    image_two, send = call(functools.partial(image_kernel, 2), image_outs, image_scratch, inputs=8)(
+        place, main, late, ext, swap(two, 0), swap(two, 1), one, two
     )
     sums = exchange(send)
     wire, y = call(send_kernel, (shape(PEERS * 3, 128), shape(8, 128)), inputs=8)(
@@ -560,8 +583,8 @@
         last_kernel,
         (shape(3, ROWS), shape(3, ROWS)),
         [vmem((3, 48, SLOTS * PEERS), F32), vmem((3, 256, SLOTS * PEERS), BF16), pad],
-        inputs=9,
-    )(place, got, main, ext, y, one, two, image_one, image_two)
+        inputs=10,
+    )(place, got, main, late, ext, y, one, two, image_one, image_two)
 
 
 def solution(mesh):

time: 140 us -> 139 us (level)
  waiting for transfers between devices: 59.6 us -> 57.9 us
    ppermute x4, waiting for transfers between devices: 11.8 us -> 10.1 us  [swap(): return lax.ppermute(plane, GX, pairs + [(j, i) for i, j in pairs])]
    pallas_call x1 -> x2, Pallas kernels: 4.31 us -> 4.5 us  [the longest x1 2.98 us: body(): call(unpack_kernel, (shape(2 * 128 * CY, 128), shape(48, 128), plane, sha...]
  transfers between devices with their start and end apart: 8 -> 8, of which waited for: 5 -> 5; matrix products, arithmetic and copies ran while one was open for 0% -> 0% of each run, Pallas kernels for 0% -> 1%
where the time goes in v8:
time: 139 us; the launch traced here: 137 us
  waiting for transfers between devices  57.9 us (42%)
  blocking collectives  42.9 us (31%)
  starting transfers between devices  19.1 us (14%)
  Pallas kernels  15.9 us (11%)
    all_to_all x1, waiting for transfers between devices, exchange(): got = lax.all_to_all(shaped, GX_GY, split_axis=0, concat_axis=0, tiled=True)  45.7 us
    all_to_all x3, blocking collectives, exchange(): got = lax.all_to_all(shaped, GX_GY, split_axis=0, concat_axis=0, tiled=True)  42.9 us
    all_to_all x1, starting transfers between devices, exchange(): got = lax.all_to_all(shaped, GX_GY, split_axis=0, concat_axis=0, tiled=True)  10.5 us
    ppermute x4, waiting for transfers between devices, swap(): return lax.ppermute(plane, GX, pairs + [(j, i) for i, j in pairs])  10.1 us
    ppermute x4, starting transfers between devices, swap(): return lax.ppermute(plane, GX, pairs + [(j, i) for i, j in pairs])  8.14 us
    pallas_call x1, Pallas kernels, body(): call(pack_kernel, (shape(PEERS * WIRE, 128), shape(8, ROWS, dtype=jnp.int...  6.89 us
    pallas_call x1, Pallas kernels, body(): call(unpack_kernel, (shape(2 * 128 * CY, 128), shape(48, 128), plane, sha...  2.98 us
  transfers between devices with their start and end apart: 8, of which 5 were waited for; matrix products, arithmetic and copies ran while one was open for 0% of the time, Pallas kernels for 1%

profile of v8, /device:TPU:2, one launch (start us, length us, event | category | flops | bytes accessed | tf_op | source)
XLA Modules:
  0.0 137.1 jit_solution(16340865721396556211)
XLA Ops:
  0.6 6.9 %shard_map.68 = (f32[6912,128]{1,0:T(8,128)}, s32[8,1024]{1,0:T(8,128)}) custom-call(f32[243,1024]{1,0:T(8,128)} %op_hbm.1, f32[144,1024]{1,0:T(8,128)} %c_hbm.1, f32[3,1024]{1,0:T(4,128)} %b_hbm.1, s32[1,1024]{1,0:T(1,128)} %bitcast.27), custom_call_target="tpu_custom_call" | custom-call | tf_op jit(solution)/shard_map/pallas_call | solution.py:520
  7.5 10.5 %all-to-all-start = ((f32[128,54,1,128]{3,2,1,0:T(1,128)}), f32[128,54,1,128]{3,2,1,0:T(1,128)S(1)}, u32[]{:S(2)}, u32[]{:S(2)}) async-start(f32[128,54,1,128]{3,2,1,0:T(1,128)} %bitcast.26), calls=%async_computation | async-start | bytes 7077888 | tf_op jit(solution)/shard_map/all_to_all | solution.py:503
  18.1 45.7 %all-to-all-done = f32[128,54,1,128]{3,2,1,0:T(1,128)S(1)} async-done(((f32[128,54,1,128]{3,2,1,0:T(1,128)}), f32[128,54,1,128]{3,2,1,0:T(1,128)S(1)}, u32[]{:S(2)}, u32[]{:S(2)}) %all-to-all-start) | async-done | bytes 3538976 | tf_op jit(solution)/shard_map/all_to_all | solution.py:503
  63.7 0.5 copy.19
  64.3 0.1 collective-permute-start
  64.4 1.1 collective-permute-done.other_ref
  65.6 3.0 %shard_map.69 = (f32[2048,128]{1,0:T(8,128)S(1)}, f32[48,128]{1,0:T(8,128)S(1)}, f32[32,128]{1,0:T(8,128)S(1)}, f32[48,128]{1,0:T(8,128)S(1)}, f32[48,128]{1,0:T(8,128)S(1)}, /*index=5*/f32[8,128]{1,0:T(8,128)S(1)}) custom-call(s32[8,128]{1,0:T(8,128)S(1)} %iota.7.place_ref, f32[54,128,128]{2,1,0:T(8,128)S(1)} %bitcast.18, ...), custom_call_target="tpu_custom_call" | custom-call | tf_op jit(solution)/shard_map/pallas_call | solution.py:543
  68.5 0.2 collective-permute-start.1
  68.8 1.0 collective-permute-done.1
  69.8 3.9 %collective-permute-start.3 = (f32[32,128]{1,0:T(8,128)S(1)}, f32[32,128]{1,0:T(8,128)S(1)}, u32[]{:S(2)}, u32[]{:S(2)}) collective-permute-start(f32[32,128]{1,0:T(8,128)S(1)} %constant_dynamic-update-slice_fusion.refs_0_.one_ref), channel_id=1, source_target_pairs={{2,4},{6,8},{10,12},{14,16},{18,20},{22,24},{26,28},{30,32},{34,36... | collective-permute-start | bytes 49160 | tf_op jit(solution)/shard_map/ppermute | solution.py:509
  73.7 0.1 collective-permute-start.2
  73.8 1.5 %shard_map.70.late_ref = f32[1024,128]{1,0:T(8,128)S(1)} custom-call(f32[54,128,128]{2,1,0:T(8,128)S(1)} %bitcast.19), custom_call_target="tpu_custom_call" | custom-call | flops 1073741824 | bytes 5000000 | tf_op jit(solution)/shard_map/pallas_call | solution.py:555
  75.3 4.4 %collective-permute-done.3.second_ref = f32[32,128]{1,0:T(8,128)S(1)} collective-permute-done((f32[32,128]{1,0:T(8,128)S(1)}, f32[32,128]{1,0:T(8,128)S(1)}, u32[]{:S(2)}, u32[]{:S(2)}) %collective-permute-start.3) | collective-permute-done | bytes 16416 | tf_op jit(solution)/shard_map/ppermute | solution.py:509
  79.8 0.4 shard_map.71
  80.3 14.1 %all_to_all.20 = f32[128,1,1,128]{3,2,1,0:T(1,128)S(1)} all-to-all(f32[128,1,1,128]{3,2,1,0:T(1,128)S(1)} %bitcast.24), channel_id=1, replica_groups=mesh['gx_0'=4,'gx_1'=4,'gx_2'=4,'gy'=2] {'gx_0','gx_1','gx_2','gy'}, dimensions={0} | all-to-all | bytes 131072 | tf_op jit(solution)/shard_map/all_to_all | solution.py:503
  94.4 0.5 shard_map.72
  94.9 3.9 %collective-permute-start.6 = (f32[32,128]{1,0:T(8,128)S(1)}, f32[32,128]{1,0:T(8,128)S(1)}, u32[]{:S(2)}, u32[]{:S(2)}) collective-permute-start(f32[32,128]{1,0:T(8,128)S(1)} %get-tuple-element.28.refs_1_.two_ref), channel_id=1, source_target_pairs={{2,4},{6,8},{10,12},{14,16},{18,20},{22,24},{26,28},{30,32},{34,36... | collective-permute-start | bytes 49160 | tf_op jit(solution)/shard_map/ppermute | solution.py:509
  98.8 0.3 collective-permute-start.5
  99.1 5.7 %collective-permute-done.6.second_ref = f32[32,128]{1,0:T(8,128)S(1)} collective-permute-done((f32[32,128]{1,0:T(8,128)S(1)}, f32[32,128]{1,0:T(8,128)S(1)}, u32[]{:S(2)}, u32[]{:S(2)}) %collective-permute-start.6) | collective-permute-done | bytes 16416 | tf_op jit(solution)/shard_map/ppermute | solution.py:509
  104.8 0.4 shard_map.73
  105.2 14.1 %all_to_all.21 = f32[128,1,1,128]{3,2,1,0:T(1,128)S(1)} all-to-all(f32[128,1,1,128]{3,2,1,0:T(1,128)S(1)} %bitcast.25), channel_id=1, replica_groups=mesh['gx_0'=4,'gx_1'=4,'gx_2'=4,'gy'=2] {'gx_0','gx_1','gx_2','gy'}, dimensions={0} | all-to-all | bytes 131072 | tf_op jit(solution)/shard_map/all_to_all | solution.py:503
  119.4 0.9 shard_map.74
  120.3 14.7 %all_to_all.22 = f32[128,3,1,128]{3,2,1,0:T(1,128)S(1)} all-to-all(f32[128,3,1,128]{3,2,1,0:T(1,128)S(1)} %bitcast.23), channel_id=1, replica_groups=mesh['gx_0'=4,'gx_1'=4,'gx_2'=4,'gy'=2] {'gx_0','gx_1','gx_2','gy'}, dimensions={0} | all-to-all | bytes 393216 | tf_op jit(solution)/shard_map/all_to_all | solution.py:503
  134.9 2.2 %shard_map.75 = (f32[3,1024]{1,0:T(4,128)}, f32[3,1024]{1,0:T(4,128)}) custom-call(s32[8,128]{1,0:T(8,128)S(1)} %iota.7.place_ref, f32[384,128]{1,0:T(8,128)S(1)} %bitcast.20, f32[2048,128]{1,0:T(8,128)S(1)} %get-tuple-element.21.main_ref, f32[1024,128]{1,0:T(8,128)S(1)} %shard_map.70.late_ref, f32[48,128]{1,0:T(8,128)S(1)} %get-tuple-element.22.ext_ref, ...), custom_call_target="tpu_custom_call" | custom-call | tf_op jit(solution)/shard_map/pallas_call | solution.py:582
  (13 shorter events, 0.2 us)
Async XLA Ops:
  7.5 56.2 %all-to-all-start = ((f32[128,54,1,128]{3,2,1,0:T(1,128)}), f32[128,54,1,128]{3,2,1,0:T(1,128)S(1)}, u32[]{:S(2)}, u32[]{:S(2)}) async-start(f32[128,54,1,128]{3,2,1,0:T(1,128)} %bitcast.26), calls=%async_computation | async-start | bytes 7077888 | tf_op jit(solution)/shard_map/all_to_all | solution.py:503
  64.3 1.2 collective-permute-start
  68.5 1.2 collective-permute-start.1
  69.8 49.6 %copy-start = (f32[144,1024]{1,0:T(8,128)S(1)}, f32[144,1024]{1,0:T(8,128)}, u32[]{:S(2)}) copy-start(f32[144,1024]{1,0:T(8,128)} %u_ref.1) | copy-start | bytes 1769476
  69.8 49.6 %copy-start.1 = (s32[8,1024]{1,0:T(8,128)S(1)}, s32[8,1024]{1,0:T(8,128)}, u32[]{:S(2)}) copy-start(s32[8,1024]{1,0:T(8,128)} %get-tuple-element.34.info_ref) | copy-start | bytes 98308
  69.8 10.0 %collective-permute-start.3 = (f32[32,128]{1,0:T(8,128)S(1)}, f32[32,128]{1,0:T(8,128)S(1)}, u32[]{:S(2)}, u32[]{:S(2)}) collective-permute-start(f32[32,128]{1,0:T(8,128)S(1)} %constant_dynamic-update-slice_fusion.refs_0_.one_ref), channel_id=1, source_target_pairs={{2,4},{6,8},{10,12},{14,16},{18,20},{22,24},{26,28},{30,32},{34,36... | collective-permute-start | bytes 49160 | tf_op jit(solution)/shard_map/ppermute | solution.py:509
  73.7 6.1 %collective-permute-start.2 = (f32[32,128]{1,0:T(8,128)S(1)}, f32[32,128]{1,0:T(8,128)S(1)}, u32[]{:S(2)}, u32[]{:S(2)}) collective-permute-start(f32[32,128]{1,0:T(8,128)S(1)} %constant_dynamic-update-slice_fusion.refs_0_.one_ref), channel_id=1, source_target_pairs={{0,2},{4,6},{8,10},{12,14},{16,18},{20,22},{24,26},{28,30},{32,34}... | collective-permute-start | bytes 49160 | tf_op jit(solution)/shard_map/ppermute | solution.py:509
  80.2 14.2 %collective-permute-start.4 = (f32[152,128]{1,0:T(8,128)S(1)}, f32[152,128]{1,0:T(8,128)S(1)}, u32[]{:S(2)}, u32[]{:S(2)}) collective-permute-start(f32[152,128]{1,0:T(8,128)S(1)} %get-tuple-element.26), channel_id=1, source_target_pairs={{0,1},{1,0},{2,3},{3,2},{4,5},{5,4},{6,7},{7,6},{8,9},{9,8},{10,11... | collective-permute-start | bytes 233480 | tf_op jit(solution)/shard_map/ppermute | solution.py:513
  94.9 9.9 %collective-permute-start.6 = (f32[32,128]{1,0:T(8,128)S(1)}, f32[32,128]{1,0:T(8,128)S(1)}, u32[]{:S(2)}, u32[]{:S(2)}) collective-permute-start(f32[32,128]{1,0:T(8,128)S(1)} %get-tuple-element.28.refs_1_.two_ref), channel_id=1, source_target_pairs={{2,4},{6,8},{10,12},{14,16},{18,20},{22,24},{26,28},{30,32},{34,36... | collective-permute-start | bytes 49160 | tf_op jit(solution)/shard_map/ppermute | solution.py:509
  98.8 6.0 %collective-permute-start.5 = (f32[32,128]{1,0:T(8,128)S(1)}, f32[32,128]{1,0:T(8,128)S(1)}, u32[]{:S(2)}, u32[]{:S(2)}) collective-permute-start(f32[32,128]{1,0:T(8,128)S(1)} %get-tuple-element.28.refs_1_.two_ref), channel_id=1, source_target_pairs={{0,2},{4,6},{8,10},{12,14},{16,18},{20,22},{24,26},{28,30},{32,34}... | collective-permute-start | bytes 49160 | tf_op jit(solution)/shard_map/ppermute | solution.py:509

commit v9 on v8

--- a/solution.py
+++ b/solution.py
@@ -102,8 +102,8 @@
 
 
 def pack_kernel(
-    op_hbm, c_hbm, b_hbm, rows_hbm, wire_hbm, info_ref,
-    op_ref, c_ref, b_ref, rows_ref, p_ref, a_ref, fold_ref, wire_ref, in_sem, out_sem,
+    op_hbm, c_hbm, b_hbm, rows_hbm, wire_hbm, info_hbm,
+    op_ref, c_ref, b_ref, rows_ref, p_ref, a_ref, fold_ref, wire_ref, info_ref, in_sem, out_sem,
 ):
     copies = [
         pltpu.make_async_copy(source, target, in_sem.at[i])
@@ -136,6 +136,8 @@
     info_ref[1:2, :] = rank.astype(jnp.int32)
     info_ref[2:3, :] = local
     info_ref[3:8, :] = jnp.zeros((5, ROWS), jnp.int32)
+    sent = [pltpu.make_async_copy(info_ref, info_hbm, out_sem.at[CHUNKS])]
+    sent[0].start()
     for copy in copies[1:]:
         copy.wait()
 
@@ -171,7 +173,6 @@
     wire_ref[pl.ds(48, PEERS, stride=WIRE), :] = half_sum(
         lax.dot_general(onehot_b, rest, NT, preferred_element_type=F32)
     )
-    sent = []
     count = PEERS // CHUNKS
     for chunk in range(CHUNKS):
         mine = rank_at[chunk * count : (chunk + 1) * count]
@@ -529,11 +530,12 @@
             vmem((3, 64, ROWS), F32),
             vmem((56, 128), F32),
             vmem((PEERS * WIRE, 128), F32),
+            vmem((8, ROWS), jnp.int32),
             pltpu.SemaphoreType.DMA((6,)),
-            pltpu.SemaphoreType.DMA((CHUNKS,)),
+            pltpu.SemaphoreType.DMA((CHUNKS + 1,)),
         ],
         in_specs=specs(hbm, hbm, hbm, hbm),
-        out_specs=specs(hbm, vmem),
+        out_specs=specs(hbm, hbm),
         limit=56,
     )(operator, basis_c, right_side, new_rows.reshape(1, ROWS))
     got = exchange(wire)

time: 139 us -> 138 us (level)
  no operation moved by 1% of the time
where the time goes in v9:
time: 138 us; the launch traced here: 137 us
  waiting for transfers between devices  57.9 us (42%)
  blocking collectives  42.9 us (31%)
  starting transfers between devices  19.1 us (14%)
  Pallas kernels  15.3 us (11%)
    all_to_all x1, waiting for transfers between devices, exchange(): got = lax.all_to_all(shaped, GX_GY, split_axis=0, concat_axis=0, tiled=True)  45.7 us
    all_to_all x3, blocking collectives, exchange(): got = lax.all_to_all(shaped, GX_GY, split_axis=0, concat_axis=0, tiled=True)  42.9 us
    all_to_all x1, starting transfers between devices, exchange(): got = lax.all_to_all(shaped, GX_GY, split_axis=0, concat_axis=0, tiled=True)  10.5 us
    ppermute x4, waiting for transfers between devices, swap(): return lax.ppermute(plane, GX, pairs + [(j, i) for i, j in pairs])  10.1 us
    ppermute x4, starting transfers between devices, swap(): return lax.ppermute(plane, GX, pairs + [(j, i) for i, j in pairs])  8.14 us
    pallas_call x1, Pallas kernels, body(): call(pack_kernel, (shape(PEERS * WIRE, 128), shape(8, ROWS, dtype=jnp.int...  6.28 us
    pallas_call x1, Pallas kernels, body(): call(unpack_kernel, (shape(2 * 128 * CY, 128), shape(48, 128), plane, sha...  2.98 us
  transfers between devices with their start and end apart: 8, of which 5 were waited for; matrix products, arithmetic and copies ran while one was open for 0% of the time, Pallas kernels for 1%

profile of v9, /device:TPU:2, one launch (start us, length us, event | category | flops | bytes accessed | tf_op | source)
XLA Modules:
  0.0 136.5 jit_solution(3193138355770628653)
XLA Ops:
  0.6 6.3 %shard_map.68 = (f32[6912,128]{1,0:T(8,128)}, s32[8,1024]{1,0:T(8,128)}) custom-call(f32[243,1024]{1,0:T(8,128)} %op_hbm.1, f32[144,1024]{1,0:T(8,128)} %c_hbm.1, f32[3,1024]{1,0:T(4,128)} %b_hbm.1, s32[1,1024]{1,0:T(1,128)} %bitcast.27), custom_call_target="tpu_custom_call" | custom-call | tf_op jit(solution)/shard_map/pallas_call | solution.py:521
  6.9 10.5 %all-to-all-start = ((f32[128,54,1,128]{3,2,1,0:T(1,128)}), f32[128,54,1,128]{3,2,1,0:T(1,128)S(1)}, u32[]{:S(2)}, u32[]{:S(2)}) async-start(f32[128,54,1,128]{3,2,1,0:T(1,128)} %bitcast.26), calls=%async_computation | async-start | bytes 7077888 | tf_op jit(solution)/shard_map/all_to_all | solution.py:504
  17.5 45.7 %all-to-all-done = f32[128,54,1,128]{3,2,1,0:T(1,128)S(1)} async-done(((f32[128,54,1,128]{3,2,1,0:T(1,128)}), f32[128,54,1,128]{3,2,1,0:T(1,128)S(1)}, u32[]{:S(2)}, u32[]{:S(2)}) %all-to-all-start) | async-done | bytes 3538976 | tf_op jit(solution)/shard_map/all_to_all | solution.py:504
  63.1 0.5 copy.19
  63.7 0.1 collective-permute-start
  63.8 1.1 collective-permute-done.other_ref
  65.0 3.0 %shard_map.69 = (f32[2048,128]{1,0:T(8,128)S(1)}, f32[48,128]{1,0:T(8,128)S(1)}, f32[32,128]{1,0:T(8,128)S(1)}, f32[48,128]{1,0:T(8,128)S(1)}, f32[48,128]{1,0:T(8,128)S(1)}, /*index=5*/f32[8,128]{1,0:T(8,128)S(1)}) custom-call(s32[8,128]{1,0:T(8,128)S(1)} %iota.7.place_ref, f32[54,128,128]{2,1,0:T(8,128)S(1)} %bitcast.18, ...), custom_call_target="tpu_custom_call" | custom-call | tf_op jit(solution)/shard_map/pallas_call | solution.py:545
  67.9 0.2 collective-permute-start.1
  68.2 1.0 collective-permute-done.1
  69.2 3.9 %collective-permute-start.3 = (f32[32,128]{1,0:T(8,128)S(1)}, f32[32,128]{1,0:T(8,128)S(1)}, u32[]{:S(2)}, u32[]{:S(2)}) collective-permute-start(f32[32,128]{1,0:T(8,128)S(1)} %constant_dynamic-update-slice_fusion.refs_0_.one_ref), channel_id=1, source_target_pairs={{2,4},{6,8},{10,12},{14,16},{18,20},{22,24},{26,28},{30,32},{34,36... | collective-permute-start | bytes 49160 | tf_op jit(solution)/shard_map/ppermute | solution.py:510
  73.1 0.1 collective-permute-start.2
  73.2 1.5 %shard_map.70.late_ref = f32[1024,128]{1,0:T(8,128)S(1)} custom-call(f32[54,128,128]{2,1,0:T(8,128)S(1)} %bitcast.19), custom_call_target="tpu_custom_call" | custom-call | flops 1073741824 | bytes 5000000 | tf_op jit(solution)/shard_map/pallas_call | solution.py:557
  74.7 4.4 %collective-permute-done.3.second_ref = f32[32,128]{1,0:T(8,128)S(1)} collective-permute-done((f32[32,128]{1,0:T(8,128)S(1)}, f32[32,128]{1,0:T(8,128)S(1)}, u32[]{:S(2)}, u32[]{:S(2)}) %collective-permute-start.3) | collective-permute-done | bytes 16416 | tf_op jit(solution)/shard_map/ppermute | solution.py:510
  79.2 0.4 shard_map.71
  79.7 14.1 %all_to_all.20 = f32[128,1,1,128]{3,2,1,0:T(1,128)S(1)} all-to-all(f32[128,1,1,128]{3,2,1,0:T(1,128)S(1)} %bitcast.24), channel_id=1, replica_groups=mesh['gx_0'=4,'gx_1'=4,'gx_2'=4,'gy'=2] {'gx_0','gx_1','gx_2','gy'}, dimensions={0} | all-to-all | bytes 131072 | tf_op jit(solution)/shard_map/all_to_all | solution.py:504
  93.8 0.5 shard_map.72
  94.3 3.9 %collective-permute-start.6 = (f32[32,128]{1,0:T(8,128)S(1)}, f32[32,128]{1,0:T(8,128)S(1)}, u32[]{:S(2)}, u32[]{:S(2)}) collective-permute-start(f32[32,128]{1,0:T(8,128)S(1)} %get-tuple-element.28.refs_1_.two_ref), channel_id=1, source_target_pairs={{2,4},{6,8},{10,12},{14,16},{18,20},{22,24},{26,28},{30,32},{34,36... | collective-permute-start | bytes 49160 | tf_op jit(solution)/shard_map/ppermute | solution.py:510
  98.2 0.3 collective-permute-start.5
  98.5 5.7 %collective-permute-done.6.second_ref = f32[32,128]{1,0:T(8,128)S(1)} collective-permute-done((f32[32,128]{1,0:T(8,128)S(1)}, f32[32,128]{1,0:T(8,128)S(1)}, u32[]{:S(2)}, u32[]{:S(2)}) %collective-permute-start.6) | collective-permute-done | bytes 16416 | tf_op jit(solution)/shard_map/ppermute | solution.py:510
  104.2 0.4 shard_map.73
  104.6 14.1 %all_to_all.21 = f32[128,1,1,128]{3,2,1,0:T(1,128)S(1)} all-to-all(f32[128,1,1,128]{3,2,1,0:T(1,128)S(1)} %bitcast.25), channel_id=1, replica_groups=mesh['gx_0'=4,'gx_1'=4,'gx_2'=4,'gy'=2] {'gx_0','gx_1','gx_2','gy'}, dimensions={0} | all-to-all | bytes 131072 | tf_op jit(solution)/shard_map/all_to_all | solution.py:504
  118.8 0.9 shard_map.74
  119.7 14.7 %all_to_all.22 = f32[128,3,1,128]{3,2,1,0:T(1,128)S(1)} all-to-all(f32[128,3,1,128]{3,2,1,0:T(1,128)S(1)} %bitcast.23), channel_id=1, replica_groups=mesh['gx_0'=4,'gx_1'=4,'gx_2'=4,'gy'=2] {'gx_0','gx_1','gx_2','gy'}, dimensions={0} | all-to-all | bytes 393216 | tf_op jit(solution)/shard_map/all_to_all | solution.py:504
  134.3 2.2 %shard_map.75 = (f32[3,1024]{1,0:T(4,128)}, f32[3,1024]{1,0:T(4,128)}) custom-call(s32[8,128]{1,0:T(8,128)S(1)} %iota.7.place_ref, f32[384,128]{1,0:T(8,128)S(1)} %bitcast.20, f32[2048,128]{1,0:T(8,128)S(1)} %get-tuple-element.21.main_ref, f32[1024,128]{1,0:T(8,128)S(1)} %shard_map.70.late_ref, f32[48,128]{1,0:T(8,128)S(1)} %get-tuple-element.22.ext_ref, ...), custom_call_target="tpu_custom_call" | custom-call | tf_op jit(solution)/shard_map/pallas_call | solution.py:584
  (13 shorter events, 0.2 us)
Async XLA Ops:
  6.9 56.2 %all-to-all-start = ((f32[128,54,1,128]{3,2,1,0:T(1,128)}), f32[128,54,1,128]{3,2,1,0:T(1,128)S(1)}, u32[]{:S(2)}, u32[]{:S(2)}) async-start(f32[128,54,1,128]{3,2,1,0:T(1,128)} %bitcast.26), calls=%async_computation | async-start | bytes 7077888 | tf_op jit(solution)/shard_map/all_to_all | solution.py:504
  63.7 1.2 collective-permute-start
  67.9 1.2 collective-permute-start.1
  69.2 49.6 %copy-start = (f32[144,1024]{1,0:T(8,128)S(1)}, f32[144,1024]{1,0:T(8,128)}, u32[]{:S(2)}) copy-start(f32[144,1024]{1,0:T(8,128)} %u_ref.1) | copy-start | bytes 1769476
  69.2 49.6 %copy-start.1 = (s32[8,1024]{1,0:T(8,128)S(1)}, s32[8,1024]{1,0:T(8,128)}, u32[]{:S(2)}) copy-start(s32[8,1024]{1,0:T(8,128)} %get-tuple-element.34.info_ref) | copy-start | bytes 98308
  69.2 10.0 %collective-permute-start.3 = (f32[32,128]{1,0:T(8,128)S(1)}, f32[32,128]{1,0:T(8,128)S(1)}, u32[]{:S(2)}, u32[]{:S(2)}) collective-permute-start(f32[32,128]{1,0:T(8,128)S(1)} %constant_dynamic-update-slice_fusion.refs_0_.one_ref), channel_id=1, source_target_pairs={{2,4},{6,8},{10,12},{14,16},{18,20},{22,24},{26,28},{30,32},{34,36... | collective-permute-start | bytes 49160 | tf_op jit(solution)/shard_map/ppermute | solution.py:510
  73.1 6.1 %collective-permute-start.2 = (f32[32,128]{1,0:T(8,128)S(1)}, f32[32,128]{1,0:T(8,128)S(1)}, u32[]{:S(2)}, u32[]{:S(2)}) collective-permute-start(f32[32,128]{1,0:T(8,128)S(1)} %constant_dynamic-update-slice_fusion.refs_0_.one_ref), channel_id=1, source_target_pairs={{0,2},{4,6},{8,10},{12,14},{16,18},{20,22},{24,26},{28,30},{32,34}... | collective-permute-start | bytes 49160 | tf_op jit(solution)/shard_map/ppermute | solution.py:510
  79.6 14.2 %collective-permute-start.4 = (f32[152,128]{1,0:T(8,128)S(1)}, f32[152,128]{1,0:T(8,128)S(1)}, u32[]{:S(2)}, u32[]{:S(2)}) collective-permute-start(f32[152,128]{1,0:T(8,128)S(1)} %get-tuple-element.26), channel_id=1, source_target_pairs={{0,1},{1,0},{2,3},{3,2},{4,5},{5,4},{6,7},{7,6},{8,9},{9,8},{10,11... | collective-permute-start | bytes 233480 | tf_op jit(solution)/shard_map/ppermute | solution.py:514
  94.3 9.9 %collective-permute-start.6 = (f32[32,128]{1,0:T(8,128)S(1)}, f32[32,128]{1,0:T(8,128)S(1)}, u32[]{:S(2)}, u32[]{:S(2)}) collective-permute-start(f32[32,128]{1,0:T(8,128)S(1)} %get-tuple-element.28.refs_1_.two_ref), channel_id=1, source_target_pairs={{2,4},{6,8},{10,12},{14,16},{18,20},{22,24},{26,28},{30,32},{34,36... | collective-permute-start | bytes 49160 | tf_op jit(solution)/shard_map/ppermute | solution.py:510
  98.2 6.0 %collective-permute-start.5 = (f32[32,128]{1,0:T(8,128)S(1)}, f32[32,128]{1,0:T(8,128)S(1)}, u32[]{:S(2)}, u32[]{:S(2)}) collective-permute-start(f32[32,128]{1,0:T(8,128)S(1)} %get-tuple-element.28.refs_1_.two_ref), channel_id=1, source_target_pairs={{0,2},{4,6},{8,10},{12,14},{16,18},{20,22},{24,26},{28,30},{32,34}... | collective-permute-start | bytes 49160 | tf_op jit(solution)/shard_map/ppermute | solution.py:510

commit v10 on v9

--- a/solution.py
+++ b/solution.py
@@ -448,7 +448,7 @@
 
 def last_kernel(
     place_ref, got_ref, main_ref, late_ref, ext_ref, y_ref, one_ref, two_ref, im_one_ref, im_two_ref,
-    sol_ref, res_ref, left_ref, right_ref, pad_ref,
+    sol_hbm, res_hbm, left_ref, right_ref, pad_ref, sol_ref, res_ref, sem,
 ):
     side = place_ref[0:1, :]
     for dx in range(3):
@@ -464,17 +464,24 @@
         put_plane(pad_ref, dx, own, jnp.concatenate(lines, axis=0), side)
         if dx == 1:
             term = own
-    image = stencil(main_ref, late_ref, ext_ref, pad_ref)
     y_one, y_two = y_ref[0:1, :], y_ref[1:2, :]
     solution = term + y_one * one_ref[0:24, :] + y_two * two_ref[0:24, :]
+    for a in range(3):
+        for y in range(CY):
+            sol_ref[a : a + 1, y * CZ : (y + 1) * CZ] = solution[a * CY + y : a * CY + y + 1, :]
+    first = pltpu.make_async_copy(sol_ref, sol_hbm, sem.at[0])
+    first.start()
+    image = stencil(main_ref, late_ref, ext_ref, pad_ref)
     for a in range(3):
         rows = slice(a * CY, (a + 1) * CY)
         residual = ext_ref[24 + a * CY : 24 + (a + 1) * CY, :] - image[a]
         residual = residual - y_one * im_one_ref[rows, :] - y_two * im_two_ref[rows, :]
         for y in range(CY):
-            cols = slice(y * CZ, (y + 1) * CZ)
-            sol_ref[a : a + 1, cols] = solution[a * CY + y : a * CY + y + 1, :]
-            res_ref[a : a + 1, cols] = residual[y : y + 1, :]
+            res_ref[a : a + 1, y * CZ : (y + 1) * CZ] = residual[y : y + 1, :]
+    second = pltpu.make_async_copy(res_ref, res_hbm, sem.at[1])
+    second.start()
+    first.wait()
+    second.wait()
 
 
 def shape(*dims, dtype=F32):
@@ -584,8 +591,16 @@
     return call(
         last_kernel,
         (shape(3, ROWS), shape(3, ROWS)),
-        [vmem((3, 48, SLOTS * PEERS), F32), vmem((3, 256, SLOTS * PEERS), BF16), pad],
+        [
+            vmem((3, 48, SLOTS * PEERS), F32),
+            vmem((3, 256, SLOTS * PEERS), BF16),
+            pad,
+            vmem((3, ROWS), F32),
+            vmem((3, ROWS), F32),
+            pltpu.SemaphoreType.DMA((2,)),
+        ],
         inputs=10,
+        out_specs=specs(hbm, hbm),
     )(place, got, main, late, ext, y, one, two, image_one, image_two)
 
 

time: 138 us -> 138 us (level)
  no operation moved by 1% of the time
where the time goes in v10:
time: 138 us; the launch traced here: 137 us
  waiting for transfers between devices  57.9 us (42%)
  blocking collectives  42.9 us (31%)
  starting transfers between devices  19.1 us (14%)
  Pallas kernels  15.3 us (11%)
    all_to_all x1, waiting for transfers between devices, exchange(): got = lax.all_to_all(shaped, GX_GY, split_axis=0, concat_axis=0, tiled=True)  45.7 us
    all_to_all x3, blocking collectives, exchange(): got = lax.all_to_all(shaped, GX_GY, split_axis=0, concat_axis=0, tiled=True)  42.9 us
    all_to_all x1, starting transfers between devices, exchange(): got = lax.all_to_all(shaped, GX_GY, split_axis=0, concat_axis=0, tiled=True)  10.5 us
    ppermute x4, waiting for transfers between devices, swap(): return lax.ppermute(plane, GX, pairs + [(j, i) for i, j in pairs])  10.1 us
    ppermute x4, starting transfers between devices, swap(): return lax.ppermute(plane, GX, pairs + [(j, i) for i, j in pairs])  8.14 us
    pallas_call x1, Pallas kernels, body(): call(pack_kernel, (shape(PEERS * WIRE, 128), shape(8, ROWS, dtype=jnp.int...  6.28 us
    pallas_call x1, Pallas kernels, body(): call(unpack_kernel, (shape(2 * 128 * CY, 128), shape(48, 128), plane, sha...  2.98 us
  transfers between devices with their start and end apart: 8, of which 5 were waited for; matrix products, arithmetic and copies ran while one was open for 0% of the time, Pallas kernels for 1%

profile of v10, /device:TPU:2, one launch (start us, length us, event | category | flops | bytes accessed | tf_op | source)
XLA Modules:
  0.0 136.7 jit_solution(4991163661864557490)
XLA Ops:
  0.6 6.3 %shard_map.68 = (f32[6912,128]{1,0:T(8,128)}, s32[8,1024]{1,0:T(8,128)}) custom-call(f32[243,1024]{1,0:T(8,128)} %op_hbm.1, f32[144,1024]{1,0:T(8,128)} %c_hbm.1, f32[3,1024]{1,0:T(4,128)} %b_hbm.1, s32[1,1024]{1,0:T(1,128)} %bitcast.27), custom_call_target="tpu_custom_call" | custom-call | tf_op jit(solution)/shard_map/pallas_call | solution.py:528
  6.9 10.5 %all-to-all-start = ((f32[128,54,1,128]{3,2,1,0:T(1,128)}), f32[128,54,1,128]{3,2,1,0:T(1,128)S(1)}, u32[]{:S(2)}, u32[]{:S(2)}) async-start(f32[128,54,1,128]{3,2,1,0:T(1,128)} %bitcast.26), calls=%async_computation | async-start | bytes 7077888 | tf_op jit(solution)/shard_map/all_to_all | solution.py:511
  17.5 45.7 %all-to-all-done = f32[128,54,1,128]{3,2,1,0:T(1,128)S(1)} async-done(((f32[128,54,1,128]{3,2,1,0:T(1,128)}), f32[128,54,1,128]{3,2,1,0:T(1,128)S(1)}, u32[]{:S(2)}, u32[]{:S(2)}) %all-to-all-start) | async-done | bytes 3538976 | tf_op jit(solution)/shard_map/all_to_all | solution.py:511
  63.1 0.5 copy.19
  63.7 0.1 collective-permute-start
  63.8 1.1 collective-permute-done.other_ref
  65.0 3.0 %shard_map.69 = (f32[2048,128]{1,0:T(8,128)S(1)}, f32[48,128]{1,0:T(8,128)S(1)}, f32[32,128]{1,0:T(8,128)S(1)}, f32[48,128]{1,0:T(8,128)S(1)}, f32[48,128]{1,0:T(8,128)S(1)}, /*index=5*/f32[8,128]{1,0:T(8,128)S(1)}) custom-call(s32[8,128]{1,0:T(8,128)S(1)} %iota.7.place_ref, f32[54,128,128]{2,1,0:T(8,128)S(1)} %bitcast.18, ...), custom_call_target="tpu_custom_call" | custom-call | tf_op jit(solution)/shard_map/pallas_call | solution.py:552
  67.9 0.2 collective-permute-start.1
  68.2 1.0 collective-permute-done.1
  69.2 3.9 %collective-permute-start.3 = (f32[32,128]{1,0:T(8,128)S(1)}, f32[32,128]{1,0:T(8,128)S(1)}, u32[]{:S(2)}, u32[]{:S(2)}) collective-permute-start(f32[32,128]{1,0:T(8,128)S(1)} %constant_dynamic-update-slice_fusion.refs_0_.one_ref), channel_id=1, source_target_pairs={{2,4},{6,8},{10,12},{14,16},{18,20},{22,24},{26,28},{30,32},{34,36... | collective-permute-start | bytes 49160 | tf_op jit(solution)/shard_map/ppermute | solution.py:517
  73.1 0.1 collective-permute-start.2
  73.2 1.5 %shard_map.70.late_ref = f32[1024,128]{1,0:T(8,128)S(1)} custom-call(f32[54,128,128]{2,1,0:T(8,128)S(1)} %bitcast.19), custom_call_target="tpu_custom_call" | custom-call | flops 1073741824 | bytes 5000000 | tf_op jit(solution)/shard_map/pallas_call | solution.py:564
  74.7 4.4 %collective-permute-done.3.second_ref = f32[32,128]{1,0:T(8,128)S(1)} collective-permute-done((f32[32,128]{1,0:T(8,128)S(1)}, f32[32,128]{1,0:T(8,128)S(1)}, u32[]{:S(2)}, u32[]{:S(2)}) %collective-permute-start.3) | collective-permute-done | bytes 16416 | tf_op jit(solution)/shard_map/ppermute | solution.py:517
  79.2 0.4 shard_map.71
  79.7 14.1 %all_to_all.20 = f32[128,1,1,128]{3,2,1,0:T(1,128)S(1)} all-to-all(f32[128,1,1,128]{3,2,1,0:T(1,128)S(1)} %bitcast.24), channel_id=1, replica_groups=mesh['gx_0'=4,'gx_1'=4,'gx_2'=4,'gy'=2] {'gx_0','gx_1','gx_2','gy'}, dimensions={0} | all-to-all | bytes 131072 | tf_op jit(solution)/shard_map/all_to_all | solution.py:511
  93.8 0.5 shard_map.72
  94.3 3.9 %collective-permute-start.6 = (f32[32,128]{1,0:T(8,128)S(1)}, f32[32,128]{1,0:T(8,128)S(1)}, u32[]{:S(2)}, u32[]{:S(2)}) collective-permute-start(f32[32,128]{1,0:T(8,128)S(1)} %get-tuple-element.28.refs_1_.two_ref), channel_id=1, source_target_pairs={{2,4},{6,8},{10,12},{14,16},{18,20},{22,24},{26,28},{30,32},{34,36... | collective-permute-start | bytes 49160 | tf_op jit(solution)/shard_map/ppermute | solution.py:517
  98.2 0.3 collective-permute-start.5
  98.5 5.7 %collective-permute-done.6.second_ref = f32[32,128]{1,0:T(8,128)S(1)} collective-permute-done((f32[32,128]{1,0:T(8,128)S(1)}, f32[32,128]{1,0:T(8,128)S(1)}, u32[]{:S(2)}, u32[]{:S(2)}) %collective-permute-start.6) | collective-permute-done | bytes 16416 | tf_op jit(solution)/shard_map/ppermute | solution.py:517
  104.2 0.4 shard_map.73
  104.6 14.1 %all_to_all.21 = f32[128,1,1,128]{3,2,1,0:T(1,128)S(1)} all-to-all(f32[128,1,1,128]{3,2,1,0:T(1,128)S(1)} %bitcast.25), channel_id=1, replica_groups=mesh['gx_0'=4,'gx_1'=4,'gx_2'=4,'gy'=2] {'gx_0','gx_1','gx_2','gy'}, dimensions={0} | all-to-all | bytes 131072 | tf_op jit(solution)/shard_map/all_to_all | solution.py:511
  118.8 0.9 shard_map.74
  119.7 14.7 %all_to_all.22 = f32[128,3,1,128]{3,2,1,0:T(1,128)S(1)} all-to-all(f32[128,3,1,128]{3,2,1,0:T(1,128)S(1)} %bitcast.23), channel_id=1, replica_groups=mesh['gx_0'=4,'gx_1'=4,'gx_2'=4,'gy'=2] {'gx_0','gx_1','gx_2','gy'}, dimensions={0} | all-to-all | bytes 393216 | tf_op jit(solution)/shard_map/all_to_all | solution.py:511
  134.3 2.2 %shard_map.75 = (f32[3,1024]{1,0:T(4,128)}, f32[3,1024]{1,0:T(4,128)}) custom-call(s32[8,128]{1,0:T(8,128)S(1)} %iota.7.place_ref, f32[384,128]{1,0:T(8,128)S(1)} %bitcast.20, f32[2048,128]{1,0:T(8,128)S(1)} %get-tuple-element.21.main_ref, f32[1024,128]{1,0:T(8,128)S(1)} %shard_map.70.late_ref, f32[48,128]{1,0:T(8,128)S(1)} %get-tuple-element.22.ext_ref, ...), custom_call_target="tpu_custom_call" | custom-call | tf_op jit(solution)/shard_map/pallas_call | solution.py:591
  (13 shorter events, 0.2 us)
Async XLA Ops:
  6.9 56.2 %all-to-all-start = ((f32[128,54,1,128]{3,2,1,0:T(1,128)}), f32[128,54,1,128]{3,2,1,0:T(1,128)S(1)}, u32[]{:S(2)}, u32[]{:S(2)}) async-start(f32[128,54,1,128]{3,2,1,0:T(1,128)} %bitcast.26), calls=%async_computation | async-start | bytes 7077888 | tf_op jit(solution)/shard_map/all_to_all | solution.py:511
  63.7 1.2 collective-permute-start
  67.9 1.2 collective-permute-start.1
  69.2 49.6 %copy-start = (f32[144,1024]{1,0:T(8,128)S(1)}, f32[144,1024]{1,0:T(8,128)}, u32[]{:S(2)}) copy-start(f32[144,1024]{1,0:T(8,128)} %u_ref.1) | copy-start | bytes 1769476
  69.2 49.6 %copy-start.1 = (s32[8,1024]{1,0:T(8,128)S(1)}, s32[8,1024]{1,0:T(8,128)}, u32[]{:S(2)}) copy-start(s32[8,1024]{1,0:T(8,128)} %get-tuple-element.34.info_ref) | copy-start | bytes 98308
  69.2 10.0 %collective-permute-start.3 = (f32[32,128]{1,0:T(8,128)S(1)}, f32[32,128]{1,0:T(8,128)S(1)}, u32[]{:S(2)}, u32[]{:S(2)}) collective-permute-start(f32[32,128]{1,0:T(8,128)S(1)} %constant_dynamic-update-slice_fusion.refs_0_.one_ref), channel_id=1, source_target_pairs={{2,4},{6,8},{10,12},{14,16},{18,20},{22,24},{26,28},{30,32},{34,36... | collective-permute-start | bytes 49160 | tf_op jit(solution)/shard_map/ppermute | solution.py:517
  73.1 6.1 %collective-permute-start.2 = (f32[32,128]{1,0:T(8,128)S(1)}, f32[32,128]{1,0:T(8,128)S(1)}, u32[]{:S(2)}, u32[]{:S(2)}) collective-permute-start(f32[32,128]{1,0:T(8,128)S(1)} %constant_dynamic-update-slice_fusion.refs_0_.one_ref), channel_id=1, source_target_pairs={{0,2},{4,6},{8,10},{12,14},{16,18},{20,22},{24,26},{28,30},{32,34}... | collective-permute-start | bytes 49160 | tf_op jit(solution)/shard_map/ppermute | solution.py:517
  79.6 14.2 %collective-permute-start.4 = (f32[152,128]{1,0:T(8,128)S(1)}, f32[152,128]{1,0:T(8,128)S(1)}, u32[]{:S(2)}, u32[]{:S(2)}) collective-permute-start(f32[152,128]{1,0:T(8,128)S(1)} %get-tuple-element.26), channel_id=1, source_target_pairs={{0,1},{1,0},{2,3},{3,2},{4,5},{5,4},{6,7},{7,6},{8,9},{9,8},{10,11... | collective-permute-start | bytes 233480 | tf_op jit(solution)/shard_map/ppermute | solution.py:521
  94.3 9.9 %collective-permute-start.6 = (f32[32,128]{1,0:T(8,128)S(1)}, f32[32,128]{1,0:T(8,128)S(1)}, u32[]{:S(2)}, u32[]{:S(2)}) collective-permute-start(f32[32,128]{1,0:T(8,128)S(1)} %get-tuple-element.28.refs_1_.two_ref), channel_id=1, source_target_pairs={{2,4},{6,8},{10,12},{14,16},{18,20},{22,24},{26,28},{30,32},{34,36... | collective-permute-start | bytes 49160 | tf_op jit(solution)/shard_map/ppermute | solution.py:517
  98.2 6.0 %collective-permute-start.5 = (f32[32,128]{1,0:T(8,128)S(1)}, f32[32,128]{1,0:T(8,128)S(1)}, u32[]{:S(2)}, u32[]{:S(2)}) collective-permute-start(f32[32,128]{1,0:T(8,128)S(1)} %get-tuple-element.28.refs_1_.two_ref), channel_id=1, source_target_pairs={{0,2},{4,6},{8,10},{12,14},{16,18},{20,22},{24,26},{28,30},{32,34}... | collective-permute-start | bytes 49160 | tf_op jit(solution)/shard_map/ppermute | solution.py:517
